TPU v7x, 32 devices: a whole 2x2x4 slice. The times are simulated.
32 devices in a mesh: groups: 2 (over x), tm: 8 (over z, y), tile: 2 (over core).
Axes of the slice: x: 2, y: 2, z: 4, core: 2. Of those that a mesh axis runs over, the one named last changes fastest.
Arguments:
- movie: bfloat16 [4, 2304, 4096], P(('groups', 'tile'), None, 'tm'), parts along dimension 0, may hold values from 0 to 4
- cycle_weights: bfloat16 [4, 2304, 56], P(('groups', 'tile')), parts along dimension 0, may hold values from -0.75 to 0.75
- footprints: bfloat16 [4, 2304, 384], P(('groups', 'tile')), parts along dimension 0, may hold values from 0.19921875 to 1
- traces: bfloat16 [4, 384, 4096], P(('groups', 'tile'), None, 'tm'), parts along dimension 0, may hold values from 0 to 1.5
- centre_row: int32 [4, 384], P(('groups', 'tile')), parts along dimension 0, may hold values from 0 to 47
- centre_col: int32 [4, 384], P(('groups', 'tile')), parts along dimension 0, may hold values from 0 to 47
- radius: int32 [4, 384], P(('groups', 'tile')), parts along dimension 0, may hold values from 4 to 9
- comp_count: int32 [4], P(('groups', 'tile')), parts along dimension 0, may hold values from 64 to 384
Outputs:
- new_footprints: bfloat16 [4, 2304, 384], P(('groups', 'tile')), parts along dimension 0
- new_traces: bfloat16 [4, 384, 4096], P(('groups', 'tile'), None, 'tm'), parts along dimension 0
There are 2 independent parts, one for each index of `groups`. A program takes and returns all parts, laid end to end along the dimension named above; each array names one. Nothing has to cross between parts.
All inputs are finite; a program needn't handle non-finite values.
Results may differ from a plain program's by a relative error of at most 0.0034.
Values may be sent and summed in bfloat16 or wider, within the bound.
No kernel may reach another device: no remote copies, remote signals or barrier semaphores. Data moves between devices by JAX's collectives and lax.ppermute only.
A program may use at most 64 MiB of HBM per device.

v0:
```python
import jax
import jax.numpy as jnp
from jax import lax
from jax.sharding import PartitionSpec as P

TILE_SIDE = 48
CYCLE = 8
KMAX = 384
PASSES = 2


RIDGE_TERM = 1.0


def with_halo(block, sides, width):
    for axis, dim in sides:
        count = lax.axis_size(axis)
        forward = [(i, i + 1) for i in range(count - 1)]
        backward = [(target, source) for source, target in forward]
        low = lax.ppermute(
            lax.slice_in_dim(block, block.shape[dim] - width, None, axis=dim), axis, forward
        )
        high = lax.ppermute(lax.slice_in_dim(block, 0, width, axis=dim), axis, backward)
        block = jnp.concatenate([low, block, high], axis=dim)
    return block


def cycle_offsets():
    found = []
    for row_step in range(-CYCLE, CYCLE + 1):
        for col_step in range(-CYCLE, CYCLE + 1):
            dist_sq = row_step * row_step + col_step * col_step
            if CYCLE * CYCLE <= dist_sq < (CYCLE + 1) * (CYCLE + 1):
                found.append((row_step, col_step))
    return found


def cycle_back(weights, window):
    frames = window.shape[2]
    grid_w = weights.reshape(TILE_SIDE, TILE_SIDE, -1)
    total = jnp.zeros((TILE_SIDE, TILE_SIDE, frames), jnp.float32)
    for index, (row_step, col_step) in enumerate(cycle_offsets()):
        top = CYCLE + row_step
        left = CYCLE + col_step
        piece = window[top : top + TILE_SIDE, left : left + TILE_SIDE, :].astype(jnp.float32)
        total = total + grid_w[:, :, index : index + 1].astype(jnp.float32) * piece
    return total.reshape(TILE_SIDE * TILE_SIDE, frames).astype(jnp.bfloat16)


def keep_mask(row_at, col_at, reach, count):
    pixel = jnp.arange(TILE_SIDE * TILE_SIDE, dtype=jnp.int32)
    row_gap = (pixel // TILE_SIDE)[:, None] - row_at[None, :]
    col_gap = (pixel % TILE_SIDE)[:, None] - col_at[None, :]
    inside = row_gap * row_gap + col_gap * col_gap <= (reach * reach)[None, :]
    live = jnp.arange(KMAX, dtype=jnp.int32) < count
    return (inside & live[None, :], live)


def footprint_move(foot, keep, grad_a, den_c):
    moved = jnp.maximum(foot.astype(jnp.float32) - grad_a / den_c[None, :], 0.0)
    return jnp.where(keep, moved, 0.0).astype(jnp.bfloat16)


def shards(movie, cycle_weights, footprints, traces, centre_row, centre_col, radius, comp_count):
    zero = jnp.zeros((), jnp.bfloat16)
    keep, live = keep_mask(centre_row[0], centre_col[0], radius[0], comp_count[0])
    foot = jnp.where(keep, footprints[0], zero)
    trace = jnp.where(live[:, None], traces[0], zero)
    den_a = jnp.sum(jnp.square(foot.astype(jnp.float32)), axis=0) + RIDGE_TERM
    frames_here = movie.shape[2]
    movie_f = movie[0].astype(jnp.float32)
    back = None
    for sweep in range(PASSES):
        prod = jnp.dot(foot, trace, preferred_element_type=jnp.float32)
        resid = (movie_f - prod).astype(jnp.bfloat16).reshape(TILE_SIDE, TILE_SIDE, frames_here)
        widened = with_halo(resid, (("tile", 1),), CYCLE)
        window = jnp.pad(widened, ((CYCLE, CYCLE), (0, 0), (0, 0)))
        back = cycle_back(cycle_weights[0], window)
        err = (prod + back.astype(jnp.float32) - movie_f).astype(jnp.bfloat16)
        grad = lax.dot_general(
            foot, err, (((0,), (0,)), ((), ())), preferred_element_type=jnp.float32
        )
        moved = jnp.maximum(trace.astype(jnp.float32) - grad / den_a[:, None], 0.0)
        trace = jnp.where(live[:, None], moved, 0.0).astype(jnp.bfloat16)
    prod = jnp.dot(foot, trace, preferred_element_type=jnp.float32)
    ferr = (prod + back.astype(jnp.float32) - movie_f).astype(jnp.bfloat16)
    energy = jnp.sum(jnp.square(trace.astype(jnp.float32)), axis=1)
    share_rows = foot.shape[0] // lax.axis_size("tm")
    grad_share = lax.psum_scatter(
        lax.dot_general(ferr, trace, (((1,), (1,)), ((), ())), preferred_element_type=jnp.float32),
        "tm",
        scatter_dimension=0,
        tiled=True,
    )
    energy_all = lax.psum(energy, "tm")
    first_row = lax.axis_index("tm") * share_rows
    foot_share = lax.dynamic_slice_in_dim(foot, first_row, share_rows, 0)
    keep_share = lax.dynamic_slice_in_dim(keep, first_row, share_rows, 0)
    moved_share = footprint_move(foot_share, keep_share, grad_share, energy_all + RIDGE_TERM)
    new_foot = lax.all_gather(moved_share, "tm", axis=0, tiled=True)
    return (new_foot[None], trace[None])


def solution(mesh):
    in_specs = (
        P(("groups", "tile"), None, "tm"),
        P(("groups", "tile"), None, None),
        P(("groups", "tile"), None, None),
        P(("groups", "tile"), None, "tm"),
        P(("groups", "tile"), None),
        P(("groups", "tile"), None),
        P(("groups", "tile"), None),
        P(("groups", "tile")),
    )
    out_specs = (P(("groups", "tile"), None, None), P(("groups", "tile"), None, "tm"))
    return jax.shard_map(shards, mesh=mesh, in_specs=in_specs, out_specs=out_specs, check_vma=False)
```

profile of v0, /device:TPU:0, one launch (start us, length us, event | category | flops | bytes accessed | tf_op | source)
XLA Modules:
  0.0 274.7 jit_solution(6336495007161943169)
XLA Ops:
  7.2 0.0 reduce-scatter.2.cloned.1.call-start
  7.9 0.7 multiply_reduce_fusion.2
  8.6 0.7 reduce
  9.3 0.7 reduce.1
  10.0 5.4 %fusion.1 = (bf16[2304,512]{1,0:T(8,128)(2,1)S(1)}, f32[2304,512]{1,0:T(8,128)}) fusion(bf16[1,2304,512]{2,1,0:T(8,128)(2,1)} %param.8, bf16[1,384,512]{2,1,0:T(8,128)(2,1)} %param.11, pred[384]{0:T(512)(128)(4,1)S(1)} %iota_compare_fusion.2, bf16[1,2304,384]{2,1,0:T(8,128)(2,1)} %param.10, s32[384]{0:T(512)S(1)} %multiply_reduce_fusion.2, ...), kind=kOutput, calls=%fused_computation.10 | convolution fusion | flops 916783104 | bytes 11623296 | tf_op jit(solution)/shard_map/dot_general | solution.py:74
  15.4 1.4 copy-done
  16.9 0.9 fusion.121
  17.8 2.4 collective-permute-start
  20.2 1.3 collective-permute-start.1
  21.5 0.9 reshape_squeeze.4
  22.6 3.7 %multiply_reduce_fusion = (f32[384]{0:T(512)S(1)}, bf16[2304,384]{1,0:T(8,128)(2,1)S(1)}) fusion(bf16[1,2304,384]{2,1,0:T(8,128)(2,1)} %param.10, pred[384]{0:T(512)(128)(4,1)S(1)} %iota_compare_fusion.2, s32[384]{0:T(512)S(1)} %multiply_reduce_fusion.2, s32[384]{0:T(512)S(1)} %reduce.1, s32[2304]{0:T(1024)S(1)} %get-tuple-element.70, s32[384]{0:T(512)S(1)} %reduce, ...), kind=kLoop, calls=%fused_computation.23 | loop fusion | flops 9731712 | bytes 3563904 | tf_op jit(solution)/shard_map/reduce_sum | solution.py:69
  26.3 0.6 select_maximum_fusion.2
  26.9 43.9 %add_convert_fusion.1 = bf16[48,48,512]{2,1,0:T(8,128)(2,1)S(1)} fusion(bf16[64,64,512]{2,1,0:T(8,128)(2,1)S(1)} %select_maximum_fusion.2, bf16[48,8,512]{2,1,0:T(8,128)(2,1)S(1)} %collective-permute-done.1, bf16[48,48,512]{2,1,0:T(8,128)(2,1)S(1)} %bitcast.347, bf16[48,8,512]{2,1,0:T(8,128)(2,1)S(1)} %collective-permute-done, ...), kind=kLoop, calls=%fused_computation.16 | loop fusion | flops 205258752 | bytes 133423104 | tf_op jit(solution)/shard_map/convert_element_type | solution.py:47
  70.9 1.4 fusion.38
  72.3 1.4 fusion.3
  73.7 0.1 fusion.120
  73.7 3.1 %collective-permute-start.2 = (bf16[48,8,512]{2,1,0:T(8,128)(2,1)S(1)}, bf16[48,8,512]{2,1,0:T(8,128)(2,1)S(1)}, u32[]{:S(2)}, u32[]{:S(2)}) collective-permute-start(bf16[48,8,512]{2,1,0:T(8,128)(2,1)S(1)} %get-tuple-element.4), channel_id=1, source_target_pairs={{0,1},{2,3},{4,5},{6,7},{8,9},{10,11},{12,13},{14,15},{16,17},{18,... | collective-permute-start | bytes 1179656 | tf_op jit(solution)/shard_map/ppermute | solution.py:20
  76.8 1.5 collective-permute-start.3
  78.3 2.1 collective-permute-done.3
  80.4 0.6 select_maximum_fusion
  81.0 43.9 %add_convert_fusion = bf16[48,48,512]{2,1,0:T(8,128)(2,1)S(1)} fusion(bf16[64,64,512]{2,1,0:T(8,128)(2,1)S(1)} %select_maximum_fusion, bf16[48,8,512]{2,1,0:T(8,128)(2,1)S(1)} %collective-permute-done.3, bf16[48,48,512]{2,1,0:T(8,128)(2,1)S(1)} %bitcast.344, bf16[48,8,512]{2,1,0:T(8,128)(2,1)S(1)} %collective-permute-done.2, ...), kind=kLoop, calls=%fused_computation.15 | loop fusion | flops 205258752 | bytes 133423104 | tf_op jit(solution)/shard_map/convert_element_type | solution.py:47
  124.9 1.4 copy-done.3
  126.3 1.3 fusion.41
  127.6 7.2 %fusion.25 = f32[2304,384]{1,0:T(8,128)} fusion(bf16[2304,512]{1,0:T(8,128)(2,1)} %bitcast.349, bf16[2304,384]{1,0:T(8,128)(2,1)S(1)} %get-tuple-element.3, bf16[1,2304,512]{2,1,0:T(8,128)(2,1)} %param.8, f32[384,512]{1,0:T(8,128)S(1)} %fusion.41, bf16[384,512]{1,0:T(8,128)(2,1)S(1)} %fusion.38, pred[384]{0:T(512)(128)(4,1)S(1)} %iota_compare_fusion.2), kind=kOutput, calls=%fused_computation.46 | convolution fusion | flops 1819803648 | bytes 11207040 | tf_op jit(solution)/shard_map/dot_general | solution.py:90
  134.8 0.0 all-gather.2.cloned.1.call-start
  134.9 1.5 fusion.7
  136.4 2.1 fusion.45
  138.5 23.1 %psum.7 = f32[384]{0:T(512)S(1)} all-reduce(f32[384]{0:T(512)S(1)} %get-tuple-element.9), channel_id=1, replica_groups=mesh['groups'=2,'tm'=8,'tile'=2] {'tm'}, use_global_device_ids=true, to_apply=%region_3.4 | all-reduce | flops 384 | bytes 3072 | tf_op jit(solution)/shard_map/psum | solution.py:95
  161.6 55.1 %reduce-scatter.2.cloned.1.call-done = f32[288,384]{1,0:T(8,128)} async-done(((f32[2304,384]{1,0:T(8,128)}), f32[288,384]{1,0:T(8,128)}) %reduce-scatter.2.cloned.1.call-update) | async-done | bytes 442384 | tf_op jit(solution)/shard_map/reduce_scatter | solution.py:89
  216.7 1.8 select_convert_fusion.3
  218.5 46.4 %all-gather.2.cloned.1.call-done = bf16[2304,384]{1,0:T(8,128)(2,1)} async-done(((bf16[288,384]{1,0:T(8,128)(2,1)}), bf16[2304,384]{1,0:T(8,128)(2,1)}) %all-gather.2.cloned.1.call-update) | async-done | bytes 1769488 | tf_op jit(solution)/shard_map/all_gather | solution.py:100
  265.0 2.9 %copy.12 = bf16[1,2304,384]{2,1,0:T(8,128)(2,1)} copy(bf16[1,2304,384]{2,1,0:T(8,128)(2,1)} %bitcast.351) | data formatting | bytes 3538944
  (29 shorter events, 0.2 us)
Async XLA Ops:
  7.2 209.5 %reduce-scatter.2.cloned.1.call-start = ((), (), s32[]{:S(2)}) async-start(), calls=%async_computation.1 | async-start | bytes 3981312 | tf_op jit(solution)/shard_map/reduce_scatter | solution.py:89
  10.0 11.5 %copy-start.5 = (bf16[1,2304,56]{1,2,0:T(8,128)(2,1)S(1)}, bf16[1,2304,56]{1,2,0:T(8,128)(2,1)}, u32[]{:S(2)}) copy-start(bf16[1,2304,56]{1,2,0:T(8,128)(2,1)} %param.9) | copy-start | bytes 774148
  15.4 1.4 copy-start
  17.8 8.5 %collective-permute-start = (bf16[48,8,512]{2,1,0:T(8,128)(2,1)}, bf16[48,8,512]{2,1,0:T(8,128)(2,1)S(1)}, u32[]{:S(2)}, u32[]{:S(2)}) collective-permute-start(bf16[48,8,512]{2,1,0:T(8,128)(2,1)} %get-tuple-element.6), channel_id=1, source_target_pairs={{0,1},{2,3},{4,5},{6,7},{8,9},{10,11},{12,13},{14,15},{16,17},{18,... | collective-permute-start | bytes 1179656 | tf_op jit(solution)/shard_map/ppermute | solution.py:20
  20.2 6.1 %collective-permute-start.1 = (bf16[48,8,512]{2,1,0:T(8,128)(2,1)}, bf16[48,8,512]{2,1,0:T(8,128)(2,1)S(1)}, u32[]{:S(2)}, u32[]{:S(2)}) collective-permute-start(bf16[48,8,512]{2,1,0:T(8,128)(2,1)} %get-tuple-element.7), channel_id=1, source_target_pairs={{1,0},{3,2},{5,4},{7,6},{9,8},{11,10},{13,12},{15,14},{17,16},{19,... | collective-permute-start | bytes 1179656 | tf_op jit(solution)/shard_map/ppermute | solution.py:23
  22.5 3.9 %copy-start.1 = (bf16[2304,512]{1,0:T(8,128)(2,1)S(1)}, bf16[2304,512]{1,0:T(8,128)(2,1)}, u32[]{:S(2)}) copy-start(bf16[2304,512]{1,0:T(8,128)(2,1)} %copy-done) | copy-start | bytes 7077892
  26.3 44.5 %slice-start = ((s8[4718592]{0:T(1024)(128)(4,1)}), s8[4194304]{0:T(1024)(128)(4,1)S(1)}, s32[]{:S(2)}) async-start(s8[4718592]{0:T(1024)(128)(4,1)} %bitcast.352), calls=%async_computation.3 | async-start | bytes 8388608
  26.9 43.9 %copy-start.2 = (bf16[1,2304,512]{2,1,0:T(8,128)(2,1)S(1)}, bf16[1,2304,512]{2,1,0:T(8,128)(2,1)}, u32[]{:S(2)}) copy-start(bf16[1,2304,512]{2,1,0:T(8,128)(2,1)} %param.8) | copy-start | bytes 7077892
  26.9 43.9 %copy-start.6 = (bf16[1,384,512]{2,1,0:T(8,128)(2,1)S(1)}, bf16[1,384,512]{2,1,0:T(8,128)(2,1)}, u32[]{:S(2)}) copy-start(bf16[1,384,512]{2,1,0:T(8,128)(2,1)} %param.11) | copy-start | bytes 1179652
  26.9 43.9 %slice-start.1 = ((s8[4718592]{0:T(1024)(128)(4,1)}), s8[524288]{0:T(1024)(128)(4,1)S(1)}, s32[]{:S(2)}) async-start(s8[4718592]{0:T(1024)(128)(4,1)} %bitcast.352), calls=%async_computation.4 | async-start | bytes 1048576
  73.7 4.6 %collective-permute-start.2 = (bf16[48,8,512]{2,1,0:T(8,128)(2,1)S(1)}, bf16[48,8,512]{2,1,0:T(8,128)(2,1)S(1)}, u32[]{:S(2)}, u32[]{:S(2)}) collective-permute-start(bf16[48,8,512]{2,1,0:T(8,128)(2,1)S(1)} %get-tuple-element.4), channel_id=1, source_target_pairs={{0,1},{2,3},{4,5},{6,7},{8,9},{10,11},{12,13},{14,15},{16,17},{18,... | collective-permute-start | bytes 1179656 | tf_op jit(solution)/shard_map/ppermute | solution.py:20
  76.8 3.6 %collective-permute-start.3 = (bf16[48,8,512]{2,1,0:T(8,128)(2,1)S(1)}, bf16[48,8,512]{2,1,0:T(8,128)(2,1)S(1)}, u32[]{:S(2)}, u32[]{:S(2)}) collective-permute-start(bf16[48,8,512]{2,1,0:T(8,128)(2,1)S(1)} %get-tuple-element.5), channel_id=1, source_target_pairs={{1,0},{3,2},{5,4},{7,6},{9,8},{11,10},{13,12},{15,14},{17,16},{19,... | collective-permute-start | bytes 1179656 | tf_op jit(solution)/shard_map/ppermute | solution.py:23
  124.9 1.4 copy-start.3
  127.6 7.2 %copy-start.4 = (f32[384,512]{1,0:T(8,128)}, f32[384,512]{1,0:T(8,128)S(1)}, u32[]{:S(2)}) copy-start(f32[384,512]{1,0:T(8,128)S(1)} %fusion.41) | copy-start | bytes 2359300
  134.8 130.2 %all-gather.2.cloned.1.call-start = ((), (), s32[]{:S(2)}) async-start(), calls=%async_computation.2 | async-start | bytes 1990656 | tf_op jit(solution)/shard_map/all_gather | solution.py:100
Sparse Core Ops, SparseCore 0:
  134.9 81.7 reduce-scatter.1
  219.5 45.4 all-gather.1
where the time goes:
time: 275 us
  waiting for transfers between devices  104 us (38%)
  other arithmetic  100 us (36%)
  blocking collectives  23.1 us (8%)
  matrix products  16.7 us (6%)
  between operations  15 us (5%)
  starting transfers between devices  8.32 us (3%)
  local copies, waits for them, and re-layouts  7.67 us (3%)
    convert_element_type x2, other arithmetic, cycle_back(): return total.reshape(TILE_SIDE * TILE_SIDE, frames).astype(jnp.bfloat16)  87.8 us
    reduce_scatter x1, waiting for transfers between devices, shards(): lax.psum_scatter(lax.dot_general(ferr, trace, (((1,), (1,)), ((), ())), p...  55.1 us
    all_gather x1, waiting for transfers between devices, shards(): new_foot = lax.all_gather(moved_share, 'tm', axis=0, tiled=True)  46.4 us
    psum x1, blocking collectives, shards(): energy_all = lax.psum(energy, 'tm')  23.1 us
    dot_general x1, matrix products, shards(): lax.dot_general(ferr, trace, (((1,), (1,)), ((), ())), preferred_element_...  7.19 us
    dot_general x2, matrix products, shards(): prod = jnp.dot(foot, trace, preferred_element_type=jnp.float32)  6.83 us
    unnamed x19, local copies, waits for them, and re-layouts  5.74 us
  transfers between devices with their start and end apart: 6, of which 3 were waited for; matrix products, arithmetic and copies ran while one was open for 3% of the time, Pallas kernels for 0%

commit v1 on v0

v1 whole, which is shorter than its diff:
```python
import functools

import jax
import jax.numpy as jnp
import numpy as np
from jax import lax
from jax.experimental import pallas as pl
from jax.experimental.pallas import tpu as pltpu
from jax.sharding import PartitionSpec as P

SIDE = 48
CYCLE = 8
PASSES = 2
RIDGE = 1.0
MAX_RADIUS = 9
BAND = 8
LANES = 128

FOLD_R = 16
FOLD_C = 19
FOLD_SHIFT = 9
SLOTS = FOLD_R * FOLD_C

f32 = jnp.float32
bf16 = jnp.bfloat16
i32 = jnp.int32


def cycle_offsets():
    found = []
    for dy in range(-CYCLE, CYCLE + 1):
        for dx in range(-CYCLE, CYCLE + 1):
            if CYCLE * CYCLE <= dy * dy + dx * dx < (CYCLE + 1) * (CYCLE + 1):
                found.append((dy, dx))
    return found


def band_tables():
    offsets = cycle_offsets()
    none = len(offsets)
    own = np.full((BAND, SIDE, BAND + 2 * CYCLE, SIDE), none, np.int32)
    for o, (dy, dx) in enumerate(offsets):
        for i in range(BAND):
            for c in range(max(0, -dx), min(SIDE, SIDE - dx)):
                own[i, c, i + CYCLE + dy, c + dx] = o
    own = own.reshape(BAND * SIDE, (BAND + 2 * CYCLE) * SIDE)
    beside = np.full((2, BAND, CYCLE, 32, CYCLE), none, np.int32)
    for o, (dy, dx) in enumerate(offsets):
        for i in range(BAND):
            for q in range(CYCLE):
                h = q + dx - CYCLE
                if 0 <= h < CYCLE:
                    beside[0, i, q, i + CYCLE + dy, h] = o
                h = q + dx + CYCLE
                if 0 <= h < CYCLE:
                    beside[1, i, q, i + CYCLE + dy, h] = o
    return own, beside.reshape(2, BAND * CYCLE, 32 * CYCLE)


def fold_rows(parts):
    share = -(-SLOTS // parts)
    block = -(-(share + 2) // 8) * 8
    row, col = np.arange(SIDE * SIDE) // SIDE, np.arange(SIDE * SIDE) % SIDE
    slot = (row % FOLD_R) * FOLD_C + (col + FOLD_SHIFT * (row // FOLD_R)) % FOLD_C
    return (slot // share * block + slot % share).astype(np.int32), share, block


def params(mib=24):
    return pltpu.CompilerParams(vmem_limit_bytes=mib * 2**20)


VM = pl.BlockSpec(memory_space=pltpu.VMEM)
SM = pl.BlockSpec(memory_space=pltpu.SMEM)


def dot(a, b):
    return jnp.dot(a, b, preferred_element_type=f32)


def disc_limit(centre_row, radius, count, row):
    gap = row - centre_row
    live = lax.broadcasted_iota(i32, centre_row.shape, 1) < count
    return jnp.where(live, radius * radius - gap * gap, -1)


def col_gap_sq(centre_col):
    gap = lax.broadcasted_iota(i32, (SIDE, centre_col.shape[1]), 0) - centre_col
    return gap * gap


def resid_band(g, tile, movie_ref, foot, trace, d_ref, r_ref, pay_ref):
    band = BAND * SIDE
    rows = pl.ds(g * band, band)
    d = movie_ref[rows, :].astype(f32) - dot(foot, trace)
    d_ref[rows, :] = d
    r_ref[rows, :] = d.astype(bf16)
    d3 = d.reshape(BAND, SIDE, d.shape[1])
    edge = jnp.where(tile == 0, d3[:, SIDE - CYCLE :], d3[:, :CYCLE])
    pay_ref[pl.ds(g * BAND * CYCLE, BAND * CYCLE), :] = edge.reshape(BAND * CYCLE, d.shape[1]).astype(bf16)


def start_kernel(tile_ref, count_ref, movie_ref, fp_ref, tr_ref, cr_ref, cc_ref, rad_ref,
                 foot_ref, trace_ref, den_ref, d_ref, r_ref, pay_ref):
    count, tile = count_ref[0], tile_ref[0]
    comps = tr_ref.shape[0]
    live = lax.broadcasted_iota(i32, (comps, 1), 0) < count
    trace = jnp.where(live, tr_ref[...].astype(f32), 0.0).astype(bf16)
    trace_ref[...] = trace
    gap_sq = col_gap_sq(cc_ref[...])
    cr, rad = cr_ref[...], rad_ref[...]
    total = jnp.zeros((8, comps), f32)
    for g in range(SIDE // BAND):
        for i in range(BAND):
            row = g * BAND + i
            keep = gap_sq <= disc_limit(cr, rad, count, row)
            foot = jnp.where(keep, fp_ref[pl.ds(row * SIDE, SIDE), :].astype(f32), 0.0)
            foot_ref[pl.ds(row * SIDE, SIDE), :] = foot.astype(bf16)
            total = total + jnp.sum((foot * foot).reshape(SIDE // 8, 8, comps), axis=0)
        resid_band(g, tile, movie_ref, foot_ref[pl.ds(g * BAND * SIDE, BAND * SIDE), :], trace,
                   d_ref, r_ref, pay_ref)
    energy = jnp.sum(total, axis=0, keepdims=True) + RIDGE
    den_ref[...] = jnp.transpose(jnp.broadcast_to(energy, (LANES, comps)))


def banded(bands_ref, r_ref, x_ref):
    band = BAND * SIDE
    for g in range(SIDE // BAND):
        low = max(0, CYCLE - g * BAND)
        high = min(BAND + 2 * CYCLE, SIDE + CYCLE - g * BAND)
        first = (g * BAND + low - CYCLE) * SIDE
        x_ref[pl.ds(g * band, band), :] = dot(
            bands_ref[g, :, low * SIDE : high * SIDE], r_ref[pl.ds(first, (high - low) * SIDE), :])


def build_kernel(tile_ref, w_ref, own_ref, beside_ref, foot_ref, r_ref,
                 bands_ref, sides_ref, footT_ref, x_ref, wide):
    tile = tile_ref[0]
    wide[...] = jnp.zeros_like(wide)
    wide[:, : w_ref.shape[1]] = w_ref[...].astype(f32)
    reach = own_ref.shape[1]
    pick = beside_ref[tile]

    def one(g, carry):
        base = pl.multiple_of(g * (BAND * SIDE), BAND * SIDE)
        edges = []
        for i in range(BAND):
            w = wide[pl.ds(base + i * SIDE, SIDE), :]
            edges.append(jnp.where(tile == 0, w[SIDE - CYCLE :], w[:CYCLE]))
            for v in range(reach // LANES):
                lanes = slice(v * LANES, (v + 1) * LANES)
                if lanes.stop <= i * SIDE or lanes.start >= (i + 2 * CYCLE + 1) * SIDE:
                    block = jnp.zeros((SIDE, LANES), bf16)
                else:
                    index = own_ref[i * SIDE : (i + 1) * SIDE, lanes]
                    block = jnp.take_along_axis(w, index, axis=1).astype(bf16)
                bands_ref[g, i * SIDE : (i + 1) * SIDE, lanes] = block
        edge = jnp.concatenate(edges, axis=0)
        for v in range(2):
            lanes = slice(v * LANES, (v + 1) * LANES)
            sides_ref[g, :, lanes] = jnp.take_along_axis(edge, pick[:, lanes], axis=1).astype(bf16)
        return carry

    lax.fori_loop(0, SIDE // BAND, one, 0)
    footT_ref[...] = jnp.transpose(foot_ref[...])
    banded(bands_ref, r_ref, x_ref)


def banded_kernel(bands_ref, r_ref, x_ref):
    banded(bands_ref, r_ref, x_ref)


def trace_step(tile, count, halo_ref, sides_ref, x_ref, d_ref, footT_ref, trace_ref, den_ref,
               wide_halo, err, back_ref=None):
    frames = x_ref.shape[1]
    band, edge = BAND * SIDE, CYCLE * SIDE
    pad = CYCLE * CYCLE
    wide_halo[:pad, :] = jnp.zeros((pad, frames), bf16)
    wide_halo[pl.ds(pad, edge), :] = halo_ref[...]
    tail = wide_halo.shape[0] - pad - edge
    wide_halo[pl.ds(pad + edge, tail), :] = jnp.zeros((tail, frames), bf16)
    for g in range(SIDE // BAND):
        rows = pl.ds(g * band, band)
        reach = sides_ref.shape[2]
        side = dot(sides_ref[g], wide_halo[pl.ds(g * BAND * CYCLE, reach), :]).reshape(BAND, CYCLE, frames)
        left = jnp.where(tile == 0, 0.0, side)
        right = jnp.where(tile == 0, side, 0.0)
        x = x_ref[rows, :].reshape(BAND, SIDE, frames)
        x = jnp.concatenate(
            [x[:, :CYCLE] + left, x[:, CYCLE : SIDE - CYCLE], x[:, SIDE - CYCLE :] + right], axis=1)
        back = x.reshape(band, frames).astype(bf16)
        if back_ref is not None:
            back_ref[rows, :] = back
        err[rows, :] = (back.astype(f32) - d_ref[rows, :]).astype(bf16)
    grad = dot(footT_ref[...], err[...])
    comps = grad.shape[0]
    live = lax.broadcasted_iota(i32, (comps, 1), 0) < count
    moved = jnp.maximum(trace_ref[...].astype(f32) - grad / den_ref[:, :1], 0.0)
    return jnp.where(live, moved, 0.0)


def pass_kernel(tile_ref, count_ref, halo_ref, sides_ref, x_ref, d_ref, footT_ref, foot_ref, trace_ref, den_ref,
                movie_ref, new_trace_ref, new_d_ref, new_r_ref, pay_ref, wide_halo, err):
    tile, count = tile_ref[0], count_ref[0]
    trace = trace_step(tile, count, halo_ref, sides_ref, x_ref, d_ref, footT_ref, trace_ref, den_ref,
                       wide_halo, err).astype(bf16)
    new_trace_ref[...] = trace
    for g in range(SIDE // BAND):
        resid_band(g, tile, movie_ref, foot_ref[pl.ds(g * BAND * SIDE, BAND * SIDE), :], trace,
                   new_d_ref, new_r_ref, pay_ref)


def last_kernel(block, share, tile_ref, count_ref, halo_ref, sides_ref, x_ref, d_ref, footT_ref, foot_ref, trace_ref,
                den_ref, movie_ref, cr_ref, cc_ref, rad_ref, slot_ref,
                new_trace_ref, part_ref, ffold_ref, wide_halo, err, back, masked):
    tile, count = tile_ref[0], count_ref[0]
    trace = trace_step(tile, count, halo_ref, sides_ref, x_ref, d_ref, footT_ref, trace_ref, den_ref,
                       wide_halo, err, back).astype(bf16)
    new_trace_ref[...] = trace
    comps = trace.shape[0]
    tf = trace.astype(f32)
    energy = jnp.sum(tf * tf, axis=1, keepdims=True)
    energy = jnp.transpose(jnp.broadcast_to(energy, (comps, LANES)))[:1]
    high = energy.astype(bf16).astype(f32)
    low = energy - high
    gap_sq = col_gap_sq(cc_ref[...])
    cr, rad = cr_ref[...], rad_ref[...]
    band = BAND * SIDE
    for g in range(SIDE // BAND):
        rows = pl.ds(g * band, band)
        prod = dot(foot_ref[rows, :], trace)
        ferr = (prod + back[rows, :].astype(f32) - movie_ref[rows, :].astype(f32)).astype(bf16)
        grad = lax.dot_general(ferr, trace, (((1,), (1,)), ((), ())), preferred_element_type=f32)
        for i in range(BAND):
            row = g * BAND + i
            keep = gap_sq <= disc_limit(cr, rad, count, row)
            masked[pl.ds(row * SIDE, SIDE), :] = jnp.where(keep, grad[i * SIDE : (i + 1) * SIDE], 0.0).astype(bf16)
    packed = part_ref.shape[0]
    at = lax.broadcasted_iota(i32, (packed, slot_ref.shape[1]), 0)
    fold = jnp.where(at == slot_ref[...], 1.0, 0.0).astype(bf16)
    inner = lax.rem(lax.broadcasted_iota(i32, (packed, comps), 0), block)
    part = dot(fold, masked[...])
    part = jnp.where(inner == share, high, jnp.where(inner == share + 1, low, part))
    part_ref[...] = part.astype(bf16)
    ffold_ref[...] = dot(fold, foot_ref[...])


def share_kernel(share, me_ref, parts_ref, ffold_ref, out_ref):
    parts, block, comps = parts_ref.shape
    total = jnp.zeros((block, comps), f32)
    for j in range(parts):
        total = total + parts_ref[j].astype(f32)
    den = total[share : share + 1] + total[share + 1 : share + 2] + RIDGE
    foot = ffold_ref[pl.ds(pl.multiple_of(me_ref[0] * block, 8), block), :]
    moved = jnp.maximum(foot - total / den, 0.0).astype(bf16)
    for j in range(parts):
        out_ref[j] = moved


def unfold_kernel(count_ref, all_ref, slot_ref, cr_ref, cc_ref, rad_ref, out_ref):
    count = count_ref[0]
    rows_in = all_ref.shape[0]
    gap_sq = col_gap_sq(cc_ref[...])
    cr, rad = cr_ref[...], rad_ref[...]
    band = BAND * SIDE
    every = all_ref[...]
    for g in range(SIDE // BAND):
        at = lax.broadcasted_iota(i32, (band, rows_in), 1)
        unfold = jnp.where(at == slot_ref[pl.ds(g * band, band), :1], 1.0, 0.0).astype(bf16)
        wide = dot(unfold, every)
        for i in range(BAND):
            row = g * BAND + i
            keep = gap_sq <= disc_limit(cr, rad, count, row)
            out_ref[pl.ds(row * SIDE, SIDE), :] = jnp.where(keep, wide[i * SIDE : (i + 1) * SIDE], 0.0).astype(bf16)


def swap(x):
    count = lax.axis_size("tile")
    return lax.ppermute(x, "tile", [(i, count - 1 - i) for i in range(count)])


def shards(movie, cycle_weights, footprints, traces, centre_row, centre_col, radius, comp_count):
    assert lax.axis_size("tile") == 2
    parts = lax.axis_size("tm")
    movie, weights, fp, tr = movie[0], cycle_weights[0], footprints[0], traces[0]
    pixels, frames = movie.shape
    comps = tr.shape[0]
    band = BAND * SIDE
    bands = SIDE // BAND
    edge = SIDE * CYCLE
    tile = lax.axis_index("tile").astype(i32).reshape(1)
    me = lax.axis_index("tm").astype(i32).reshape(1)
    own, beside = band_tables()
    slots, share, block = fold_rows(parts)
    packed = parts * block
    sds = jax.ShapeDtypeStruct
    halo_pad = pltpu.VMEM((edge + 3 * CYCLE * CYCLE, frames), bf16)
    err_buf = pltpu.VMEM((pixels, frames), bf16)

    foot, trace, den, d, r, pay = pl.pallas_call(
        start_kernel,
        out_shape=(sds((pixels, comps), bf16), sds((comps, frames), bf16), sds((comps, LANES), f32),
                   sds((pixels, frames), f32), sds((pixels, frames), bf16), sds((edge, frames), bf16)),
        in_specs=[SM, SM] + [VM] * 6, out_specs=[VM] * 6, compiler_params=params(),
    )(tile, comp_count, movie, fp, tr, centre_row, centre_col, radius)
    halo = swap(pay)
    band_w, side_w, footT, x = pl.pallas_call(
        build_kernel,
        out_shape=(sds((bands, band, own.shape[1]), bf16), sds((bands, CYCLE * BAND, beside.shape[2]), bf16),
                   sds((comps, pixels), bf16), sds((pixels, frames), f32)),
        in_specs=[SM] + [VM] * 5, out_specs=[VM] * 4,
        scratch_shapes=[pltpu.VMEM((pixels, LANES), f32)], compiler_params=params(),
        cost_estimate=pl.CostEstimate(flops=4_000_000_000, bytes_accessed=20_000_000, transcendentals=0),
    )(tile, weights, jnp.asarray(own), jnp.asarray(beside), foot, r)
    trace, d, r, pay = pl.pallas_call(
        pass_kernel,
        out_shape=(sds((comps, frames), bf16), sds((pixels, frames), f32), sds((pixels, frames), bf16),
                   sds((edge, frames), bf16)),
        in_specs=[SM, SM] + [VM] * 9, out_specs=[VM] * 4,
        scratch_shapes=[halo_pad, err_buf], compiler_params=params(),
    )(tile, comp_count, halo, side_w, x, d, footT, foot, trace, den, movie)
    halo = swap(pay)
    x = pl.pallas_call(
        banded_kernel,
        out_shape=sds((pixels, frames), f32),
        in_specs=[VM, VM], out_specs=VM, compiler_params=params(),
        cost_estimate=pl.CostEstimate(flops=4_000_000_000, bytes_accessed=20_000_000, transcendentals=0),
    )(band_w, r)
    slot_lane = jnp.asarray(slots.reshape(1, pixels))
    slot_col = jnp.asarray(slots.reshape(pixels, 1))
    trace, part, ffold = pl.pallas_call(
        functools.partial(last_kernel, block, share),
        out_shape=(sds((comps, frames), bf16), sds((packed, comps), bf16), sds((packed, comps), f32)),
        in_specs=[SM, SM] + [VM] * 13, out_specs=[VM] * 3,
        scratch_shapes=[halo_pad, err_buf, pltpu.VMEM((pixels, frames), bf16), pltpu.VMEM((pixels, comps), bf16)],
        compiler_params=params(32),
    )(tile, comp_count, halo, side_w, x, d, footT, foot, trace, den, movie, centre_row, centre_col, radius, slot_lane)
    received = lax.all_to_all(part.reshape(parts, block, comps), "tm", 0, 0, tiled=False)
    moved = pl.pallas_call(
        functools.partial(share_kernel, share),
        out_shape=sds((parts, block, comps), bf16),
        in_specs=[SM, VM, VM], out_specs=VM, compiler_params=params(),
    )(me, received, ffold)
    every = lax.all_to_all(moved, "tm", 0, 0, tiled=False).reshape(packed, comps)
    new_foot = pl.pallas_call(
        unfold_kernel,
        out_shape=sds((pixels, comps), bf16),
        in_specs=[SM] + [VM] * 5, out_specs=VM, compiler_params=params(),
    )(comp_count, every, slot_col, centre_row, centre_col, radius)
    return (new_foot[None], trace[None])


def solution(mesh):
    in_specs = (
        P(("groups", "tile"), None, "tm"),
        P(("groups", "tile"), None, None),
        P(("groups", "tile"), None, None),
        P(("groups", "tile"), None, "tm"),
        P(("groups", "tile"), None),
        P(("groups", "tile"), None),
        P(("groups", "tile"), None),
        P(("groups", "tile")),
    )
    out_specs = (P(("groups", "tile"), None, None), P(("groups", "tile"), None, "tm"))
    return jax.shard_map(shards, mesh=mesh, in_specs=in_specs, out_specs=out_specs, check_vma=False)
```

time: 275 us -> 78.2 us (0.28)
  other arithmetic: 100 us -> 0 us
  waiting for transfers between devices: 104 us -> 8.86 us
  Pallas kernels: 0 us -> 26.3 us
  matrix products: 16.7 us -> 0 us
  local copies, waits for them, and re-layouts: 7.67 us -> 21.4 us
  between operations: 15 us -> 1.42 us
  blocking collectives: 23.1 us -> 11.6 us
    convert_element_type x3 -> x0, other arithmetic: 89.6 us -> none  [the longest x2 87.8 us: cycle_back(): return total.reshape(TILE_SIDE * TILE_SIDE, frames).astype(jnp.bfloat16)]
    reduce_scatter x1 -> x0, waiting for transfers between devices: 55.1 us -> none  [shards(): lax.psum_scatter(lax.dot_general(ferr, trace, (((1,), (1,)), ((), ())), p...]
    all_gather x1 -> x0, waiting for transfers between devices: 46.4 us -> none  [shards(): new_foot = lax.all_gather(moved_share, 'tm', axis=0, tiled=True)]
    pallas_call x0 -> x7, Pallas kernels: none -> 26.3 us  [the longest x1 9.62 us: shards(): pl.pallas_call(build_kernel, out_shape=(sds((bands, band, own.shape[1]),...]
    psum x1 -> x0, blocking collectives: 23.1 us -> none  [shards(): energy_all = lax.psum(energy, 'tm')]
    dot_general x5 -> x0, matrix products: 16.7 us -> none  [the longest x1 7.19 us: shards(): lax.dot_general(ferr, trace, (((1,), (1,)), ((), ())), preferred_element_...]
    unnamed x19 -> x41, local copies, waits for them, and re-layouts: 5.74 us -> 21.4 us
    all_to_all x0 -> x1, blocking collectives: none -> 11.6 us  [shards(): lax.all_to_all(moved, 'tm', 0, 0, tiled=False).reshape(packed, comps)]
  transfers between devices with their start and end apart: 6 -> 3, of which waited for: 3 -> 1; matrix products, arithmetic and copies ran while one was open for 3% -> 2% of each run, Pallas kernels for 0% -> 16%
where the time goes in v1:
time: 78.2 us; the launch traced here: 77.6 us
  Pallas kernels  26.3 us (34%)
  local copies, waits for them, and re-layouts  21.4 us (27%)
  blocking collectives  11.6 us (15%)
  waiting for transfers between devices  8.86 us (11%)
  starting transfers between devices  8.03 us (10%)
  between operations  1.42 us (2%)
    unnamed x41, local copies, waits for them, and re-layouts  21.4 us
    all_to_all x1, blocking collectives, shards(): lax.all_to_all(moved, 'tm', 0, 0, tiled=False).reshape(packed, comps)  11.6 us
    pallas_call x1, Pallas kernels, shards(): pl.pallas_call(build_kernel, out_shape=(sds((bands, band, own.shape[1]),...  9.62 us
    all_to_all x1, waiting for transfers between devices, shards(): lax.all_to_all(part.reshape(parts, block, comps), 'tm', 0, 0, tiled=False)  8.85 us
    all_to_all x1, starting transfers between devices, shards(): lax.all_to_all(part.reshape(parts, block, comps), 'tm', 0, 0, tiled=False)  7.45 us
    pallas_call x1, Pallas kernels, shards(): pl.pallas_call(functools.partial(last_kernel, block, share), out_shape=(s...  5.95 us
    pallas_call x1, Pallas kernels, shards(): pl.pallas_call(banded_kernel, out_shape=sds((pixels, frames), f32), in_sp...  2.81 us
    pallas_call x1, Pallas kernels, shards(): pl.pallas_call(pass_kernel, out_shape=(sds((comps, frames), bf16), sds((p...  2.75 us
  transfers between devices with their start and end apart: 3, of which 1 were waited for; matrix products, arithmetic and copies ran while one was open for 2% of the time, Pallas kernels for 16%

profile of v1, /device:TPU:0, one launch (start us, length us, event | category | flops | bytes accessed | tf_op | source)
XLA Modules:
  0.0 77.6 jit_solution(11392822065793217741)
XLA Ops:
  1.3 0.0 copy-start
  1.3 1.7 %copy-done = bf16[1,2304,512]{2,1,0:T(8,128)(2,1)S(1)} copy-done((bf16[1,2304,512]{2,1,0:T(8,128)(2,1)S(1)}, bf16[1,2304,512]{2,1,0:T(8,128)(2,1)}, u32[]{:S(2)}) %copy-start) | copy-done | bytes 2359320
  3.0 1.5 %copy-done.4 = bf16[1,2304,384]{2,1,0:T(8,128)(2,1)S(1)} copy-done((bf16[1,2304,384]{2,1,0:T(8,128)(2,1)S(1)}, bf16[1,2304,384]{2,1,0:T(8,128)(2,1)}, u32[]{:S(2)}) %copy-start.4) | copy-done | bytes 1769496
  4.4 1.0 %copy-done.6 = bf16[1,384,512]{2,1,0:T(8,128)(2,1)S(1)} copy-done((bf16[1,384,512]{2,1,0:T(8,128)(2,1)S(1)}, bf16[1,384,512]{2,1,0:T(8,128)(2,1)}, u32[]{:S(2)}) %copy-start.6) | copy-done | bytes 393240
  5.4 0.7 copy-done.7
  6.1 0.7 copy-done.9
  6.8 0.7 copy-done.11
  7.5 2.5 %shard_map.131 = (bf16[2304,384]{1,0:T(8,128)(2,1)S(1)}, bf16[384,512]{1,0:T(8,128)(2,1)S(1)}, f32[384,128]{1,0:T(8,128)S(1)}, f32[2304,512]{1,0:T(8,128)S(1)}, ...) custom-call(s32[1]{0:T(128)} %bitcast.1.tile_ref, s32[1]{0:T(128)S(6)} %copy.15.count_ref, ...), custom_call_target="tpu_custom_call" | custom-call | tf_op jit(solution)/shard_map/pallas_call | solution.py:299
  10.0 2.2 %copy-done.2 = f32[2304,512]{1,0:T(8,128)} copy-done((f32[2304,512]{1,0:T(8,128)}, f32[2304,512]{1,0:T(8,128)S(1)}, u32[]{:S(2)}) %copy-start.2) | copy-done | bytes 4718616
  12.2 1.4 %copy-done.14 = bf16[2304,512]{1,0:T(8,128)(2,1)} copy-done((bf16[2304,512]{1,0:T(8,128)(2,1)}, bf16[2304,512]{1,0:T(8,128)(2,1)S(1)}, u32[]{:S(2)}) %copy-start.14) | copy-done | bytes 2359320
  13.6 0.5 collective-permute-start
  14.1 1.3 %copy.14 = bf16[1,2304,56]{2,1,0:T(8,128)(2,1)S(1)} copy(bf16[1,2304,56]{1,2,0:T(8,128)(2,1)} %param.13) | data formatting | bytes 516096 | tf_op args[1]
  15.4 0.0 copy-done.17
  15.4 0.0 copy-start.15
  15.4 1.7 %copy-done.15 = bf16[2304,512]{1,0:T(8,128)(2,1)S(1)} copy-done((bf16[2304,512]{1,0:T(8,128)(2,1)S(1)}, bf16[2304,512]{1,0:T(8,128)(2,1)}, u32[]{:S(2)}) %copy-start.15) | copy-done | bytes 2359320
  17.1 1.5 %copy-done.16 = s32[384,1152]{1,0:T(8,128)S(1)} copy-done((s32[384,1152]{1,0:T(8,128)S(1)}, s32[384,1152]{1,0:T(8,128)}, u32[]{:S(2)}) %copy-start.16) | copy-done | bytes 1769496
  18.5 9.6 %shard_map.132 = (bf16[6,384,1152]{2,1,0:T(8,128)(2,1)S(1)}, bf16[6,64,256]{2,1,0:T(8,128)(2,1)S(1)}, bf16[384,2304]{1,0:T(8,128)(2,1)S(1)}, f32[2304,512]{1,0:T(8,128)S(1)}) custom-call(s32[1]{0:T(128)} %bitcast.1.tile_ref, bf16[2304,56]{1,0:T(8,128)(2,1)S(1)} %bitcast.15, s32[384,1152]{1,0:T(8,128)S(1)} %copy-done.16, s32[2,64,256]{2,1,0:T(8,128)S(1)} %copy-done.17, ...), custom_call_target="tpu_custom_call" | custom-call | flops 4000000000 | bytes 20000000 | tf_op jit(solution)/shard_map/pallas_call | solution.py:306
  28.2 2.3 %copy-done.18 = bf16[6,384,1152]{2,1,0:T(8,128)(2,1)} copy-done((bf16[6,384,1152]{2,1,0:T(8,128)(2,1)}, bf16[6,384,1152]{2,1,0:T(8,128)(2,1)S(1)}, u32[]{:S(2)}) %copy-start.18) | copy-done | bytes 5308440
  30.5 0.0 collective-permute-done.halo_ref
  30.5 2.3 %copy-done.3 = f32[2304,512]{1,0:T(8,128)S(1)} copy-done((f32[2304,512]{1,0:T(8,128)S(1)}, f32[2304,512]{1,0:T(8,128)}, u32[]{:S(2)}) %copy-start.3) | copy-done | bytes 4718616
  32.8 2.7 %shard_map.133 = (bf16[384,512]{1,0:T(8,128)(2,1)S(1)}, f32[2304,512]{1,0:T(8,128)S(1)}, bf16[2304,512]{1,0:T(8,128)(2,1)S(1)}, bf16[384,512]{1,0:T(8,128)(2,1)S(1)}) custom-call(s32[1]{0:T(128)} %bitcast.1.tile_ref, s32[1]{0:T(128)S(6)} %copy.15.count_ref, bf16[384,512]{1,0:T(8,128)(2,1)S(1)} %collective-permute-done.halo_ref, ...), custom_call_target="tpu_custom_call" | custom-call | tf_op jit(solution)/shard_map/pallas_call | solution.py:314
  35.6 0.1 collective-permute-start.1
  35.7 2.5 %copy-done.19 = bf16[6,384,1152]{2,1,0:T(8,128)(2,1)S(1)} copy-done((bf16[6,384,1152]{2,1,0:T(8,128)(2,1)S(1)}, bf16[6,384,1152]{2,1,0:T(8,128)(2,1)}, u32[]{:S(2)}) %copy-start.19) | copy-done | bytes 5308440
  38.2 2.8 %shard_map.134.x_ref = f32[2304,512]{1,0:T(8,128)S(1)} custom-call(bf16[6,384,1152]{2,1,0:T(8,128)(2,1)S(1)} %copy-done.19, bf16[2304,512]{1,0:T(8,128)(2,1)S(1)} %get-tuple-element.30.r_ref), custom_call_target="tpu_custom_call" | custom-call | flops 4000000000 | bytes 20000000 | tf_op jit(solution)/shard_map/pallas_call | solution.py:322
  41.0 0.0 collective-permute-done.1.halo_ref
  41.1 5.9 %shard_map.135 = (bf16[384,512]{1,0:T(8,128)(2,1)}, bf16[320,384]{1,0:T(8,128)(2,1)}, f32[320,384]{1,0:T(8,128)S(1)}) custom-call(s32[1]{0:T(128)} %bitcast.1.tile_ref, s32[1]{0:T(128)S(6)} %copy.15.count_ref, bf16[384,512]{1,0:T(8,128)(2,1)S(1)} %collective-permute-done.1.halo_ref, bf16[6,64,256]{2,1,0:T(8,128)(2,1)S(1)} %get-tuple-element.22.sides_ref, ...), custom_call_target="tpu_custom_call" | custom-call | tf_op jit(solution)/shard_map/pallas_call | solution.py:330
  47.0 0.0 copy-start.5
  47.0 7.5 %all-to-all-start = ((bf16[8,40,384]{2,1,0:T(8,128)(2,1)}), bf16[8,40,384]{2,1,0:T(8,128)(2,1)S(1)}, u32[]{:S(2)}, u32[]{:S(2)}) async-start(bf16[8,40,384]{2,1,0:T(8,128)(2,1)} %bitcast.6), calls=%async_computation | async-start | bytes 491520 | tf_op jit(solution)/shard_map/all_to_all | solution.py:337
  54.5 8.9 %all-to-all-done.parts_ref = bf16[8,40,384]{2,1,0:T(8,128)(2,1)S(1)} async-done(((bf16[8,40,384]{2,1,0:T(8,128)(2,1)}), bf16[8,40,384]{2,1,0:T(8,128)(2,1)S(1)}, u32[]{:S(2)}, u32[]{:S(2)}) %all-to-all-start) | async-done | bytes 245792 | tf_op jit(solution)/shard_map/all_to_all | solution.py:337
  63.3 0.1 shard_map.136
  63.4 11.6 %all_to_all.10 = bf16[8,40,384]{2,1,0:T(8,128)(2,1)S(1)} all-to-all(bf16[8,40,384]{2,1,0:T(8,128)(2,1)S(1)} %shard_map.136), channel_id=1, replica_groups=mesh['groups'=2,'tm'=8,'tile'=2] {'tm'}, dimensions={0} | all-to-all | bytes 491520 | tf_op jit(solution)/shard_map/all_to_all | solution.py:343
  75.0 2.6 %shard_map.137 = bf16[2304,384]{1,0:T(8,128)(2,1)} custom-call(s32[1]{0:T(128)S(6)} %copy.15.count_ref, bf16[320,384]{1,0:T(8,128)(2,1)S(1)} %bitcast.14, s32[2304,1]{1,0:T(8,128)S(1)} %copy-done.5, s32[1,384]{1,0:T(1,128)S(1)} %copy-done.8, s32[1,384]{1,0:T(1,128)S(1)} %copy-done.10, s32[1,384]{1,0:T(1,128)S(1)} %copy-done.12), custom_call_target="tpu_custom_call" | custom-call | tf_op jit(solution)/shard_map/pallas_call | solution.py:344
  (23 shorter events, 0.0 us)
Async XLA Ops:
  1.3 1.7 %copy-start = (bf16[1,2304,512]{2,1,0:T(8,128)(2,1)S(1)}, bf16[1,2304,512]{2,1,0:T(8,128)(2,1)}, u32[]{:S(2)}) copy-start(bf16[1,2304,512]{2,1,0:T(8,128)(2,1)} %param.12) | copy-start | bytes 7077892
  2.9 1.5 %copy-start.4 = (bf16[1,2304,384]{2,1,0:T(8,128)(2,1)S(1)}, bf16[1,2304,384]{2,1,0:T(8,128)(2,1)}, u32[]{:S(2)}) copy-start(bf16[1,2304,384]{2,1,0:T(8,128)(2,1)} %param.14) | copy-start | bytes 5308420
  4.4 1.0 %copy-start.6 = (bf16[1,384,512]{2,1,0:T(8,128)(2,1)S(1)}, bf16[1,384,512]{2,1,0:T(8,128)(2,1)}, u32[]{:S(2)}) copy-start(bf16[1,384,512]{2,1,0:T(8,128)(2,1)} %param.15) | copy-start | bytes 1179652
  5.4 0.7 copy-start.7
  6.1 0.7 copy-start.9
  6.8 0.7 copy-start.11
  7.5 7.9 %copy-start.17 = (s32[2,64,256]{2,1,0:T(8,128)S(1)}, s32[2,64,256]{2,1,0:T(8,128)}, u32[]{:S(2)}) copy-start(s32[2,64,256]{2,1,0:T(8,128)} %constant.17.clone.beside_ref) | copy-start | bytes 393220
  10.0 2.2 %copy-start.2 = (f32[2304,512]{1,0:T(8,128)}, f32[2304,512]{1,0:T(8,128)S(1)}, u32[]{:S(2)}) copy-start(f32[2304,512]{1,0:T(8,128)S(1)} %get-tuple-element.24.d_ref) | copy-start | bytes 14155780
  12.2 1.4 %copy-start.14 = (bf16[2304,512]{1,0:T(8,128)(2,1)}, bf16[2304,512]{1,0:T(8,128)(2,1)S(1)}, u32[]{:S(2)}) copy-start(bf16[2304,512]{1,0:T(8,128)(2,1)S(1)} %get-tuple-element.21.r_ref) | copy-start | bytes 7077892
  13.6 16.9 %collective-permute-start = (bf16[384,512]{1,0:T(8,128)(2,1)}, bf16[384,512]{1,0:T(8,128)(2,1)S(1)}, u32[]{:S(2)}, u32[]{:S(2)}) collective-permute-start(bf16[384,512]{1,0:T(8,128)(2,1)} %get-tuple-element.19), channel_id=1, source_target_pairs={{0,1},{1,0},{2,3},{3,2},{4,5},{5,4},{6,7},{7,6},{8,9},{9,8},{10,11... | collective-permute-start | bytes 1179656 | tf_op jit(solution)/shard_map/ppermute | solution.py:278
  15.4 1.7 %copy-start.15 = (bf16[2304,512]{1,0:T(8,128)(2,1)S(1)}, bf16[2304,512]{1,0:T(8,128)(2,1)}, u32[]{:S(2)}) copy-start(bf16[2304,512]{1,0:T(8,128)(2,1)} %copy-done.14) | copy-start | bytes 7077892
  17.1 1.5 %copy-start.16 = (s32[384,1152]{1,0:T(8,128)S(1)}, s32[384,1152]{1,0:T(8,128)}, u32[]{:S(2)}) copy-start(s32[384,1152]{1,0:T(8,128)} %constant.16.clone.own_ref) | copy-start | bytes 5308420
  18.5 12.0 %copy-start.1 = (bf16[1,2304,512]{2,1,0:T(8,128)(2,1)S(1)}, bf16[1,2304,512]{2,1,0:T(8,128)(2,1)}, u32[]{:S(2)}) copy-start(bf16[1,2304,512]{2,1,0:T(8,128)(2,1)} %param.12) | copy-start | bytes 7077892
  28.2 2.3 %copy-start.18 = (bf16[6,384,1152]{2,1,0:T(8,128)(2,1)}, bf16[6,384,1152]{2,1,0:T(8,128)(2,1)S(1)}, u32[]{:S(2)}) copy-start(bf16[6,384,1152]{2,1,0:T(8,128)(2,1)S(1)} %get-tuple-element.29.bands_ref) | copy-start | bytes 15925252
  30.5 2.3 %copy-start.3 = (f32[2304,512]{1,0:T(8,128)S(1)}, f32[2304,512]{1,0:T(8,128)}, u32[]{:S(2)}) copy-start(f32[2304,512]{1,0:T(8,128)} %copy-done.2) | copy-start | bytes 14155780
  35.6 5.4 %collective-permute-start.1 = (bf16[384,512]{1,0:T(8,128)(2,1)S(1)}, bf16[384,512]{1,0:T(8,128)(2,1)S(1)}, u32[]{:S(2)}, u32[]{:S(2)}) collective-permute-start(bf16[384,512]{1,0:T(8,128)(2,1)S(1)} %get-tuple-element.28), channel_id=1, source_target_pairs={{0,1},{1,0},{2,3},{3,2},{4,5},{5,4},{6,7},{7,6},{8,9},{9,8},{10,11... | collective-permute-start | bytes 1179656 | tf_op jit(solution)/shard_map/ppermute | solution.py:278
  35.7 2.5 %copy-start.19 = (bf16[6,384,1152]{2,1,0:T(8,128)(2,1)S(1)}, bf16[6,384,1152]{2,1,0:T(8,128)(2,1)}, u32[]{:S(2)}) copy-start(bf16[6,384,1152]{2,1,0:T(8,128)(2,1)} %copy-done.18) | copy-start | bytes 15925252
  38.2 2.8 %copy-start.8 = (s32[1,384]{1,0:T(1,128)S(1)}, s32[1,384]{1,0:T(1,128)}, u32[]{:S(2)}) copy-start(s32[1,384]{1,0:T(1,128)} %cr_ref.5) | copy-start | bytes 4612
  38.2 2.8 %copy-start.10 = (s32[1,384]{1,0:T(1,128)S(1)}, s32[1,384]{1,0:T(1,128)}, u32[]{:S(2)}) copy-start(s32[1,384]{1,0:T(1,128)} %cc_ref.5) | copy-start | bytes 4612
  38.2 2.9 %copy-start.12 = (s32[1,384]{1,0:T(1,128)S(1)}, s32[1,384]{1,0:T(1,128)}, u32[]{:S(2)}) copy-start(s32[1,384]{1,0:T(1,128)} %rad_ref.5) | copy-start | bytes 4612
  38.2 2.9 %copy-start.13 = (s32[1,2304]{1,0:T(1,128)S(1)}, s32[1,2304]{1,0:T(1,128)}, u32[]{:S(2)}) copy-start(s32[1,2304]{1,0:T(1,128)} %constant.18.clone.slot_ref) | copy-start | bytes 27652
  47.0 28.0 %copy-start.5 = (s32[2304,1]{1,0:T(8,128)S(1)}, s32[2304,1]{1,0:T(8,128)}, u32[]{:S(2)}) copy-start(s32[2304,1]{1,0:T(8,128)} %constant.19.clone.slot_ref) | copy-start | bytes 27652
  47.0 16.3 %all-to-all-start = ((bf16[8,40,384]{2,1,0:T(8,128)(2,1)}), bf16[8,40,384]{2,1,0:T(8,128)(2,1)S(1)}, u32[]{:S(2)}, u32[]{:S(2)}) async-start(bf16[8,40,384]{2,1,0:T(8,128)(2,1)} %bitcast.6), calls=%async_computation | async-start | bytes 491520 | tf_op jit(solution)/shard_map/all_to_all | solution.py:337

commit v2 on v1

v2 whole, which is shorter than its diff:
```python
import functools

import jax
import jax.numpy as jnp
import numpy as np
from jax import lax
from jax.experimental import pallas as pl
from jax.experimental.pallas import tpu as pltpu
from jax.sharding import PartitionSpec as P

SIDE = 48
CYCLE = 8
PASSES = 2
RIDGE = 1.0
MAX_RADIUS = 9
BAND = 8
LANES = 128
OFFS_PAD = 64

FOLD_R = 16
FOLD_C = 19
FOLD_SHIFT = 9
SLOTS = FOLD_R * FOLD_C

f32 = jnp.float32
bf16 = jnp.bfloat16
i32 = jnp.int32


def cycle_offsets():
    found = []
    for dy in range(-CYCLE, CYCLE + 1):
        for dx in range(-CYCLE, CYCLE + 1):
            if CYCLE * CYCLE <= dy * dy + dx * dx < (CYCLE + 1) * (CYCLE + 1):
                found.append((dy, dx))
    return found


def band_tables():
    offsets = cycle_offsets()
    none = len(offsets)
    reach = (BAND + 2 * CYCLE) * SIDE
    own = np.full((OFFS_PAD, 1), -1, np.int32)
    beside = np.full((2, BAND, CYCLE, 32, CYCLE), none, np.int32)
    for o, (dy, dx) in enumerate(offsets):
        own[o, 0] = ((CYCLE + dy) * SIDE + dx) % reach
        for i in range(BAND):
            for q in range(CYCLE):
                h = q + dx - CYCLE
                if 0 <= h < CYCLE:
                    beside[0, i, q, i + CYCLE + dy, h] = o
                h = q + dx + CYCLE
                if 0 <= h < CYCLE:
                    beside[1, i, q, i + CYCLE + dy, h] = o
    return own, beside.reshape(2, BAND * CYCLE, 32 * CYCLE)


def fold_rows(parts):
    share = -(-SLOTS // parts)
    block = -(-(share + 2) // 8) * 8
    assert SLOTS // 2 % share == 0 and FOLD_R == 2 * BAND
    low = np.arange(SIDE // FOLD_R)[:, None, None]
    row, col = np.arange(BAND)[:, None], np.arange(SIDE)
    slot = row * FOLD_C + (col + FOLD_SHIFT * low) % FOLD_C
    return (slot // share * block + slot % share).astype(np.int32).reshape(1, -1), share, block


def params(mib=12):
    return pltpu.CompilerParams(vmem_limit_bytes=mib * 2**20)


VM = pl.BlockSpec(memory_space=pltpu.VMEM)
HB = pl.BlockSpec(memory_space=pltpu.HBM)
SM = pl.BlockSpec(memory_space=pltpu.SMEM)


def dot(a, b):
    return jnp.dot(a, b, preferred_element_type=f32)


def disc_limit(centre_row, radius, count, row):
    gap = row - centre_row
    live = lax.broadcasted_iota(i32, centre_row.shape, 1) < count
    return jnp.where(live, radius * radius - gap * gap, -1)


def col_gap_sq(centre_col):
    gap = lax.broadcasted_iota(i32, (SIDE, centre_col.shape[1]), 0) - centre_col
    return gap * gap


def resid_band(g, tile, movie_ref, foot, trace, d_ref, r_ref, pay_ref):
    band = BAND * SIDE
    rows = pl.ds(g * band, band)
    d = movie_ref[rows, :].astype(f32) - dot(foot, trace)
    d_ref[rows, :] = d
    r_ref[rows, :] = d.astype(bf16)
    d3 = d.reshape(BAND, SIDE, d.shape[1])
    edge = jnp.where(tile == 0, d3[:, SIDE - CYCLE :], d3[:, :CYCLE])
    pay_ref[pl.ds(g * BAND * CYCLE, BAND * CYCLE), :] = edge.reshape(BAND * CYCLE, d.shape[1]).astype(bf16)


def start_kernel(tile_ref, count_ref, movie_hbm, fp_hbm, tr_hbm, cr_hbm, cc_hbm, rad_hbm,
                 foot_ref, trace_ref, den_ref, d_ref, r_ref, pay_ref, movie_ref,
                 fp_ref, tr_ref, cr_ref, cc_ref, rad_ref, sems):
    count, tile = count_ref[0], tile_ref[0]
    comps = tr_ref.shape[0]
    band = BAND * SIDE
    bands = SIDE // BAND
    small = [pltpu.make_async_copy(src, dst, sems.at[2 * bands + n]) for n, (src, dst) in enumerate(
        ((cr_hbm, cr_ref), (cc_hbm, cc_ref), (rad_hbm, rad_ref), (tr_hbm, tr_ref)))]
    fps, movies = [], []
    for g in range(bands):
        rows = pl.ds(g * band, band)
        fps.append(pltpu.make_async_copy(fp_hbm.at[rows, :], fp_ref.at[rows, :], sems.at[g]))
        movies.append(pltpu.make_async_copy(movie_hbm.at[rows, :], movie_ref.at[rows, :], sems.at[bands + g]))
    for n, copy in enumerate(small):
        copy.start()
    for g in range(bands):
        fps[g].start()
        movies[g].start()
    for copy in small:
        copy.wait()
    live = lax.broadcasted_iota(i32, (comps, 1), 0) < count
    trace = jnp.where(live, tr_ref[...].astype(f32), 0.0).astype(bf16)
    trace_ref[...] = trace
    gap_sq = col_gap_sq(cc_ref[...])
    cr, rad = cr_ref[...], rad_ref[...]
    total = jnp.zeros((8, comps), f32)
    for g in range(bands):
        fps[g].wait()
        for i in range(BAND):
            row = g * BAND + i
            keep = gap_sq <= disc_limit(cr, rad, count, row)
            foot = jnp.where(keep, fp_ref[pl.ds(row * SIDE, SIDE), :].astype(f32), 0.0)
            foot_ref[pl.ds(row * SIDE, SIDE), :] = foot.astype(bf16)
            total = total + jnp.sum((foot * foot).reshape(SIDE // 8, 8, comps), axis=0)
        movies[g].wait()
        resid_band(g, tile, movie_ref, foot_ref[pl.ds(g * band, band), :], trace, d_ref, r_ref, pay_ref)
    energy = jnp.sum(total, axis=0, keepdims=True) + RIDGE
    den_ref[...] = jnp.transpose(jnp.broadcast_to(energy, (LANES, comps)))


def banded(bands_ref, r_ref, x_ref):
    band = BAND * SIDE
    for g in range(SIDE // BAND):
        low = max(0, CYCLE - g * BAND)
        high = min(BAND + 2 * CYCLE, SIDE + CYCLE - g * BAND)
        first = (g * BAND + low - CYCLE) * SIDE
        x_ref[pl.ds(g * band, band), :] = dot(
            bands_ref[g, :, low * SIDE : high * SIDE], r_ref[pl.ds(first, (high - low) * SIDE), :])


def build_kernel(tile_ref, w_ref, own_ref, beside_ref, r_ref, bands_ref, sides_ref, x_ref, weights, wide):
    tile = tile_ref[0]
    bands = SIDE // BAND
    reach = bands_ref.shape[2]
    blocks = reach // LANES
    offs = w_ref.shape[0]
    eye = lax.broadcasted_iota(i32, (offs, LANES), 0) == lax.broadcasted_iota(i32, (offs, LANES), 1)
    weights[...] = lax.dot_general(w_ref[...], jnp.where(eye, 1.0, 0.0).astype(bf16), (((0,), (0,)), ((), ())),
                                   preferred_element_type=f32)
    pixel = lax.broadcasted_iota(i32, (SIDE, LANES), 0)
    lane = lax.broadcasted_iota(i32, (SIDE, LANES), 1)
    carried = lane < pixel
    period = 3
    inside = [jnp.abs(lax.rem(lane + v * LANES, SIDE) - pixel) <= CYCLE for v in range(period)]
    at = own_ref[...]
    target = lax.broadcasted_iota(i32, (OFFS_PAD, reach), 1)
    for i in range(BAND):
        moved = at + i * SIDE
        moved = jnp.where(moved >= reach, moved - reach, moved)
        pick = jnp.where(target == jnp.where(at < 0, -1, moved), 1.0, 0.0).astype(bf16)
        w = jnp.concatenate(
            [weights[(g * BAND + i) * SIDE : (g * BAND + i + 1) * SIDE, :OFFS_PAD] for g in range(bands)], axis=0)
        wide[...] = dot(w.astype(bf16), pick)
        for g in range(bands):
            turned = [pltpu.roll(wide[g * SIDE : (g + 1) * SIDE, v * LANES : (v + 1) * LANES], 0, 1,
                                 stride=1, stride_axis=0) for v in range(blocks)]
            for v in range(blocks):
                block = jnp.where(carried, turned[v - 1], turned[v])
                bands_ref[g, i * SIDE : (i + 1) * SIDE, v * LANES : (v + 1) * LANES] = jnp.where(
                    inside[v % period], block, 0.0).astype(bf16)
    beside = beside_ref[tile]
    for g in range(bands):
        edges = []
        for i in range(BAND):
            base = (g * BAND + i) * SIDE
            edges.append(jnp.where(tile == 0, weights[base + SIDE - CYCLE : base + SIDE, :],
                                   weights[base : base + CYCLE, :]))
        edge = jnp.concatenate(edges, axis=0)
        for v in range(2):
            lanes = slice(v * LANES, (v + 1) * LANES)
            sides_ref[g, :, lanes] = jnp.take_along_axis(edge, beside[:, lanes], axis=1).astype(bf16)
    banded(bands_ref, r_ref, x_ref)


def banded_kernel(bands_ref, r_ref, x_ref):
    banded(bands_ref, r_ref, x_ref)


def trace_step(tile, count, halo_ref, sides_ref, x_ref, d_ref, foot_ref, trace_ref, den_ref,
               wide_halo, err, back_ref=None):
    frames = x_ref.shape[1]
    band, edge = BAND * SIDE, CYCLE * SIDE
    pad = CYCLE * CYCLE
    wide_halo[:pad, :] = jnp.zeros((pad, frames), bf16)
    wide_halo[pl.ds(pad, edge), :] = halo_ref[...]
    tail = wide_halo.shape[0] - pad - edge
    wide_halo[pl.ds(pad + edge, tail), :] = jnp.zeros((tail, frames), bf16)
    for g in range(SIDE // BAND):
        rows = pl.ds(g * band, band)
        reach = sides_ref.shape[2]
        side = dot(sides_ref[g], wide_halo[pl.ds(g * BAND * CYCLE, reach), :]).reshape(BAND, CYCLE, frames)
        left = jnp.where(tile == 0, 0.0, side)
        right = jnp.where(tile == 0, side, 0.0)
        x = x_ref[rows, :].reshape(BAND, SIDE, frames)
        x = jnp.concatenate(
            [x[:, :CYCLE] + left, x[:, CYCLE : SIDE - CYCLE], x[:, SIDE - CYCLE :] + right], axis=1)
        back = x.reshape(band, frames).astype(bf16)
        if back_ref is not None:
            back_ref[rows, :] = back
        err[rows, :] = (back.astype(f32) - d_ref[rows, :]).astype(bf16)
    grad = lax.dot_general(foot_ref[...], err[...], (((0,), (0,)), ((), ())), preferred_element_type=f32)
    comps = grad.shape[0]
    live = lax.broadcasted_iota(i32, (comps, 1), 0) < count
    moved = jnp.maximum(trace_ref[...].astype(f32) - grad / den_ref[:, :1], 0.0)
    return jnp.where(live, moved, 0.0)


def pass_kernel(tile_ref, count_ref, halo_ref, sides_ref, x_ref, d_ref, foot_ref, trace_ref, den_ref,
                movie_ref, new_trace_ref, new_d_ref, new_r_ref, pay_ref, wide_halo, err):
    tile, count = tile_ref[0], count_ref[0]
    trace = trace_step(tile, count, halo_ref, sides_ref, x_ref, d_ref, foot_ref, trace_ref, den_ref,
                       wide_halo, err).astype(bf16)
    new_trace_ref[...] = trace
    for g in range(SIDE // BAND):
        resid_band(g, tile, movie_ref, foot_ref[pl.ds(g * BAND * SIDE, BAND * SIDE), :], trace,
                   new_d_ref, new_r_ref, pay_ref)


def last_kernel(block, share, tile_ref, count_ref, halo_ref, sides_ref, x_ref, d_ref, foot_ref, trace_ref,
                den_ref, movie_ref, cr_ref, cc_ref, rad_ref, slot_ref,
                trace_hbm, part_ref, fold_ref, wide_halo, err, back, masked, new_trace, sem):
    tile, count = tile_ref[0], count_ref[0]
    trace = trace_step(tile, count, halo_ref, sides_ref, x_ref, d_ref, foot_ref, trace_ref, den_ref,
                       wide_halo, err, back).astype(bf16)
    new_trace[...] = trace
    store = pltpu.make_async_copy(new_trace, trace_hbm, sem)
    store.start()
    comps = trace.shape[0]
    tf = trace.astype(f32)
    energy = jnp.sum(tf * tf, axis=1, keepdims=True)
    energy = jnp.transpose(jnp.broadcast_to(energy, (comps, LANES)))[:1]
    high = energy.astype(bf16).astype(f32)
    low = energy - high
    gap_sq = col_gap_sq(cc_ref[...])
    cr, rad = cr_ref[...], rad_ref[...]
    band = BAND * SIDE
    for g in range(SIDE // BAND):
        rows = pl.ds(g * band, band)
        prod = dot(foot_ref[rows, :], trace)
        ferr = (prod + back[rows, :].astype(f32) - movie_ref[rows, :].astype(f32)).astype(bf16)
        grad = lax.dot_general(ferr, trace, (((1,), (1,)), ((), ())), preferred_element_type=f32)
        for i in range(BAND):
            row = g * BAND + i
            keep = gap_sq <= disc_limit(cr, rad, count, row)
            masked[g % 2, pl.ds(g // 2 * band + i * SIDE, SIDE), :] = jnp.where(
                keep, grad[i * SIDE : (i + 1) * SIDE], 0.0).astype(bf16)
    half, taken = fold_ref.shape
    at = lax.broadcasted_iota(i32, (half, taken), 0)
    fold = jnp.where(at == slot_ref[...], 1.0, 0.0).astype(bf16)
    fold_ref[...] = fold
    inner = lax.rem(lax.broadcasted_iota(i32, (half, comps), 0), block)
    for h in range(2):
        part = dot(fold, masked[h])
        part = jnp.where(inner == share, high, jnp.where(inner == share + 1, low, part))
        part_ref[h * half : (h + 1) * half, :] = part.astype(bf16)
    store.wait()


def foot_fold_kernel(fold_ref, foot_ref, out_ref):
    half = fold_ref.shape[0]
    band = BAND * SIDE
    for h in range(2):
        foot = jnp.concatenate(
            [foot_ref[g * band : (g + 1) * band, :] for g in range(h, SIDE // BAND, 2)], axis=0)
        out_ref[h * half : (h + 1) * half, :] = dot(fold_ref[...], foot)


def share_kernel(share, me_ref, parts_ref, ffold_ref, out_ref):
    parts, block, comps = parts_ref.shape
    total = jnp.zeros((block, comps), f32)
    for j in range(parts):
        total = total + parts_ref[j].astype(f32)
    den = total[share : share + 1] + total[share + 1 : share + 2] + RIDGE
    foot = ffold_ref[pl.ds(pl.multiple_of(me_ref[0] * block, 8), block), :]
    moved = jnp.maximum(foot - total / den, 0.0).astype(bf16)
    for j in range(parts):
        out_ref[j] = moved


def unfold_kernel(count_ref, all_ref, fold_ref, cr_ref, cc_ref, rad_ref, out_hbm, buf, sems):
    count = count_ref[0]
    half = fold_ref.shape[0]
    gap_sq = col_gap_sq(cc_ref[...])
    cr, rad = cr_ref[...], rad_ref[...]
    band = BAND * SIDE
    stores = []
    for g in range(SIDE // BAND):
        h, b = g % 2, g // 2
        wide = lax.dot_general(fold_ref[:, b * band : (b + 1) * band], all_ref[h * half : (h + 1) * half, :],
                               (((0,), (0,)), ((), ())), preferred_element_type=f32)
        for i in range(BAND):
            row = g * BAND + i
            keep = gap_sq <= disc_limit(cr, rad, count, row)
            buf[pl.ds(row * SIDE, SIDE), :] = jnp.where(keep, wide[i * SIDE : (i + 1) * SIDE], 0.0).astype(bf16)
        rows = pl.ds(g * band, band)
        stores.append(pltpu.make_async_copy(buf.at[rows, :], out_hbm.at[rows, :], sems.at[g]))
        stores[-1].start()
    for store in stores:
        store.wait()


def swap(x):
    count = lax.axis_size("tile")
    return lax.ppermute(x, "tile", [(i, count - 1 - i) for i in range(count)])


def shards(movie, cycle_weights, footprints, traces, centre_row, centre_col, radius, comp_count):
    assert lax.axis_size("tile") == 2
    parts = lax.axis_size("tm")
    movie, fp, tr = movie[0], footprints[0], traces[0]
    weights = jnp.swapaxes(cycle_weights[0], 0, 1)
    pixels, frames = movie.shape
    comps = tr.shape[0]
    band = BAND * SIDE
    bands = SIDE // BAND
    edge = SIDE * CYCLE
    reach = (BAND + 2 * CYCLE) * SIDE
    tile = lax.axis_index("tile").astype(i32).reshape(1)
    me = lax.axis_index("tm").astype(i32).reshape(1)
    own, beside = band_tables()
    slots, share, block = fold_rows(parts)
    packed = parts * block
    sds = jax.ShapeDtypeStruct
    halo_pad = pltpu.VMEM((edge + 3 * CYCLE * CYCLE, frames), bf16)
    err_buf = pltpu.VMEM((pixels, frames), bf16)
    one_row = pltpu.VMEM((1, comps), i32)

    foot, trace, den, d, r, pay, movie = pl.pallas_call(
        start_kernel,
        out_shape=(sds((pixels, comps), bf16), sds((comps, frames), bf16), sds((comps, LANES), f32),
                   sds((pixels, frames), f32), sds((pixels, frames), bf16), sds((edge, frames), bf16),
                   sds((pixels, frames), bf16)),
        in_specs=[SM, SM] + [HB] * 6, out_specs=[VM] * 7,
        scratch_shapes=[pltpu.VMEM((pixels, comps), bf16), pltpu.VMEM((comps, frames), bf16),
                        one_row, one_row, one_row, pltpu.SemaphoreType.DMA((2 * bands + 4,))],
        compiler_params=params(),
    )(tile, comp_count, movie, fp, tr, centre_row, centre_col, radius)
    halo = swap(pay)
    banded_cost = pl.CostEstimate(flops=4_000_000_000, bytes_accessed=20_000_000, transcendentals=0)
    band_w, side_w, x = pl.pallas_call(
        build_kernel,
        out_shape=(sds((bands, band, reach), bf16), sds((bands, CYCLE * BAND, beside.shape[2]), bf16),
                   sds((pixels, frames), f32)),
        in_specs=[SM] + [VM] * 4, out_specs=[VM] * 3,
        scratch_shapes=[pltpu.VMEM((pixels, LANES), f32), pltpu.VMEM((bands * SIDE, reach), f32)],
        compiler_params=params(), cost_estimate=banded_cost,
    )(tile, weights, jnp.asarray(own), jnp.asarray(beside), r)
    trace, d, r, pay = pl.pallas_call(
        pass_kernel,
        out_shape=(sds((comps, frames), bf16), sds((pixels, frames), f32), sds((pixels, frames), bf16),
                   sds((edge, frames), bf16)),
        in_specs=[SM, SM] + [VM] * 8, out_specs=[VM] * 4,
        scratch_shapes=[halo_pad, err_buf], compiler_params=params(),
    )(tile, comp_count, halo, side_w, x, d, foot, trace, den, movie)
    halo = swap(pay)
    x = pl.pallas_call(
        banded_kernel,
        out_shape=sds((pixels, frames), f32),
        in_specs=[VM, VM], out_specs=VM, compiler_params=params(), cost_estimate=banded_cost,
    )(band_w, r)
    trace, part, fold = pl.pallas_call(
        functools.partial(last_kernel, block, share),
        out_shape=(sds((comps, frames), bf16), sds((packed, comps), bf16), sds((packed // 2, slots.shape[1]), bf16)),
        in_specs=[SM, SM] + [VM] * 12, out_specs=[HB, VM, VM],
        scratch_shapes=[halo_pad, err_buf, pltpu.VMEM((pixels, frames), bf16), pltpu.VMEM((2, pixels // 2, comps), bf16),
                        pltpu.VMEM((comps, frames), bf16), pltpu.SemaphoreType.DMA],
        compiler_params=params(14),
    )(tile, comp_count, halo, side_w, x, d, foot, trace, den, movie, centre_row, centre_col, radius, jnp.asarray(slots))
    received = lax.all_to_all(part.reshape(parts, block, comps), "tm", 0, 0, tiled=False)
    ffold = pl.pallas_call(
        foot_fold_kernel,
        out_shape=sds((packed, comps), f32),
        in_specs=[VM, VM], out_specs=VM, compiler_params=params(),
    )(fold, foot)
    moved = pl.pallas_call(
        functools.partial(share_kernel, share),
        out_shape=sds((parts, block, comps), bf16),
        in_specs=[SM, VM, VM], out_specs=VM, compiler_params=params(),
    )(me, received, ffold)
    every = lax.all_to_all(moved, "tm", 0, 0, tiled=False).reshape(packed, comps)
    new_foot = pl.pallas_call(
        unfold_kernel,
        out_shape=sds((pixels, comps), bf16),
        in_specs=[SM] + [VM] * 5, out_specs=HB,
        scratch_shapes=[pltpu.VMEM((pixels, comps), bf16), pltpu.SemaphoreType.DMA((bands,))],
        compiler_params=params(),
    )(comp_count, every, fold, centre_row, centre_col, radius)
    return (new_foot[None], trace[None])


def solution(mesh):
    in_specs = (
        P(("groups", "tile"), None, "tm"),
        P(("groups", "tile"), None, None),
        P(("groups", "tile"), None, None),
        P(("groups", "tile"), None, "tm"),
        P(("groups", "tile"), None),
        P(("groups", "tile"), None),
        P(("groups", "tile"), None),
        P(("groups", "tile")),
    )
    out_specs = (P(("groups", "tile"), None, None), P(("groups", "tile"), None, "tm"))
    return jax.shard_map(shards, mesh=mesh, in_specs=in_specs, out_specs=out_specs, check_vma=False)
```

time: 78.2 us -> 60.9 us (0.78)
  local copies, waits for them, and re-layouts: 21.4 us -> 6.2 us
  Pallas kernels: 26.3 us -> 24.8 us
    unnamed x41 -> x26, local copies, waits for them, and re-layouts: 21.4 us -> 6.2 us
    pallas_call x1 -> x2, Pallas kernels: 9.62 us -> 6.17 us  [the longest x1 5.6 us: shards(): pl.pallas_call(build_kernel, out_shape=(sds((bands, band, reach), bf16),...]
    pallas_call x1, Pallas kernels: 2.49 us -> 4.89 us  [shards(): pl.pallas_call(start_kernel, out_shape=(sds((pixels, comps), bf16), sds((...]
    pallas_call x1, Pallas kernels: 2.59 us -> 1.58 us  [shards(): pl.pallas_call(unfold_kernel, out_shape=sds((pixels, comps), bf16), in_sp...]
  transfers between devices with their start and end apart: 3 -> 3, of which waited for: 1 -> 1; matrix products, arithmetic and copies ran while one was open for 2% -> 0% of each run, Pallas kernels for 16% -> 15%
where the time goes in v2:
time: 60.9 us; the launch traced here: 60.4 us
  Pallas kernels  24.8 us (41%)
  blocking collectives  11.6 us (19%)
  waiting for transfers between devices  8.32 us (14%)
  starting transfers between devices  7.94 us (13%)
  local copies, waits for them, and re-layouts  6.2 us (10%)
  between operations  1.57 us (3%)
    all_to_all x1, blocking collectives, shards(): lax.all_to_all(moved, 'tm', 0, 0, tiled=False).reshape(packed, comps)  11.6 us
    all_to_all x1, waiting for transfers between devices, shards(): lax.all_to_all(part.reshape(parts, block, comps), 'tm', 0, 0, tiled=False)  8.32 us
    all_to_all x1, starting transfers between devices, shards(): lax.all_to_all(part.reshape(parts, block, comps), 'tm', 0, 0, tiled=False)  7.29 us
    pallas_call x1, Pallas kernels, shards(): pl.pallas_call(functools.partial(last_kernel, block, share), out_shape=(s...  6.35 us
    unnamed x26, local copies, waits for them, and re-layouts  6.2 us
    pallas_call x1, Pallas kernels, shards(): pl.pallas_call(build_kernel, out_shape=(sds((bands, band, reach), bf16),...  5.6 us
    pallas_call x1, Pallas kernels, shards(): pl.pallas_call(start_kernel, out_shape=(sds((pixels, comps), bf16), sds((...  4.89 us
    pallas_call x1, Pallas kernels, shards(): pl.pallas_call(pass_kernel, out_shape=(sds((comps, frames), bf16), sds((p...  2.91 us
  transfers between devices with their start and end apart: 3, of which 1 were waited for; matrix products, arithmetic and copies ran while one was open for 0% of the time, Pallas kernels for 15%

profile of v2, /device:TPU:0, one launch (start us, length us, event | category | flops | bytes accessed | tf_op | source)
XLA Modules:
  0.0 60.4 jit_solution(13092598516337522780)
XLA Ops:
  1.3 0.0 copy-start
  1.3 1.7 %copy-done = bf16[1,2304,512]{2,1,0:T(8,128)(2,1)S(1)} copy-done((bf16[1,2304,512]{2,1,0:T(8,128)(2,1)S(1)}, bf16[1,2304,512]{2,1,0:T(8,128)(2,1)}, u32[]{:S(2)}) %copy-start) | copy-done | bytes 2359320
  2.9 0.0 copy-start.1
  3.0 1.5 %copy-done.1 = bf16[1,2304,384]{2,1,0:T(8,128)(2,1)S(1)} copy-done((bf16[1,2304,384]{2,1,0:T(8,128)(2,1)S(1)}, bf16[1,2304,384]{2,1,0:T(8,128)(2,1)}, u32[]{:S(2)}) %copy-start.1) | copy-done | bytes 1769496
  4.4 1.0 %copy-done.2 = bf16[1,384,512]{2,1,0:T(8,128)(2,1)S(1)} copy-done((bf16[1,384,512]{2,1,0:T(8,128)(2,1)S(1)}, bf16[1,384,512]{2,1,0:T(8,128)(2,1)}, u32[]{:S(2)}) %copy-start.2) | copy-done | bytes 393240
  5.4 0.7 %copy-done.3 = s32[1,384]{1,0:T(1,128)S(1)} copy-done((s32[1,384]{1,0:T(1,128)S(1)}, s32[1,384]{1,0:T(1,128)}, u32[]{:S(2)}) %copy-start.3) | copy-done | bytes 1560
  6.1 0.7 %copy-done.5 = s32[1,384]{1,0:T(1,128)S(1)} copy-done((s32[1,384]{1,0:T(1,128)S(1)}, s32[1,384]{1,0:T(1,128)}, u32[]{:S(2)}) %copy-start.5) | copy-done | bytes 1560
  6.8 0.7 %copy-done.7 = s32[1,384]{1,0:T(1,128)S(1)} copy-done((s32[1,384]{1,0:T(1,128)S(1)}, s32[1,384]{1,0:T(1,128)}, u32[]{:S(2)}) %copy-start.7) | copy-done | bytes 1560
  7.5 4.9 %shard_map.122 = (bf16[2304,384]{1,0:T(8,128)(2,1)S(1)}, bf16[384,512]{1,0:T(8,128)(2,1)S(1)}, f32[384,128]{1,0:T(8,128)S(1)}, f32[2304,512]{1,0:T(8,128)S(1)}, ...) custom-call(s32[1]{0:T(128)} %bitcast.1.tile_ref, ...), custom_call_target="tpu_custom_call" | custom-call | tf_op jit(solution)/shard_map/pallas_call | solution.py:351
  12.4 0.6 collective-permute-start
  12.9 0.0 copy-done.10
  12.9 0.0 copy-done.11
  12.9 0.0 copy-done.12
  12.9 5.6 %shard_map.123 = (bf16[6,384,1152]{2,1,0:T(8,128)(2,1)S(1)}, bf16[6,64,256]{2,1,0:T(8,128)(2,1)S(1)}, f32[2304,512]{1,0:T(8,128)S(1)}) custom-call(s32[1]{0:T(128)} %bitcast.1.tile_ref, bf16[56,2304]{1,0:T(8,128)(2,1)S(1)} %bitcast.16, s32[64,1]{1,0:T(8,128)S(1)} %copy-done.12, s32[2,64,256]{2,1,0:T(8,128)S(1)} %copy-done.11, ...), custom_call_target="tpu_custom_call" | custom-call | flops 4000000000 | bytes 20000000 | tf_op jit(solution)/shard_map/pallas_call | solution.py:363
  18.5 0.0 collective-permute-done.halo_ref
  18.6 2.9 %shard_map.124 = (bf16[384,512]{1,0:T(8,128)(2,1)S(1)}, f32[2304,512]{1,0:T(8,128)S(1)}, bf16[2304,512]{1,0:T(8,128)(2,1)S(1)}, bf16[384,512]{1,0:T(8,128)(2,1)S(1)}) custom-call(s32[1]{0:T(128)} %bitcast.1.tile_ref, s32[1]{0:T(128)S(6)} %copy.13.count_ref, bf16[384,512]{1,0:T(8,128)(2,1)S(1)} %collective-permute-done.halo_ref, ...), custom_call_target="tpu_custom_call" | custom-call | tf_op jit(solution)/shard_map/pallas_call | solution.py:371
  21.5 0.1 collective-permute-start.1
  21.6 0.0 copy-start.9
  21.6 2.8 %shard_map.125.x_ref = f32[2304,512]{1,0:T(8,128)S(1)} custom-call(bf16[6,384,1152]{2,1,0:T(8,128)(2,1)S(1)} %get-tuple-element.29.bands_ref, bf16[2304,512]{1,0:T(8,128)(2,1)S(1)} %get-tuple-element.30.r_ref), custom_call_target="tpu_custom_call" | custom-call | flops 4000000000 | bytes 20000000 | tf_op jit(solution)/shard_map/pallas_call | solution.py:379
  24.4 0.0 collective-permute-done.1.halo_ref
  24.4 0.0 copy-done.4
  24.4 0.0 copy-done.6
  24.4 0.0 copy-done.9
  24.4 6.3 %shard_map.126 = (bf16[384,512]{1,0:T(8,128)(2,1)}, bf16[320,384]{1,0:T(8,128)(2,1)}, bf16[160,1152]{1,0:T(8,128)(2,1)S(1)}) custom-call(s32[1]{0:T(128)} %bitcast.1.tile_ref, s32[1]{0:T(128)S(6)} %copy.13.count_ref, bf16[384,512]{1,0:T(8,128)(2,1)S(1)} %collective-permute-done.1.halo_ref, bf16[6,64,256]{2,1,0:T(8,128)(2,1)S(1)} %get-tuple-element.21.sides_ref, ...), custom_call_target="tpu_custom_call" | custom-call | tf_op jit(solution)/shard_map/pallas_call | solution.py:384
  30.8 0.0 copy-start.8
  30.8 7.3 %all-to-all-start = ((bf16[8,40,384]{2,1,0:T(8,128)(2,1)}), bf16[8,40,384]{2,1,0:T(8,128)(2,1)S(1)}, u32[]{:S(2)}, u32[]{:S(2)}) async-start(bf16[8,40,384]{2,1,0:T(8,128)(2,1)} %bitcast.7), calls=%async_computation | async-start | bytes 491520 | tf_op jit(solution)/shard_map/all_to_all | solution.py:392
  38.1 0.6 shard_map.127.ffold_ref
  38.7 8.3 %all-to-all-done.parts_ref = bf16[8,40,384]{2,1,0:T(8,128)(2,1)S(1)} async-done(((bf16[8,40,384]{2,1,0:T(8,128)(2,1)}), bf16[8,40,384]{2,1,0:T(8,128)(2,1)S(1)}, u32[]{:S(2)}, u32[]{:S(2)}) %all-to-all-start) | async-done | bytes 245792 | tf_op jit(solution)/shard_map/all_to_all | solution.py:392
  47.0 0.1 shard_map.128
  47.0 11.6 %all_to_all.10 = bf16[8,40,384]{2,1,0:T(8,128)(2,1)S(1)} all-to-all(bf16[8,40,384]{2,1,0:T(8,128)(2,1)S(1)} %shard_map.128), channel_id=1, replica_groups=mesh['groups'=2,'tm'=8,'tile'=2] {'tm'}, dimensions={0} | all-to-all | bytes 491520 | tf_op jit(solution)/shard_map/all_to_all | solution.py:403
  58.7 0.0 copy-done.8
  58.7 1.6 %shard_map.129 = bf16[2304,384]{1,0:T(8,128)(2,1)} custom-call(s32[1]{0:T(128)S(6)} %copy.13.count_ref, bf16[320,384]{1,0:T(8,128)(2,1)S(1)} %bitcast.14, bf16[160,1152]{1,0:T(8,128)(2,1)S(1)} %get-tuple-element.34.fold_ref, s32[1,384]{1,0:T(1,128)S(1)} %copy-done.4, s32[1,384]{1,0:T(1,128)S(1)} %copy-done.6, s32[1,384]{1,0:T(1,128)S(1)} %copy-done.8), custom_call_target="tpu_custom_call" | custom-call | tf_op jit(solution)/shard_map/pallas_call | solution.py:404
  (9 shorter events, 0.0 us)
Async XLA Ops:
  1.3 1.7 %copy-start = (bf16[1,2304,512]{2,1,0:T(8,128)(2,1)S(1)}, bf16[1,2304,512]{2,1,0:T(8,128)(2,1)}, u32[]{:S(2)}) copy-start(bf16[1,2304,512]{2,1,0:T(8,128)(2,1)} %param.11) | copy-start | bytes 7077892
  2.9 1.5 %copy-start.1 = (bf16[1,2304,384]{2,1,0:T(8,128)(2,1)S(1)}, bf16[1,2304,384]{2,1,0:T(8,128)(2,1)}, u32[]{:S(2)}) copy-start(bf16[1,2304,384]{2,1,0:T(8,128)(2,1)} %param.13) | copy-start | bytes 5308420
  4.4 1.0 %copy-start.2 = (bf16[1,384,512]{2,1,0:T(8,128)(2,1)S(1)}, bf16[1,384,512]{2,1,0:T(8,128)(2,1)}, u32[]{:S(2)}) copy-start(bf16[1,384,512]{2,1,0:T(8,128)(2,1)} %param.14) | copy-start | bytes 1179652
  5.4 0.7 %copy-start.3 = (s32[1,384]{1,0:T(1,128)S(1)}, s32[1,384]{1,0:T(1,128)}, u32[]{:S(2)}) copy-start(s32[1,384]{1,0:T(1,128)} %cr_ref.3) | copy-start | bytes 4612
  6.1 0.7 %copy-start.5 = (s32[1,384]{1,0:T(1,128)S(1)}, s32[1,384]{1,0:T(1,128)}, u32[]{:S(2)}) copy-start(s32[1,384]{1,0:T(1,128)} %cc_ref.3) | copy-start | bytes 4612
  6.8 0.7 %copy-start.7 = (s32[1,384]{1,0:T(1,128)S(1)}, s32[1,384]{1,0:T(1,128)}, u32[]{:S(2)}) copy-start(s32[1,384]{1,0:T(1,128)} %rad_ref.3) | copy-start | bytes 4612
  7.5 5.5 %copy-start.10 = (bf16[1,2304,56]{1,2,0:T(8,128)(2,1)S(1)}, bf16[1,2304,56]{1,2,0:T(8,128)(2,1)}, u32[]{:S(2)}) copy-start(bf16[1,2304,56]{1,2,0:T(8,128)(2,1)} %param.12) | copy-start | bytes 774148
  7.5 5.5 %copy-start.11 = (s32[2,64,256]{2,1,0:T(8,128)S(1)}, s32[2,64,256]{2,1,0:T(8,128)}, u32[]{:S(2)}) copy-start(s32[2,64,256]{2,1,0:T(8,128)} %constant.15.clone.beside_ref) | copy-start | bytes 393220
  7.5 5.5 %copy-start.12 = (s32[64,1]{1,0:T(8,128)S(1)}, s32[64,1]{1,0:T(8,128)}, u32[]{:S(2)}) copy-start(s32[64,1]{1,0:T(8,128)} %constant.14.clone.own_ref) | copy-start | bytes 772
  12.4 6.2 %collective-permute-start = (bf16[384,512]{1,0:T(8,128)(2,1)S(1)}, bf16[384,512]{1,0:T(8,128)(2,1)S(1)}, u32[]{:S(2)}, u32[]{:S(2)}) collective-permute-start(bf16[384,512]{1,0:T(8,128)(2,1)S(1)} %get-tuple-element.19), channel_id=1, source_target_pairs={{0,1},{1,0},{2,3},{3,2},{4,5},{5,4},{6,7},{7,6},{8,9},{9,8},{10,11... | collective-permute-start | bytes 1179656 | tf_op jit(solution)/shard_map/ppermute | solution.py:327
  21.5 2.9 %collective-permute-start.1 = (bf16[384,512]{1,0:T(8,128)(2,1)S(1)}, bf16[384,512]{1,0:T(8,128)(2,1)S(1)}, u32[]{:S(2)}, u32[]{:S(2)}) collective-permute-start(bf16[384,512]{1,0:T(8,128)(2,1)S(1)} %get-tuple-element.28), channel_id=1, source_target_pairs={{0,1},{1,0},{2,3},{3,2},{4,5},{5,4},{6,7},{7,6},{8,9},{9,8},{10,11... | collective-permute-start | bytes 1179656 | tf_op jit(solution)/shard_map/ppermute | solution.py:327
  21.6 2.9 %copy-start.4 = (s32[1,384]{1,0:T(1,128)S(1)}, s32[1,384]{1,0:T(1,128)}, u32[]{:S(2)}) copy-start(s32[1,384]{1,0:T(1,128)} %cr_ref.3) | copy-start | bytes 4612
  21.6 2.9 %copy-start.6 = (s32[1,384]{1,0:T(1,128)S(1)}, s32[1,384]{1,0:T(1,128)}, u32[]{:S(2)}) copy-start(s32[1,384]{1,0:T(1,128)} %cc_ref.3) | copy-start | bytes 4612
  21.6 2.9 %copy-start.9 = (s32[1,1152]{1,0:T(1,128)S(1)}, s32[1,1152]{1,0:T(1,128)}, u32[]{:S(2)}) copy-start(s32[1,1152]{1,0:T(1,128)} %constant.16.clone.slot_ref) | copy-start | bytes 13828
  30.8 27.9 %copy-start.8 = (s32[1,384]{1,0:T(1,128)S(1)}, s32[1,384]{1,0:T(1,128)}, u32[]{:S(2)}) copy-start(s32[1,384]{1,0:T(1,128)} %rad_ref.3) | copy-start | bytes 4612
  30.8 16.2 %all-to-all-start = ((bf16[8,40,384]{2,1,0:T(8,128)(2,1)}), bf16[8,40,384]{2,1,0:T(8,128)(2,1)S(1)}, u32[]{:S(2)}, u32[]{:S(2)}) async-start(bf16[8,40,384]{2,1,0:T(8,128)(2,1)} %bitcast.7), calls=%async_computation | async-start | bytes 491520 | tf_op jit(solution)/shard_map/all_to_all | solution.py:392

commit v3 on v2

--- a/solution.py
+++ b/solution.py
@@ -357,7 +357,7 @@
         scratch_shapes=[pltpu.VMEM((pixels, comps), bf16), pltpu.VMEM((comps, frames), bf16),
                         one_row, one_row, one_row, pltpu.SemaphoreType.DMA((2 * bands + 4,))],
         compiler_params=params(),
-    )(tile, comp_count, movie, fp, tr, centre_row, centre_col, radius)
+    )(tile, comp_count, *[pltpu.with_memory_space_constraint(v, pltpu.HBM) for v in (movie, fp, tr, centre_row, centre_col, radius)])
     halo = swap(pay)
     banded_cost = pl.CostEstimate(flops=4_000_000_000, bytes_accessed=20_000_000, transcendentals=0)
     band_w, side_w, x = pl.pallas_call(

time: 60.9 us -> 54 us (0.89)
  local copies, waits for them, and re-layouts: 6.2 us -> 0.04 us
  Pallas kernels: 24.8 us -> 24.1 us
    unnamed x26 -> x14, local copies, waits for them, and re-layouts: 6.2 us -> 0.04 us
    pallas_call x1, Pallas kernels: 4.89 us -> 4.27 us  [shards(): pl.pallas_call(start_kernel, out_shape=(sds((pixels, comps), bf16), sds((...]
  transfers between devices with their start and end apart: 3 -> 3, of which waited for: 1 -> 1; matrix products, arithmetic and copies ran while one was open for 0% -> 0% of each run, Pallas kernels for 15% -> 17%
where the time goes in v3:
time: 54 us; the launch traced here: 53.7 us
  Pallas kernels  24.1 us (45%)
  blocking collectives  11.6 us (21%)
  waiting for transfers between devices  8.33 us (15%)
  starting transfers between devices  7.93 us (15%)
  between operations  1.62 us (3%)
    all_to_all x1, blocking collectives, shards(): lax.all_to_all(moved, 'tm', 0, 0, tiled=False).reshape(packed, comps)  11.6 us
    all_to_all x1, waiting for transfers between devices, shards(): lax.all_to_all(part.reshape(parts, block, comps), 'tm', 0, 0, tiled=False)  8.33 us
    all_to_all x1, starting transfers between devices, shards(): lax.all_to_all(part.reshape(parts, block, comps), 'tm', 0, 0, tiled=False)  7.27 us
    pallas_call x1, Pallas kernels, shards(): pl.pallas_call(functools.partial(last_kernel, block, share), out_shape=(s...  6.35 us
    pallas_call x1, Pallas kernels, shards(): pl.pallas_call(build_kernel, out_shape=(sds((bands, band, reach), bf16),...  5.6 us
    pallas_call x1, Pallas kernels, shards(): pl.pallas_call(start_kernel, out_shape=(sds((pixels, comps), bf16), sds((...  4.27 us
    pallas_call x1, Pallas kernels, shards(): pl.pallas_call(pass_kernel, out_shape=(sds((comps, frames), bf16), sds((p...  2.92 us
    pallas_call x1, Pallas kernels, shards(): pl.pallas_call(banded_kernel, out_shape=sds((pixels, frames), f32), in_sp...  2.81 us
  transfers between devices with their start and end apart: 3, of which 1 were waited for; matrix products, arithmetic and copies ran while one was open for 0% of the time, Pallas kernels for 17%

profile of v3, /device:TPU:0, one launch (start us, length us, event | category | flops | bytes accessed | tf_op | source)
XLA Modules:
  0.0 53.7 jit_solution(3758438673988307593)
XLA Ops:
  0.6 0.0 copy-start.5
  0.6 0.0 copy-start.6
  0.7 0.0 copy-start.4
  1.4 4.3 %shard_map.122 = (bf16[2304,384]{1,0:T(8,128)(2,1)S(1)}, bf16[384,512]{1,0:T(8,128)(2,1)S(1)}, f32[384,128]{1,0:T(8,128)S(1)}, f32[2304,512]{1,0:T(8,128)S(1)}, ...) custom-call(s32[1]{0:T(128)} %bitcast.1.tile_ref, ...), custom_call_target="tpu_custom_call" | custom-call | tf_op jit(solution)/shard_map/pallas_call | solution.py:351
  5.6 0.6 %collective-permute-start = (bf16[384,512]{1,0:T(8,128)(2,1)S(1)}, bf16[384,512]{1,0:T(8,128)(2,1)S(1)}, u32[]{:S(2)}, u32[]{:S(2)}) collective-permute-start(bf16[384,512]{1,0:T(8,128)(2,1)S(1)} %get-tuple-element.19), channel_id=1, source_target_pairs={{0,1},{1,0},{2,3},{3,2},{4,5},{5,4},{6,7},{7,6},{8,9},{9,8},{10,11... | collective-permute-start | bytes 1179656 | tf_op jit(solution)/shard_map/ppermute | solution.py:327
  6.2 0.0 copy-done.5
  6.2 0.0 copy-done.6
  6.2 0.0 copy-done.4
  6.2 5.6 %shard_map.123 = (bf16[6,384,1152]{2,1,0:T(8,128)(2,1)S(1)}, bf16[6,64,256]{2,1,0:T(8,128)(2,1)S(1)}, f32[2304,512]{1,0:T(8,128)S(1)}) custom-call(s32[1]{0:T(128)} %bitcast.1.tile_ref, bf16[56,2304]{1,0:T(8,128)(2,1)S(1)} %bitcast.13, s32[64,1]{1,0:T(8,128)S(1)} %copy-done.6, s32[2,64,256]{2,1,0:T(8,128)S(1)} %copy-done.5, ...), custom_call_target="tpu_custom_call" | custom-call | flops 4000000000 | bytes 20000000 | tf_op jit(solution)/shard_map/pallas_call | solution.py:363
  11.8 0.0 collective-permute-done.halo_ref
  11.8 2.9 %shard_map.124 = (bf16[384,512]{1,0:T(8,128)(2,1)S(1)}, f32[2304,512]{1,0:T(8,128)S(1)}, bf16[2304,512]{1,0:T(8,128)(2,1)S(1)}, bf16[384,512]{1,0:T(8,128)(2,1)S(1)}) custom-call(s32[1]{0:T(128)} %bitcast.1.tile_ref, s32[1]{0:T(128)S(6)} %copy.13.count_ref, bf16[384,512]{1,0:T(8,128)(2,1)S(1)} %collective-permute-done.halo_ref, ...), custom_call_target="tpu_custom_call" | custom-call | tf_op jit(solution)/shard_map/pallas_call | solution.py:371
  14.7 0.1 collective-permute-start.1
  14.9 0.0 copy-start
  14.9 0.0 copy-start.1
  14.9 0.0 copy-start.2
  14.9 0.0 copy-start.3
  14.9 2.8 %shard_map.125.x_ref = f32[2304,512]{1,0:T(8,128)S(1)} custom-call(bf16[6,384,1152]{2,1,0:T(8,128)(2,1)S(1)} %get-tuple-element.29.bands_ref, bf16[2304,512]{1,0:T(8,128)(2,1)S(1)} %get-tuple-element.30.r_ref), custom_call_target="tpu_custom_call" | custom-call | flops 4000000000 | bytes 20000000 | tf_op jit(solution)/shard_map/pallas_call | solution.py:379
  17.7 0.0 collective-permute-done.1.halo_ref
  17.7 0.0 copy-done
  17.7 0.0 copy-done.1
  17.7 0.0 copy-done.2
  17.7 0.0 copy-done.3
  17.7 6.4 %shard_map.126 = (bf16[384,512]{1,0:T(8,128)(2,1)}, bf16[320,384]{1,0:T(8,128)(2,1)}, bf16[160,1152]{1,0:T(8,128)(2,1)S(1)}) custom-call(s32[1]{0:T(128)} %bitcast.1.tile_ref, s32[1]{0:T(128)S(6)} %copy.13.count_ref, bf16[384,512]{1,0:T(8,128)(2,1)S(1)} %collective-permute-done.1.halo_ref, bf16[6,64,256]{2,1,0:T(8,128)(2,1)S(1)} %get-tuple-element.21.sides_ref, ...), custom_call_target="tpu_custom_call" | custom-call | tf_op jit(solution)/shard_map/pallas_call | solution.py:384
  24.1 7.3 %all-to-all-start = ((bf16[8,40,384]{2,1,0:T(8,128)(2,1)}), bf16[8,40,384]{2,1,0:T(8,128)(2,1)S(1)}, u32[]{:S(2)}, u32[]{:S(2)}) async-start(bf16[8,40,384]{2,1,0:T(8,128)(2,1)} %bitcast.7), calls=%async_computation | async-start | bytes 491520 | tf_op jit(solution)/shard_map/all_to_all | solution.py:392
  31.4 0.6 %shard_map.127.ffold_ref = f32[320,384]{1,0:T(8,128)S(1)} custom-call(bf16[160,1152]{1,0:T(8,128)(2,1)S(1)} %get-tuple-element.34.fold_ref, bf16[2304,384]{1,0:T(8,128)(2,1)S(1)} %get-tuple-element.24.foot_ref), custom_call_target="tpu_custom_call" | custom-call | tf_op jit(solution)/shard_map/pallas_call | solution.py:393
  31.9 8.3 %all-to-all-done.parts_ref = bf16[8,40,384]{2,1,0:T(8,128)(2,1)S(1)} async-done(((bf16[8,40,384]{2,1,0:T(8,128)(2,1)}), bf16[8,40,384]{2,1,0:T(8,128)(2,1)S(1)}, u32[]{:S(2)}, u32[]{:S(2)}) %all-to-all-start) | async-done | bytes 245792 | tf_op jit(solution)/shard_map/all_to_all | solution.py:392
  40.3 0.1 shard_map.128
  40.3 11.6 %all_to_all.10 = bf16[8,40,384]{2,1,0:T(8,128)(2,1)S(1)} all-to-all(bf16[8,40,384]{2,1,0:T(8,128)(2,1)S(1)} %shard_map.128), channel_id=1, replica_groups=mesh['groups'=2,'tm'=8,'tile'=2] {'tm'}, dimensions={0} | all-to-all | bytes 491520 | tf_op jit(solution)/shard_map/all_to_all | solution.py:403
  52.0 1.6 %shard_map.129 = bf16[2304,384]{1,0:T(8,128)(2,1)} custom-call(s32[1]{0:T(128)S(6)} %copy.13.count_ref, bf16[320,384]{1,0:T(8,128)(2,1)S(1)} %bitcast.12, bf16[160,1152]{1,0:T(8,128)(2,1)S(1)} %get-tuple-element.34.fold_ref, s32[1,384]{1,0:T(1,128)S(1)} %copy-done, s32[1,384]{1,0:T(1,128)S(1)} %copy-done.1, s32[1,384]{1,0:T(1,128)S(1)} %copy-done.2), custom_call_target="tpu_custom_call" | custom-call | tf_op jit(solution)/shard_map/pallas_call | solution.py:404
Async XLA Ops:
  0.6 5.6 %copy-start.5 = (s32[2,64,256]{2,1,0:T(8,128)S(1)}, s32[2,64,256]{2,1,0:T(8,128)}, u32[]{:S(2)}) copy-start(s32[2,64,256]{2,1,0:T(8,128)} %constant.15.clone.beside_ref) | copy-start | bytes 393220
  0.6 5.6 %copy-start.6 = (s32[64,1]{1,0:T(8,128)S(1)}, s32[64,1]{1,0:T(8,128)}, u32[]{:S(2)}) copy-start(s32[64,1]{1,0:T(8,128)} %constant.14.clone.own_ref) | copy-start | bytes 772
  0.7 5.6 %copy-start.4 = (bf16[1,2304,56]{1,2,0:T(8,128)(2,1)S(1)}, bf16[1,2304,56]{1,2,0:T(8,128)(2,1)}, u32[]{:S(2)}) copy-start(bf16[1,2304,56]{1,2,0:T(8,128)(2,1)} %param.12) | copy-start | bytes 774148
  5.6 6.2 %collective-permute-start = (bf16[384,512]{1,0:T(8,128)(2,1)S(1)}, bf16[384,512]{1,0:T(8,128)(2,1)S(1)}, u32[]{:S(2)}, u32[]{:S(2)}) collective-permute-start(bf16[384,512]{1,0:T(8,128)(2,1)S(1)} %get-tuple-element.19), channel_id=1, source_target_pairs={{0,1},{1,0},{2,3},{3,2},{4,5},{5,4},{6,7},{7,6},{8,9},{9,8},{10,11... | collective-permute-start | bytes 1179656 | tf_op jit(solution)/shard_map/ppermute | solution.py:327
  14.7 3.0 %collective-permute-start.1 = (bf16[384,512]{1,0:T(8,128)(2,1)S(1)}, bf16[384,512]{1,0:T(8,128)(2,1)S(1)}, u32[]{:S(2)}, u32[]{:S(2)}) collective-permute-start(bf16[384,512]{1,0:T(8,128)(2,1)S(1)} %get-tuple-element.28), channel_id=1, source_target_pairs={{0,1},{1,0},{2,3},{3,2},{4,5},{5,4},{6,7},{7,6},{8,9},{9,8},{10,11... | collective-permute-start | bytes 1179656 | tf_op jit(solution)/shard_map/ppermute | solution.py:327
  14.9 2.9 %copy-start = (s32[1,384]{1,0:T(1,128)S(1)}, s32[1,384]{1,0:T(1,128)}, u32[]{:S(2)}) copy-start(s32[1,384]{1,0:T(1,128)} %cr_ref.3) | copy-start | bytes 4612
  14.9 2.9 %copy-start.1 = (s32[1,384]{1,0:T(1,128)S(1)}, s32[1,384]{1,0:T(1,128)}, u32[]{:S(2)}) copy-start(s32[1,384]{1,0:T(1,128)} %cc_ref.3) | copy-start | bytes 4612
  14.9 2.9 %copy-start.2 = (s32[1,384]{1,0:T(1,128)S(1)}, s32[1,384]{1,0:T(1,128)}, u32[]{:S(2)}) copy-start(s32[1,384]{1,0:T(1,128)} %rad_ref.3) | copy-start | bytes 4612
  14.9 2.9 %copy-start.3 = (s32[1,1152]{1,0:T(1,128)S(1)}, s32[1,1152]{1,0:T(1,128)}, u32[]{:S(2)}) copy-start(s32[1,1152]{1,0:T(1,128)} %constant.16.clone.slot_ref) | copy-start | bytes 13828
  24.1 16.2 %all-to-all-start = ((bf16[8,40,384]{2,1,0:T(8,128)(2,1)}), bf16[8,40,384]{2,1,0:T(8,128)(2,1)S(1)}, u32[]{:S(2)}, u32[]{:S(2)}) async-start(bf16[8,40,384]{2,1,0:T(8,128)(2,1)} %bitcast.7), calls=%async_computation | async-start | bytes 491520 | tf_op jit(solution)/shard_map/all_to_all | solution.py:392

commit v4 on v3

--- a/solution.py
+++ b/solution.py
@@ -16,6 +16,10 @@
 BAND = 8
 LANES = 128
 OFFS_PAD = 64
+HALF = SIDE // 2
+REACH = HALF + CYCLE
+COL_STEP = SIDE - REACH
+RANGE = (BAND + 2 * CYCLE) * REACH
 
 FOLD_R = 16
 FOLD_C = 19
@@ -39,11 +43,10 @@
 def band_tables():
     offsets = cycle_offsets()
     none = len(offsets)
-    reach = (BAND + 2 * CYCLE) * SIDE
-    own = np.full((OFFS_PAD, 1), -1, np.int32)
+    own = np.full((OFFS_PAD, LANES), -1, np.int32)
     beside = np.full((2, BAND, CYCLE, 32, CYCLE), none, np.int32)
     for o, (dy, dx) in enumerate(offsets):
-        own[o, 0] = ((CYCLE + dy) * SIDE + dx) % reach
+        own[o] = ((CYCLE + dy) * REACH + dx) % RANGE
         for i in range(BAND):
             for q in range(CYCLE):
                 h = q + dx - CYCLE
@@ -91,36 +94,80 @@
 
 def resid_band(g, tile, movie_ref, foot, trace, d_ref, r_ref, pay_ref):
     band = BAND * SIDE
-    rows = pl.ds(g * band, band)
-    d = movie_ref[rows, :].astype(f32) - dot(foot, trace)
-    d_ref[rows, :] = d
-    r_ref[rows, :] = d.astype(bf16)
+    d = movie_ref[pl.ds(g * band, band), :].astype(f32) - dot(foot, trace)
     d3 = d.reshape(BAND, SIDE, d.shape[1])
+    d_ref[pl.ds(g * BAND, BAND)] = d3
+    r_ref[pl.ds(g * BAND, BAND)] = d3.astype(bf16)
     edge = jnp.where(tile == 0, d3[:, SIDE - CYCLE :], d3[:, :CYCLE])
     pay_ref[pl.ds(g * BAND * CYCLE, BAND * CYCLE), :] = edge.reshape(BAND * CYCLE, d.shape[1]).astype(bf16)
 
 
+def build_bands(tile, w, at, beside, bands_ref, sides_ref, weights, wide):
+    bands = SIDE // BAND
+    blocks = RANGE // LANES
+    offs = w.shape[0]
+    eye = lax.broadcasted_iota(i32, (offs, LANES), 0) == lax.broadcasted_iota(i32, (offs, LANES), 1)
+    weights[...] = lax.dot_general(w, jnp.where(eye, 1.0, 0.0).astype(bf16), (((0,), (0,)), ((), ())),
+                                   preferred_element_type=f32)
+    column = lax.broadcasted_iota(i32, (HALF, LANES), 0)
+    lane = lax.broadcasted_iota(i32, (HALF, LANES), 1)
+    shifts = [(HALF - COL_STEP) * h for h in range(2)]
+    carried = [lane < column + shift for shift in shifts]
+    inside = [jnp.abs(lax.rem(lane, REACH) - column - shift) <= CYCLE for shift in shifts]
+    target = lax.broadcasted_iota(i32, (OFFS_PAD, RANGE), 1)
+    for i in range(0, BAND, 2):
+        for k in range(2):
+            moved = at + (i + k) * REACH
+            moved = jnp.where(moved >= RANGE, moved - RANGE, moved)
+            pick = jnp.where(target == jnp.where(at < 0, -1, moved), 1.0, 0.0).astype(bf16)
+            rows = [weights[(g * BAND + i + k) * SIDE : (g * BAND + i + k + 1) * SIDE, :OFFS_PAD] for g in range(bands)]
+            wide[k] = dot(jnp.concatenate(rows, axis=0).astype(bf16), pick)
+        for g in range(bands):
+            for h in range(2):
+                start = g * SIDE + h * HALF
+                turned = [[pltpu.roll(wide[k, start : start + HALF, v * LANES : (v + 1) * LANES], shifts[h], 1,
+                                      stride=1, stride_axis=0) for v in range(blocks)] for k in range(2)]
+                for v in range(blocks):
+                    pair = [jnp.where(inside[h], jnp.where(carried[h], turned[k][v - 1], turned[k][v]), 0.0)
+                            for k in range(2)]
+                    bands_ref[g, h, i * HALF : (i + 2) * HALF, v * LANES : (v + 1) * LANES] = jnp.concatenate(
+                        pair, axis=0).astype(bf16)
+    for g in range(bands):
+        edges = []
+        for i in range(BAND):
+            base = (g * BAND + i) * SIDE
+            edges.append(jnp.where(tile == 0, weights[base + SIDE - CYCLE : base + SIDE, :],
+                                   weights[base : base + CYCLE, :]))
+        edge = jnp.concatenate(edges, axis=0)
+        for v in range(2):
+            lanes = slice(v * LANES, (v + 1) * LANES)
+            sides_ref[g, :, lanes] = jnp.take_along_axis(edge, beside[:, lanes], axis=1).astype(bf16)
+
+
 def start_kernel(tile_ref, count_ref, movie_hbm, fp_hbm, tr_hbm, cr_hbm, cc_hbm, rad_hbm,
-                 foot_ref, trace_ref, den_ref, d_ref, r_ref, pay_ref, movie_ref,
-                 fp_ref, tr_ref, cr_ref, cc_ref, rad_ref, sems):
+                 w_hbm, own_hbm, beside_hbm,
+                 foot_ref, trace_ref, den_ref, d_ref, r_ref, pay_ref, movie_ref, bands_ref, sides_ref,
+                 fp_ref, tr_ref, cr_ref, cc_ref, rad_ref, w_ref, own_ref, beside_ref, weights, wide, sems):
     count, tile = count_ref[0], tile_ref[0]
     comps = tr_ref.shape[0]
     band = BAND * SIDE
     bands = SIDE // BAND
     small = [pltpu.make_async_copy(src, dst, sems.at[2 * bands + n]) for n, (src, dst) in enumerate(
-        ((cr_hbm, cr_ref), (cc_hbm, cc_ref), (rad_hbm, rad_ref), (tr_hbm, tr_ref)))]
+        ((w_hbm, w_ref), (own_hbm, own_ref), (beside_hbm.at[tile], beside_ref),
+         (cr_hbm, cr_ref), (cc_hbm, cc_ref), (rad_hbm, rad_ref), (tr_hbm, tr_ref)))]
     fps, movies = [], []
     for g in range(bands):
         rows = pl.ds(g * band, band)
         fps.append(pltpu.make_async_copy(fp_hbm.at[rows, :], fp_ref.at[rows, :], sems.at[g]))
         movies.append(pltpu.make_async_copy(movie_hbm.at[rows, :], movie_ref.at[rows, :], sems.at[bands + g]))
-    for n, copy in enumerate(small):
+    for copy in small:
         copy.start()
     for g in range(bands):
         fps[g].start()
         movies[g].start()
     for copy in small:
         copy.wait()
+    build_bands(tile, w_ref[...], own_ref[:, :1], beside_ref[...], bands_ref, sides_ref, weights, wide)
     live = lax.broadcasted_iota(i32, (comps, 1), 0) < count
     trace = jnp.where(live, tr_ref[...].astype(f32), 0.0).astype(bf16)
     trace_ref[...] = trace
@@ -141,67 +188,21 @@
     den_ref[...] = jnp.transpose(jnp.broadcast_to(energy, (LANES, comps)))
 
 
-def banded(bands_ref, r_ref, x_ref):
-    band = BAND * SIDE
+def banded_kernel(bands_ref, r_ref, x_ref):
+    frames = r_ref.shape[2]
     for g in range(SIDE // BAND):
         low = max(0, CYCLE - g * BAND)
         high = min(BAND + 2 * CYCLE, SIDE + CYCLE - g * BAND)
-        first = (g * BAND + low - CYCLE) * SIDE
-        x_ref[pl.ds(g * band, band), :] = dot(
-            bands_ref[g, :, low * SIDE : high * SIDE], r_ref[pl.ds(first, (high - low) * SIDE), :])
-
-
-def build_kernel(tile_ref, w_ref, own_ref, beside_ref, r_ref, bands_ref, sides_ref, x_ref, weights, wide):
-    tile = tile_ref[0]
-    bands = SIDE // BAND
-    reach = bands_ref.shape[2]
-    blocks = reach // LANES
-    offs = w_ref.shape[0]
-    eye = lax.broadcasted_iota(i32, (offs, LANES), 0) == lax.broadcasted_iota(i32, (offs, LANES), 1)
-    weights[...] = lax.dot_general(w_ref[...], jnp.where(eye, 1.0, 0.0).astype(bf16), (((0,), (0,)), ((), ())),
-                                   preferred_element_type=f32)
-    pixel = lax.broadcasted_iota(i32, (SIDE, LANES), 0)
-    lane = lax.broadcasted_iota(i32, (SIDE, LANES), 1)
-    carried = lane < pixel
-    period = 3
-    inside = [jnp.abs(lax.rem(lane + v * LANES, SIDE) - pixel) <= CYCLE for v in range(period)]
-    at = own_ref[...]
-    target = lax.broadcasted_iota(i32, (OFFS_PAD, reach), 1)
-    for i in range(BAND):
-        moved = at + i * SIDE
-        moved = jnp.where(moved >= reach, moved - reach, moved)
-        pick = jnp.where(target == jnp.where(at < 0, -1, moved), 1.0, 0.0).astype(bf16)
-        w = jnp.concatenate(
-            [weights[(g * BAND + i) * SIDE : (g * BAND + i + 1) * SIDE, :OFFS_PAD] for g in range(bands)], axis=0)
-        wide[...] = dot(w.astype(bf16), pick)
-        for g in range(bands):
-            turned = [pltpu.roll(wide[g * SIDE : (g + 1) * SIDE, v * LANES : (v + 1) * LANES], 0, 1,
-                                 stride=1, stride_axis=0) for v in range(blocks)]
-            for v in range(blocks):
-                block = jnp.where(carried, turned[v - 1], turned[v])
-                bands_ref[g, i * SIDE : (i + 1) * SIDE, v * LANES : (v + 1) * LANES] = jnp.where(
-                    inside[v % period], block, 0.0).astype(bf16)
-    beside = beside_ref[tile]
-    for g in range(bands):
-        edges = []
-        for i in range(BAND):
-            base = (g * BAND + i) * SIDE
-            edges.append(jnp.where(tile == 0, weights[base + SIDE - CYCLE : base + SIDE, :],
-                                   weights[base : base + CYCLE, :]))
-        edge = jnp.concatenate(edges, axis=0)
-        for v in range(2):
-            lanes = slice(v * LANES, (v + 1) * LANES)
-            sides_ref[g, :, lanes] = jnp.take_along_axis(edge, beside[:, lanes], axis=1).astype(bf16)
-    banded(bands_ref, r_ref, x_ref)
-
-
-def banded_kernel(bands_ref, r_ref, x_ref):
-    banded(bands_ref, r_ref, x_ref)
+        first = g * BAND + low - CYCLE
+        for h in range(2):
+            r = r_ref[first : first + high - low, h * COL_STEP : h * COL_STEP + REACH, :]
+            x = dot(bands_ref[g, h, :, low * REACH : high * REACH], r.reshape((high - low) * REACH, frames))
+            x_ref[g * BAND : (g + 1) * BAND, h * HALF : (h + 1) * HALF, :] = x.reshape(BAND, HALF, frames)
 
 
 def trace_step(tile, count, halo_ref, sides_ref, x_ref, d_ref, foot_ref, trace_ref, den_ref,
                wide_halo, err, back_ref=None):
-    frames = x_ref.shape[1]
+    frames = x_ref.shape[2]
     band, edge = BAND * SIDE, CYCLE * SIDE
     pad = CYCLE * CYCLE
     wide_halo[:pad, :] = jnp.zeros((pad, frames), bf16)
@@ -214,13 +215,14 @@
         side = dot(sides_ref[g], wide_halo[pl.ds(g * BAND * CYCLE, reach), :]).reshape(BAND, CYCLE, frames)
         left = jnp.where(tile == 0, 0.0, side)
         right = jnp.where(tile == 0, side, 0.0)
-        x = x_ref[rows, :].reshape(BAND, SIDE, frames)
+        x = x_ref[pl.ds(g * BAND, BAND)]
         x = jnp.concatenate(
             [x[:, :CYCLE] + left, x[:, CYCLE : SIDE - CYCLE], x[:, SIDE - CYCLE :] + right], axis=1)
         back = x.reshape(band, frames).astype(bf16)
         if back_ref is not None:
             back_ref[rows, :] = back
-        err[rows, :] = (back.astype(f32) - d_ref[rows, :]).astype(bf16)
+        d = d_ref[pl.ds(g * BAND, BAND)].reshape(band, frames)
+        err[rows, :] = (back.astype(f32) - d).astype(bf16)
     grad = lax.dot_general(foot_ref[...], err[...], (((0,), (0,)), ((), ())), preferred_element_type=f32)
     comps = grad.shape[0]
     live = lax.broadcasted_iota(i32, (comps, 1), 0) < count
@@ -337,7 +339,6 @@
     band = BAND * SIDE
     bands = SIDE // BAND
     edge = SIDE * CYCLE
-    reach = (BAND + 2 * CYCLE) * SIDE
     tile = lax.axis_index("tile").astype(i32).reshape(1)
     me = lax.axis_index("tm").astype(i32).reshape(1)
     own, beside = band_tables()
@@ -348,39 +349,36 @@
     err_buf = pltpu.VMEM((pixels, frames), bf16)
     one_row = pltpu.VMEM((1, comps), i32)
 
-    foot, trace, den, d, r, pay, movie = pl.pallas_call(
+    d_shape, r_shape = sds((SIDE, SIDE, frames), f32), sds((SIDE, SIDE, frames), bf16)
+    inputs = [pltpu.with_memory_space_constraint(v, pltpu.HBM) for v in (
+        movie, fp, tr, centre_row, centre_col, radius, weights, jnp.asarray(own), jnp.asarray(beside))]
+    foot, trace, den, d, r, pay, movie, band_w, side_w = pl.pallas_call(
         start_kernel,
         out_shape=(sds((pixels, comps), bf16), sds((comps, frames), bf16), sds((comps, LANES), f32),
-                   sds((pixels, frames), f32), sds((pixels, frames), bf16), sds((edge, frames), bf16),
-                   sds((pixels, frames), bf16)),
-        in_specs=[SM, SM] + [HB] * 6, out_specs=[VM] * 7,
+                   d_shape, r_shape, sds((edge, frames), bf16), sds((pixels, frames), bf16),
+                   sds((bands, 2, BAND * HALF, RANGE), bf16), sds((bands, CYCLE * BAND, beside.shape[2]), bf16)),
+        in_specs=[SM, SM] + [HB] * 9, out_specs=[VM] * 9,
         scratch_shapes=[pltpu.VMEM((pixels, comps), bf16), pltpu.VMEM((comps, frames), bf16),
-                        one_row, one_row, one_row, pltpu.SemaphoreType.DMA((2 * bands + 4,))],
-        compiler_params=params(),
-    )(tile, comp_count, *[pltpu.with_memory_space_constraint(v, pltpu.HBM) for v in (movie, fp, tr, centre_row, centre_col, radius)])
+                        one_row, one_row, one_row, pltpu.VMEM(weights.shape, bf16), pltpu.VMEM(own.shape, i32),
+                        pltpu.VMEM(beside.shape[1:], i32), pltpu.VMEM((pixels, LANES), f32),
+                        pltpu.VMEM((2, bands * SIDE, RANGE), f32), pltpu.SemaphoreType.DMA((2 * bands + 7,))],
+        compiler_params=params(16),
+    )(tile, comp_count, *inputs)
+    banded = pl.pallas_call(
+        banded_kernel,
+        out_shape=d_shape, in_specs=[VM, VM], out_specs=VM, compiler_params=params(),
+        cost_estimate=pl.CostEstimate(flops=4_000_000_000, bytes_accessed=20_000_000, transcendentals=0),
+    )
     halo = swap(pay)
-    banded_cost = pl.CostEstimate(flops=4_000_000_000, bytes_accessed=20_000_000, transcendentals=0)
-    band_w, side_w, x = pl.pallas_call(
-        build_kernel,
-        out_shape=(sds((bands, band, reach), bf16), sds((bands, CYCLE * BAND, beside.shape[2]), bf16),
-                   sds((pixels, frames), f32)),
-        in_specs=[SM] + [VM] * 4, out_specs=[VM] * 3,
-        scratch_shapes=[pltpu.VMEM((pixels, LANES), f32), pltpu.VMEM((bands * SIDE, reach), f32)],
-        compiler_params=params(), cost_estimate=banded_cost,
-    )(tile, weights, jnp.asarray(own), jnp.asarray(beside), r)
+    x = banded(band_w, r)
     trace, d, r, pay = pl.pallas_call(
         pass_kernel,
-        out_shape=(sds((comps, frames), bf16), sds((pixels, frames), f32), sds((pixels, frames), bf16),
-                   sds((edge, frames), bf16)),
+        out_shape=(sds((comps, frames), bf16), d_shape, r_shape, sds((edge, frames), bf16)),
         in_specs=[SM, SM] + [VM] * 8, out_specs=[VM] * 4,
         scratch_shapes=[halo_pad, err_buf], compiler_params=params(),
     )(tile, comp_count, halo, side_w, x, d, foot, trace, den, movie)
     halo = swap(pay)
-    x = pl.pallas_call(
-        banded_kernel,
-        out_shape=sds((pixels, frames), f32),
-        in_specs=[VM, VM], out_specs=VM, compiler_params=params(), cost_estimate=banded_cost,
-    )(band_w, r)
+    x = banded(band_w, r)
     trace, part, fold = pl.pallas_call(
         functools.partial(last_kernel, block, share),
         out_shape=(sds((comps, frames), bf16), sds((packed, comps), bf16), sds((packed // 2, slots.shape[1]), bf16)),

time: 54 us -> 51.3 us (0.950)
  Pallas kernels: 24.1 us -> 21.6 us
    pallas_call x3, Pallas kernels: 11.3 us -> 6.52 us  [the longest x2 3.61 us: shards(): x = banded(band_w, r)]
    pallas_call x1, Pallas kernels: 4.27 us -> 6.57 us  [shards(): pl.pallas_call(start_kernel, out_shape=(sds((pixels, comps), bf16), sds((...]
  transfers between devices with their start and end apart: 3 -> 3, of which waited for: 1 -> 1; matrix products, arithmetic and copies ran while one was open for 0% -> 0% of each run, Pallas kernels for 17% -> 8%
where the time goes in v4:
time: 51.3 us; the launch traced here: 51.1 us
  Pallas kernels  21.6 us (42%)
  blocking collectives  11.6 us (23%)
  waiting for transfers between devices  8.34 us (16%)
  starting transfers between devices  7.91 us (15%)
  between operations  1.57 us (3%)
    all_to_all x1, blocking collectives, shards(): lax.all_to_all(moved, 'tm', 0, 0, tiled=False).reshape(packed, comps)  11.6 us
    all_to_all x1, waiting for transfers between devices, shards(): lax.all_to_all(part.reshape(parts, block, comps), 'tm', 0, 0, tiled=False)  8.34 us
    all_to_all x1, starting transfers between devices, shards(): lax.all_to_all(part.reshape(parts, block, comps), 'tm', 0, 0, tiled=False)  7.28 us
    pallas_call x1, Pallas kernels, shards(): pl.pallas_call(start_kernel, out_shape=(sds((pixels, comps), bf16), sds((...  6.57 us
    pallas_call x1, Pallas kernels, shards(): pl.pallas_call(functools.partial(last_kernel, block, share), out_shape=(s...  6.32 us
    pallas_call x2, Pallas kernels, shards(): x = banded(band_w, r)  3.61 us
    pallas_call x1, Pallas kernels, shards(): pl.pallas_call(pass_kernel, out_shape=(sds((comps, frames), bf16), d_shap...  2.91 us
    pallas_call x1, Pallas kernels, shards(): pl.pallas_call(unfold_kernel, out_shape=sds((pixels, comps), bf16), in_sp...  1.58 us
  transfers between devices with their start and end apart: 3, of which 1 were waited for; matrix products, arithmetic and copies ran while one was open for 0% of the time, Pallas kernels for 8%

profile of v4, /device:TPU:0, one launch (start us, length us, event | category | flops | bytes accessed | tf_op | source)
XLA Modules:
  0.0 51.1 jit_solution(2743912370643418162)
XLA Ops:
  1.3 6.6 %shard_map.122 = (bf16[2304,384]{1,0:T(8,128)(2,1)S(1)}, bf16[384,512]{1,0:T(8,128)(2,1)S(1)}, f32[384,128]{1,0:T(8,128)S(1)}, f32[48,48,512]{2,1,0:T(8,128)S(1)...) custom-call(s32[1]{0:T(128)} %bitcast.1.tile_ref, ...), custom_call_target="tpu_custom_call" | custom-call | tf_op jit(solution)/shard_map/pallas_call | solution.py:355
  7.9 0.6 %collective-permute-start = (bf16[384,512]{1,0:T(8,128)(2,1)S(1)}, bf16[384,512]{1,0:T(8,128)(2,1)S(1)}, u32[]{:S(2)}, u32[]{:S(2)}) collective-permute-start(bf16[384,512]{1,0:T(8,128)(2,1)S(1)} %get-tuple-element.18), channel_id=1, source_target_pairs={{0,1},{1,0},{2,3},{3,2},{4,5},{5,4},{6,7},{7,6},{8,9},{9,8},{10,11... | collective-permute-start | bytes 1179656 | tf_op jit(solution)/shard_map/ppermute | solution.py:329
  8.4 1.8 %shard_map.123.x_ref = f32[48,48,512]{2,1,0:T(8,128)S(1)} custom-call(bf16[6,2,192,768]{3,2,1,0:T(8,128)(2,1)S(1)} %get-tuple-element.20.bands_ref, bf16[48,48,512]{2,1,0:T(8,128)(2,1)S(1)} %get-tuple-element.21.r_ref), custom_call_target="tpu_custom_call" | custom-call | flops 4000000000 | bytes 20000000 | tf_op jit(solution)/shard_map/pallas_call | solution.py:373
  10.2 0.0 collective-permute-done.halo_ref
  10.2 2.9 %shard_map.124 = (bf16[384,512]{1,0:T(8,128)(2,1)S(1)}, f32[48,48,512]{2,1,0:T(8,128)S(1)}, bf16[48,48,512]{2,1,0:T(8,128)(2,1)S(1)}, bf16[384,512]{1,0:T(8,128)(2,1)S(1)}) custom-call(s32[1]{0:T(128)} %bitcast.1.tile_ref, s32[1]{0:T(128)S(6)} %copy.13.count_ref, bf16[384,512]{1,0:T(8,128)(2,1)S(1)} %collective-permute-done.halo_ref, ...), custom_call_target="tpu_custom_call" | custom-call | tf_op jit(solution)/shard_map/pallas_call | solution.py:374
  13.2 0.1 collective-permute-start.1
  13.2 0.0 copy-start
  13.2 0.0 copy-start.1
  13.3 0.0 copy-start.2
  13.3 0.0 copy-start.3
  13.3 1.8 %shard_map.125.x_ref = f32[48,48,512]{2,1,0:T(8,128)S(1)} custom-call(bf16[6,2,192,768]{3,2,1,0:T(8,128)(2,1)S(1)} %get-tuple-element.20.bands_ref, bf16[48,48,512]{2,1,0:T(8,128)(2,1)S(1)} %get-tuple-element.28.r_ref), custom_call_target="tpu_custom_call" | custom-call | flops 4000000000 | bytes 20000000 | tf_op jit(solution)/shard_map/pallas_call | solution.py:381
  15.1 0.0 collective-permute-done.1.halo_ref
  15.1 0.0 copy-done
  15.1 0.0 copy-done.1
  15.1 0.0 copy-done.2
  15.1 0.0 copy-done.3
  15.1 6.3 %shard_map.126 = (bf16[384,512]{1,0:T(8,128)(2,1)}, bf16[320,384]{1,0:T(8,128)(2,1)}, bf16[160,1152]{1,0:T(8,128)(2,1)S(1)}) custom-call(s32[1]{0:T(128)} %bitcast.1.tile_ref, s32[1]{0:T(128)S(6)} %copy.13.count_ref, bf16[384,512]{1,0:T(8,128)(2,1)S(1)} %collective-permute-done.1.halo_ref, bf16[6,64,256]{2,1,0:T(8,128)(2,1)S(1)} %get-tuple-element.19.sides_ref, ...), custom_call_target="tpu_custom_call" | custom-call | tf_op jit(solution)/shard_map/pallas_call | solution.py:382
  21.5 7.3 %all-to-all-start = ((bf16[8,40,384]{2,1,0:T(8,128)(2,1)}), bf16[8,40,384]{2,1,0:T(8,128)(2,1)S(1)}, u32[]{:S(2)}, u32[]{:S(2)}) async-start(bf16[8,40,384]{2,1,0:T(8,128)(2,1)} %bitcast.7), calls=%async_computation | async-start | bytes 491520 | tf_op jit(solution)/shard_map/all_to_all | solution.py:390
  28.7 0.6 %shard_map.127.ffold_ref = f32[320,384]{1,0:T(8,128)S(1)} custom-call(bf16[160,1152]{1,0:T(8,128)(2,1)S(1)} %get-tuple-element.32.fold_ref, bf16[2304,384]{1,0:T(8,128)(2,1)S(1)} %get-tuple-element.23.foot_ref), custom_call_target="tpu_custom_call" | custom-call | tf_op jit(solution)/shard_map/pallas_call | solution.py:391
  29.3 8.3 %all-to-all-done.parts_ref = bf16[8,40,384]{2,1,0:T(8,128)(2,1)S(1)} async-done(((bf16[8,40,384]{2,1,0:T(8,128)(2,1)}), bf16[8,40,384]{2,1,0:T(8,128)(2,1)S(1)}, u32[]{:S(2)}, u32[]{:S(2)}) %all-to-all-start) | async-done | bytes 245792 | tf_op jit(solution)/shard_map/all_to_all | solution.py:390
  37.6 0.1 shard_map.128
  37.7 11.6 %all_to_all.10 = bf16[8,40,384]{2,1,0:T(8,128)(2,1)S(1)} all-to-all(bf16[8,40,384]{2,1,0:T(8,128)(2,1)S(1)} %shard_map.128), channel_id=1, replica_groups=mesh['groups'=2,'tm'=8,'tile'=2] {'tm'}, dimensions={0} | all-to-all | bytes 491520 | tf_op jit(solution)/shard_map/all_to_all | solution.py:401
  49.3 1.6 %shard_map.129 = bf16[2304,384]{1,0:T(8,128)(2,1)} custom-call(s32[1]{0:T(128)S(6)} %copy.13.count_ref, bf16[320,384]{1,0:T(8,128)(2,1)S(1)} %bitcast.12, bf16[160,1152]{1,0:T(8,128)(2,1)S(1)} %get-tuple-element.32.fold_ref, s32[1,384]{1,0:T(1,128)S(1)} %copy-done, s32[1,384]{1,0:T(1,128)S(1)} %copy-done.1, s32[1,384]{1,0:T(1,128)S(1)} %copy-done.2), custom_call_target="tpu_custom_call" | custom-call | tf_op jit(solution)/shard_map/pallas_call | solution.py:402
Async XLA Ops:
  7.9 2.4 %collective-permute-start = (bf16[384,512]{1,0:T(8,128)(2,1)S(1)}, bf16[384,512]{1,0:T(8,128)(2,1)S(1)}, u32[]{:S(2)}, u32[]{:S(2)}) collective-permute-start(bf16[384,512]{1,0:T(8,128)(2,1)S(1)} %get-tuple-element.18), channel_id=1, source_target_pairs={{0,1},{1,0},{2,3},{3,2},{4,5},{5,4},{6,7},{7,6},{8,9},{9,8},{10,11... | collective-permute-start | bytes 1179656 | tf_op jit(solution)/shard_map/ppermute | solution.py:329
  13.2 1.9 %collective-permute-start.1 = (bf16[384,512]{1,0:T(8,128)(2,1)S(1)}, bf16[384,512]{1,0:T(8,128)(2,1)S(1)}, u32[]{:S(2)}, u32[]{:S(2)}) collective-permute-start(bf16[384,512]{1,0:T(8,128)(2,1)S(1)} %get-tuple-element.27), channel_id=1, source_target_pairs={{0,1},{1,0},{2,3},{3,2},{4,5},{5,4},{6,7},{7,6},{8,9},{9,8},{10,11... | collective-permute-start | bytes 1179656 | tf_op jit(solution)/shard_map/ppermute | solution.py:329
  13.2 1.9 %copy-start = (s32[1,384]{1,0:T(1,128)S(1)}, s32[1,384]{1,0:T(1,128)}, u32[]{:S(2)}) copy-start(s32[1,384]{1,0:T(1,128)} %cr_ref.3) | copy-start | bytes 4612
  13.2 1.9 %copy-start.1 = (s32[1,384]{1,0:T(1,128)S(1)}, s32[1,384]{1,0:T(1,128)}, u32[]{:S(2)}) copy-start(s32[1,384]{1,0:T(1,128)} %cc_ref.3) | copy-start | bytes 4612
  13.3 1.9 %copy-start.2 = (s32[1,384]{1,0:T(1,128)S(1)}, s32[1,384]{1,0:T(1,128)}, u32[]{:S(2)}) copy-start(s32[1,384]{1,0:T(1,128)} %rad_ref.3) | copy-start | bytes 4612
  13.3 1.9 %copy-start.3 = (s32[1,1152]{1,0:T(1,128)S(1)}, s32[1,1152]{1,0:T(1,128)}, u32[]{:S(2)}) copy-start(s32[1,1152]{1,0:T(1,128)} %constant.16.clone.slot_ref) | copy-start | bytes 13828
  21.5 16.2 %all-to-all-start = ((bf16[8,40,384]{2,1,0:T(8,128)(2,1)}), bf16[8,40,384]{2,1,0:T(8,128)(2,1)S(1)}, u32[]{:S(2)}, u32[]{:S(2)}) async-start(bf16[8,40,384]{2,1,0:T(8,128)(2,1)} %bitcast.7), calls=%async_computation | async-start | bytes 491520 | tf_op jit(solution)/shard_map/all_to_all | solution.py:390

commit v5 on v4

--- a/solution.py
+++ b/solution.py
@@ -92,11 +92,10 @@
     return gap * gap
 
 
-def resid_band(g, tile, movie_ref, foot, trace, d_ref, r_ref, pay_ref):
+def resid_band(g, tile, movie_ref, foot, trace, r_ref, pay_ref):
     band = BAND * SIDE
     d = movie_ref[pl.ds(g * band, band), :].astype(f32) - dot(foot, trace)
     d3 = d.reshape(BAND, SIDE, d.shape[1])
-    d_ref[pl.ds(g * BAND, BAND)] = d3
     r_ref[pl.ds(g * BAND, BAND)] = d3.astype(bf16)
     edge = jnp.where(tile == 0, d3[:, SIDE - CYCLE :], d3[:, :CYCLE])
     pay_ref[pl.ds(g * BAND * CYCLE, BAND * CYCLE), :] = edge.reshape(BAND * CYCLE, d.shape[1]).astype(bf16)
@@ -146,7 +145,7 @@
 
 def start_kernel(tile_ref, count_ref, movie_hbm, fp_hbm, tr_hbm, cr_hbm, cc_hbm, rad_hbm,
                  w_hbm, own_hbm, beside_hbm,
-                 foot_ref, trace_ref, den_ref, d_ref, r_ref, pay_ref, movie_ref, bands_ref, sides_ref,
+                 foot_ref, trace_ref, den_ref, r_ref, pay_ref, movie_ref, bands_ref, sides_ref,
                  fp_ref, tr_ref, cr_ref, cc_ref, rad_ref, w_ref, own_ref, beside_ref, weights, wide, sems):
     count, tile = count_ref[0], tile_ref[0]
     comps = tr_ref.shape[0]
@@ -165,9 +164,11 @@
     for g in range(bands):
         fps[g].start()
         movies[g].start()
-    for copy in small:
+    for copy in small[:3]:
         copy.wait()
     build_bands(tile, w_ref[...], own_ref[:, :1], beside_ref[...], bands_ref, sides_ref, weights, wide)
+    for copy in small[3:] + fps + movies:
+        copy.wait()
     live = lax.broadcasted_iota(i32, (comps, 1), 0) < count
     trace = jnp.where(live, tr_ref[...].astype(f32), 0.0).astype(bf16)
     trace_ref[...] = trace
@@ -175,32 +176,35 @@
     cr, rad = cr_ref[...], rad_ref[...]
     total = jnp.zeros((8, comps), f32)
     for g in range(bands):
-        fps[g].wait()
         for i in range(BAND):
             row = g * BAND + i
             keep = gap_sq <= disc_limit(cr, rad, count, row)
             foot = jnp.where(keep, fp_ref[pl.ds(row * SIDE, SIDE), :].astype(f32), 0.0)
             foot_ref[pl.ds(row * SIDE, SIDE), :] = foot.astype(bf16)
             total = total + jnp.sum((foot * foot).reshape(SIDE // 8, 8, comps), axis=0)
-        movies[g].wait()
-        resid_band(g, tile, movie_ref, foot_ref[pl.ds(g * band, band), :], trace, d_ref, r_ref, pay_ref)
+        resid_band(g, tile, movie_ref, foot_ref[pl.ds(g * band, band), :], trace, r_ref, pay_ref)
     energy = jnp.sum(total, axis=0, keepdims=True) + RIDGE
-    den_ref[...] = jnp.transpose(jnp.broadcast_to(energy, (LANES, comps)))
-
-
-def banded_kernel(bands_ref, r_ref, x_ref):
+    den_ref[...] = jnp.transpose(jnp.broadcast_to(1.0 / energy, (LANES, comps)))
+
+
+def banded_kernel(tile_ref, bands_ref, r_ref, x_ref, edge_ref):
+    tile = tile_ref[0]
     frames = r_ref.shape[2]
     for g in range(SIDE // BAND):
         low = max(0, CYCLE - g * BAND)
         high = min(BAND + 2 * CYCLE, SIDE + CYCLE - g * BAND)
         first = g * BAND + low - CYCLE
+        halves = []
         for h in range(2):
             r = r_ref[first : first + high - low, h * COL_STEP : h * COL_STEP + REACH, :]
             x = dot(bands_ref[g, h, :, low * REACH : high * REACH], r.reshape((high - low) * REACH, frames))
-            x_ref[g * BAND : (g + 1) * BAND, h * HALF : (h + 1) * HALF, :] = x.reshape(BAND, HALF, frames)
-
-
-def trace_step(tile, count, halo_ref, sides_ref, x_ref, d_ref, foot_ref, trace_ref, den_ref,
+            halves.append(x.reshape(BAND, HALF, frames))
+        rows = pl.ds(g * BAND, BAND)
+        edge_ref[rows] = jnp.where(tile == 0, halves[1][:, HALF - CYCLE :], halves[0][:, :CYCLE])
+        x_ref[rows] = jnp.concatenate(halves, axis=1).astype(bf16)
+
+
+def trace_step(tile, count, halo_ref, sides_ref, x_ref, edge_ref, r_ref, foot_ref, trace_ref, den_ref,
                wide_halo, err, back_ref=None):
     frames = x_ref.shape[2]
     band, edge = BAND * SIDE, CYCLE * SIDE
@@ -210,75 +214,77 @@
     tail = wide_halo.shape[0] - pad - edge
     wide_halo[pl.ds(pad + edge, tail), :] = jnp.zeros((tail, frames), bf16)
     for g in range(SIDE // BAND):
-        rows = pl.ds(g * band, band)
+        rows = pl.ds(g * BAND, BAND)
         reach = sides_ref.shape[2]
         side = dot(sides_ref[g], wide_halo[pl.ds(g * BAND * CYCLE, reach), :]).reshape(BAND, CYCLE, frames)
-        left = jnp.where(tile == 0, 0.0, side)
-        right = jnp.where(tile == 0, side, 0.0)
-        x = x_ref[pl.ds(g * BAND, BAND)]
-        x = jnp.concatenate(
-            [x[:, :CYCLE] + left, x[:, CYCLE : SIDE - CYCLE], x[:, SIDE - CYCLE :] + right], axis=1)
-        back = x.reshape(band, frames).astype(bf16)
+        side = (edge_ref[rows] + side).astype(bf16).astype(f32)
+        x = x_ref[rows].astype(f32)
+        left = jnp.where(tile == 0, x[:, :CYCLE], side)
+        right = jnp.where(tile == 0, side, x[:, SIDE - CYCLE :])
+        back = jnp.concatenate([left, x[:, CYCLE : SIDE - CYCLE], right], axis=1)
         if back_ref is not None:
-            back_ref[rows, :] = back
-        d = d_ref[pl.ds(g * BAND, BAND)].reshape(band, frames)
-        err[rows, :] = (back.astype(f32) - d).astype(bf16)
+            back_ref[rows] = back.astype(bf16)
+        err[pl.ds(g * band, band), :] = (back - r_ref[rows].astype(f32)).reshape(band, frames).astype(bf16)
     grad = lax.dot_general(foot_ref[...], err[...], (((0,), (0,)), ((), ())), preferred_element_type=f32)
     comps = grad.shape[0]
     live = lax.broadcasted_iota(i32, (comps, 1), 0) < count
-    moved = jnp.maximum(trace_ref[...].astype(f32) - grad / den_ref[:, :1], 0.0)
+    moved = jnp.maximum(trace_ref[...].astype(f32) - grad * den_ref[:, :1], 0.0)
     return jnp.where(live, moved, 0.0)
 
 
-def pass_kernel(tile_ref, count_ref, halo_ref, sides_ref, x_ref, d_ref, foot_ref, trace_ref, den_ref,
-                movie_ref, new_trace_ref, new_d_ref, new_r_ref, pay_ref, wide_halo, err):
+def pass_kernel(tile_ref, count_ref, halo_ref, sides_ref, x_ref, edge_ref, r_ref, foot_ref, trace_ref, den_ref,
+                movie_ref, new_trace_ref, new_r_ref, pay_ref, wide_halo, err):
     tile, count = tile_ref[0], count_ref[0]
-    trace = trace_step(tile, count, halo_ref, sides_ref, x_ref, d_ref, foot_ref, trace_ref, den_ref,
+    trace = trace_step(tile, count, halo_ref, sides_ref, x_ref, edge_ref, r_ref, foot_ref, trace_ref, den_ref,
                        wide_halo, err).astype(bf16)
     new_trace_ref[...] = trace
     for g in range(SIDE // BAND):
         resid_band(g, tile, movie_ref, foot_ref[pl.ds(g * BAND * SIDE, BAND * SIDE), :], trace,
-                   new_d_ref, new_r_ref, pay_ref)
-
-
-def last_kernel(block, share, tile_ref, count_ref, halo_ref, sides_ref, x_ref, d_ref, foot_ref, trace_ref,
+                   new_r_ref, pay_ref)
+
+
+def last_kernel(block, share, tile_ref, count_ref, halo_ref, sides_ref, x_ref, edge_ref, r_ref, foot_ref, trace_ref,
                 den_ref, movie_ref, cr_ref, cc_ref, rad_ref, slot_ref,
-                trace_hbm, part_ref, fold_ref, wide_halo, err, back, masked, new_trace, sem):
+                trace_hbm, part_hbm, fold_ref, wide_halo, err, back, masked, new_trace, part_ref, sems):
     tile, count = tile_ref[0], count_ref[0]
-    trace = trace_step(tile, count, halo_ref, sides_ref, x_ref, d_ref, foot_ref, trace_ref, den_ref,
+    trace = trace_step(tile, count, halo_ref, sides_ref, x_ref, edge_ref, r_ref, foot_ref, trace_ref, den_ref,
                        wide_halo, err, back).astype(bf16)
     new_trace[...] = trace
-    store = pltpu.make_async_copy(new_trace, trace_hbm, sem)
-    store.start()
+    stores = [pltpu.make_async_copy(new_trace, trace_hbm, sems.at[2])]
+    stores[0].start()
     comps = trace.shape[0]
     tf = trace.astype(f32)
     energy = jnp.sum(tf * tf, axis=1, keepdims=True)
     energy = jnp.transpose(jnp.broadcast_to(energy, (comps, LANES)))[:1]
     high = energy.astype(bf16).astype(f32)
     low = energy - high
-    gap_sq = col_gap_sq(cc_ref[...])
-    cr, rad = cr_ref[...], rad_ref[...]
-    band = BAND * SIDE
-    for g in range(SIDE // BAND):
-        rows = pl.ds(g * band, band)
-        prod = dot(foot_ref[rows, :], trace)
-        ferr = (prod + back[rows, :].astype(f32) - movie_ref[rows, :].astype(f32)).astype(bf16)
-        grad = lax.dot_general(ferr, trace, (((1,), (1,)), ((), ())), preferred_element_type=f32)
-        for i in range(BAND):
-            row = g * BAND + i
-            keep = gap_sq <= disc_limit(cr, rad, count, row)
-            masked[g % 2, pl.ds(g // 2 * band + i * SIDE, SIDE), :] = jnp.where(
-                keep, grad[i * SIDE : (i + 1) * SIDE], 0.0).astype(bf16)
     half, taken = fold_ref.shape
     at = lax.broadcasted_iota(i32, (half, taken), 0)
     fold = jnp.where(at == slot_ref[...], 1.0, 0.0).astype(bf16)
     fold_ref[...] = fold
     inner = lax.rem(lax.broadcasted_iota(i32, (half, comps), 0), block)
+    gap_sq = col_gap_sq(cc_ref[...])
+    cr, rad = cr_ref[...], rad_ref[...]
+    band = BAND * SIDE
     for h in range(2):
+        for g in range(h, SIDE // BAND, 2):
+            rows = pl.ds(g * band, band)
+            prod = dot(foot_ref[rows, :], trace)
+            old = back[pl.ds(g * BAND, BAND)].reshape(band, prod.shape[1]).astype(f32)
+            ferr = (prod + old - movie_ref[rows, :].astype(f32)).astype(bf16)
+            grad = lax.dot_general(ferr, trace, (((1,), (1,)), ((), ())), preferred_element_type=f32)
+            for i in range(BAND):
+                keep = gap_sq <= disc_limit(cr, rad, count, g * BAND + i)
+                masked[h, pl.ds(g // 2 * band + i * SIDE, SIDE), :] = jnp.where(
+                    keep, grad[i * SIDE : (i + 1) * SIDE], 0.0).astype(bf16)
         part = dot(fold, masked[h])
         part = jnp.where(inner == share, high, jnp.where(inner == share + 1, low, part))
-        part_ref[h * half : (h + 1) * half, :] = part.astype(bf16)
-    store.wait()
+        rows = pl.ds(h * half, half)
+        part_ref[rows, :] = part.astype(bf16)
+        stores.append(pltpu.make_async_copy(part_ref.at[rows, :], part_hbm.at[rows, :], sems.at[h]))
+        stores[-1].start()
+    for store in stores:
+        store.wait()
 
 
 def foot_fold_kernel(fold_ref, foot_ref, out_ref):
@@ -349,15 +355,15 @@
     err_buf = pltpu.VMEM((pixels, frames), bf16)
     one_row = pltpu.VMEM((1, comps), i32)
 
-    d_shape, r_shape = sds((SIDE, SIDE, frames), f32), sds((SIDE, SIDE, frames), bf16)
+    r_shape = sds((SIDE, SIDE, frames), bf16)
     inputs = [pltpu.with_memory_space_constraint(v, pltpu.HBM) for v in (
         movie, fp, tr, centre_row, centre_col, radius, weights, jnp.asarray(own), jnp.asarray(beside))]
-    foot, trace, den, d, r, pay, movie, band_w, side_w = pl.pallas_call(
+    foot, trace, den, r, pay, movie, band_w, side_w = pl.pallas_call(
         start_kernel,
         out_shape=(sds((pixels, comps), bf16), sds((comps, frames), bf16), sds((comps, LANES), f32),
-                   d_shape, r_shape, sds((edge, frames), bf16), sds((pixels, frames), bf16),
+                   r_shape, sds((edge, frames), bf16), sds((pixels, frames), bf16),
                    sds((bands, 2, BAND * HALF, RANGE), bf16), sds((bands, CYCLE * BAND, beside.shape[2]), bf16)),
-        in_specs=[SM, SM] + [HB] * 9, out_specs=[VM] * 9,
+        in_specs=[SM, SM] + [HB] * 9, out_specs=[VM] * 8,
         scratch_shapes=[pltpu.VMEM((pixels, comps), bf16), pltpu.VMEM((comps, frames), bf16),
                         one_row, one_row, one_row, pltpu.VMEM(weights.shape, bf16), pltpu.VMEM(own.shape, i32),
                         pltpu.VMEM(beside.shape[1:], i32), pltpu.VMEM((pixels, LANES), f32),
@@ -366,27 +372,30 @@
     )(tile, comp_count, *inputs)
     banded = pl.pallas_call(
         banded_kernel,
-        out_shape=d_shape, in_specs=[VM, VM], out_specs=VM, compiler_params=params(),
+        out_shape=(r_shape, sds((SIDE, CYCLE, frames), f32)), in_specs=[SM, VM, VM], out_specs=[VM, VM],
+        compiler_params=params(),
         cost_estimate=pl.CostEstimate(flops=4_000_000_000, bytes_accessed=20_000_000, transcendentals=0),
     )
     halo = swap(pay)
-    x = banded(band_w, r)
-    trace, d, r, pay = pl.pallas_call(
+    x, beyond = banded(tile, band_w, r)
+    trace, new_r, pay = pl.pallas_call(
         pass_kernel,
-        out_shape=(sds((comps, frames), bf16), d_shape, r_shape, sds((edge, frames), bf16)),
-        in_specs=[SM, SM] + [VM] * 8, out_specs=[VM] * 4,
+        out_shape=(sds((comps, frames), bf16), r_shape, sds((edge, frames), bf16)),
+        in_specs=[SM, SM] + [VM] * 9, out_specs=[VM] * 3,
         scratch_shapes=[halo_pad, err_buf], compiler_params=params(),
-    )(tile, comp_count, halo, side_w, x, d, foot, trace, den, movie)
+    )(tile, comp_count, halo, side_w, x, beyond, r, foot, trace, den, movie)
+    r = new_r
     halo = swap(pay)
-    x = banded(band_w, r)
+    x, beyond = banded(tile, band_w, r)
     trace, part, fold = pl.pallas_call(
         functools.partial(last_kernel, block, share),
         out_shape=(sds((comps, frames), bf16), sds((packed, comps), bf16), sds((packed // 2, slots.shape[1]), bf16)),
-        in_specs=[SM, SM] + [VM] * 12, out_specs=[HB, VM, VM],
-        scratch_shapes=[halo_pad, err_buf, pltpu.VMEM((pixels, frames), bf16), pltpu.VMEM((2, pixels // 2, comps), bf16),
-                        pltpu.VMEM((comps, frames), bf16), pltpu.SemaphoreType.DMA],
+        in_specs=[SM, SM] + [VM] * 13, out_specs=[HB, HB, VM],
+        scratch_shapes=[halo_pad, err_buf, pltpu.VMEM(r_shape.shape, bf16), pltpu.VMEM((2, pixels // 2, comps), bf16),
+                        pltpu.VMEM((comps, frames), bf16), pltpu.VMEM((packed, comps), bf16),
+                        pltpu.SemaphoreType.DMA((3,))],
         compiler_params=params(14),
-    )(tile, comp_count, halo, side_w, x, d, foot, trace, den, movie, centre_row, centre_col, radius, jnp.asarray(slots))
+    )(tile, comp_count, halo, side_w, x, beyond, r, foot, trace, den, movie, centre_row, centre_col, radius, jnp.asarray(slots))
     received = lax.all_to_all(part.reshape(parts, block, comps), "tm", 0, 0, tiled=False)
     ffold = pl.pallas_call(
         foot_fold_kernel,

time: 51.3 us -> 49.2 us (0.959)
  Pallas kernels: 21.6 us -> 19.5 us
    pallas_call x1, Pallas kernels: 6.57 us -> 4.97 us  [shards(): pl.pallas_call(start_kernel, out_shape=(sds((pixels, comps), bf16), sds((...]
  transfers between devices with their start and end apart: 3 -> 3, of which waited for: 1 -> 1; matrix products, arithmetic and copies ran while one was open for 0% -> 0% of each run, Pallas kernels for 8% -> 9%
where the time goes in v5:
time: 49.2 us; the launch traced here: 49 us
  Pallas kernels  19.5 us (40%)
  blocking collectives  11.6 us (24%)
  waiting for transfers between devices  8.33 us (17%)
  starting transfers between devices  7.92 us (16%)
  between operations  1.58 us (3%)
    all_to_all x1, blocking collectives, shards(): lax.all_to_all(moved, 'tm', 0, 0, tiled=False).reshape(packed, comps)  11.6 us
    all_to_all x1, waiting for transfers between devices, shards(): lax.all_to_all(part.reshape(parts, block, comps), 'tm', 0, 0, tiled=False)  8.33 us
    all_to_all x1, starting transfers between devices, shards(): lax.all_to_all(part.reshape(parts, block, comps), 'tm', 0, 0, tiled=False)  7.26 us
    pallas_call x1, Pallas kernels, shards(): pl.pallas_call(functools.partial(last_kernel, block, share), out_shape=(s...  5.82 us
    pallas_call x1, Pallas kernels, shards(): pl.pallas_call(start_kernel, out_shape=(sds((pixels, comps), bf16), sds((...  4.97 us
    pallas_call x2, Pallas kernels, shards(): x, beyond = banded(tile, band_w, r)  3.61 us
    pallas_call x1, Pallas kernels, shards(): pl.pallas_call(pass_kernel, out_shape=(sds((comps, frames), bf16), r_shap...  2.91 us
    pallas_call x1, Pallas kernels, shards(): pl.pallas_call(unfold_kernel, out_shape=sds((pixels, comps), bf16), in_sp...  1.58 us
  transfers between devices with their start and end apart: 3, of which 1 were waited for; matrix products, arithmetic and copies ran while one was open for 0% of the time, Pallas kernels for 9%

profile of v5, /device:TPU:0, one launch (start us, length us, event | category | flops | bytes accessed | tf_op | source)
XLA Modules:
  0.0 49.0 jit_solution(12378510691389202190)
XLA Ops:
  1.3 5.0 %shard_map.122 = (bf16[2304,384]{1,0:T(8,128)(2,1)S(1)}, bf16[384,512]{1,0:T(8,128)(2,1)S(1)}, f32[384,128]{1,0:T(8,128)S(1)}, bf16[48,48,512]{2,1,0:T(8,128)(2,...) custom-call(s32[1]{0:T(128)} %bitcast.1.tile_ref, ...), custom_call_target="tpu_custom_call" | custom-call | tf_op jit(solution)/shard_map/pallas_call | solution.py:361
  6.3 0.6 %collective-permute-start = (bf16[384,512]{1,0:T(8,128)(2,1)S(1)}, bf16[384,512]{1,0:T(8,128)(2,1)S(1)}, u32[]{:S(2)}, u32[]{:S(2)}) collective-permute-start(bf16[384,512]{1,0:T(8,128)(2,1)S(1)} %get-tuple-element.20), channel_id=1, source_target_pairs={{0,1},{1,0},{2,3},{3,2},{4,5},{5,4},{6,7},{7,6},{8,9},{9,8},{10,11... | collective-permute-start | bytes 1179656 | tf_op jit(solution)/shard_map/ppermute | solution.py:335
  6.8 1.8 %shard_map.123 = (bf16[48,48,512]{2,1,0:T(8,128)(2,1)S(1)}, f32[48,8,512]{2,1,0:T(8,128)S(1)}) custom-call(s32[1]{0:T(128)} %bitcast.1.tile_ref, bf16[6,2,192,768]{3,2,1,0:T(8,128)(2,1)S(1)} %get-tuple-element.22.bands_ref, bf16[48,48,512]{2,1,0:T(8,128)(2,1)S(1)} %get-tuple-element.23.r_ref), custom_call_target="tpu_custom_call" | custom-call | flops 4000000000 | bytes 20000000 | tf_op jit(solution)/shard_map/pallas_call | solution.py:380
  8.6 0.0 collective-permute-done.halo_ref
  8.7 2.9 %shard_map.124 = (bf16[384,512]{1,0:T(8,128)(2,1)S(1)}, bf16[48,48,512]{2,1,0:T(8,128)(2,1)S(1)}, bf16[384,512]{1,0:T(8,128)(2,1)S(1)}) custom-call(s32[1]{0:T(128)} %bitcast.1.tile_ref, s32[1]{0:T(128)S(6)} %copy.13.count_ref, bf16[384,512]{1,0:T(8,128)(2,1)S(1)} %collective-permute-done.halo_ref, bf16[6,64,256]{2,1,0:T(8,128)(2,1)S(1)} %get-tuple-element.21.sides_ref, ...), custom_call_target="tpu_custom_call" | custom-call | tf_op jit(solution)/shard_map/pallas_call | solution.py:381
  11.6 0.1 collective-permute-start.1
  11.7 0.0 copy-start
  11.7 0.0 copy-start.1
  11.7 0.0 copy-start.2
  11.7 0.0 copy-start.3
  11.7 1.8 %shard_map.125 = (bf16[48,48,512]{2,1,0:T(8,128)(2,1)S(1)}, f32[48,8,512]{2,1,0:T(8,128)S(1)}) custom-call(s32[1]{0:T(128)} %bitcast.1.tile_ref, bf16[6,2,192,768]{3,2,1,0:T(8,128)(2,1)S(1)} %get-tuple-element.22.bands_ref, bf16[48,48,512]{2,1,0:T(8,128)(2,1)S(1)} %get-tuple-element.31.r_ref), custom_call_target="tpu_custom_call" | custom-call | flops 4000000000 | bytes 20000000 | tf_op jit(solution)/shard_map/pallas_call | solution.py:389
  13.5 0.0 collective-permute-done.1.halo_ref
  13.5 0.0 copy-done
  13.5 0.0 copy-done.1
  13.6 0.0 copy-done.2
  13.6 0.0 copy-done.3
  13.6 5.8 %shard_map.126 = (bf16[384,512]{1,0:T(8,128)(2,1)}, bf16[320,384]{1,0:T(8,128)(2,1)}, bf16[160,1152]{1,0:T(8,128)(2,1)S(1)}) custom-call(s32[1]{0:T(128)} %bitcast.1.tile_ref, s32[1]{0:T(128)S(6)} %copy.13.count_ref, bf16[384,512]{1,0:T(8,128)(2,1)S(1)} %collective-permute-done.1.halo_ref, bf16[6,64,256]{2,1,0:T(8,128)(2,1)S(1)} %get-tuple-element.21.sides_ref, ...), custom_call_target="tpu_custom_call" | custom-call | tf_op jit(solution)/shard_map/pallas_call | solution.py:390
  19.4 7.3 %all-to-all-start = ((bf16[8,40,384]{2,1,0:T(8,128)(2,1)}), bf16[8,40,384]{2,1,0:T(8,128)(2,1)S(1)}, u32[]{:S(2)}, u32[]{:S(2)}) async-start(bf16[8,40,384]{2,1,0:T(8,128)(2,1)} %bitcast.7), calls=%async_computation | async-start | bytes 491520 | tf_op jit(solution)/shard_map/all_to_all | solution.py:399
  26.7 0.6 %shard_map.127.ffold_ref = f32[320,384]{1,0:T(8,128)S(1)} custom-call(bf16[160,1152]{1,0:T(8,128)(2,1)S(1)} %get-tuple-element.36.fold_ref, bf16[2304,384]{1,0:T(8,128)(2,1)S(1)} %get-tuple-element.26.foot_ref), custom_call_target="tpu_custom_call" | custom-call | tf_op jit(solution)/shard_map/pallas_call | solution.py:400
  27.2 8.3 %all-to-all-done.parts_ref = bf16[8,40,384]{2,1,0:T(8,128)(2,1)S(1)} async-done(((bf16[8,40,384]{2,1,0:T(8,128)(2,1)}), bf16[8,40,384]{2,1,0:T(8,128)(2,1)S(1)}, u32[]{:S(2)}, u32[]{:S(2)}) %all-to-all-start) | async-done | bytes 245792 | tf_op jit(solution)/shard_map/all_to_all | solution.py:399
  35.6 0.1 shard_map.128
  35.6 11.6 %all_to_all.10 = bf16[8,40,384]{2,1,0:T(8,128)(2,1)S(1)} all-to-all(bf16[8,40,384]{2,1,0:T(8,128)(2,1)S(1)} %shard_map.128), channel_id=1, replica_groups=mesh['groups'=2,'tm'=8,'tile'=2] {'tm'}, dimensions={0} | all-to-all | bytes 491520 | tf_op jit(solution)/shard_map/all_to_all | solution.py:410
  47.2 1.6 %shard_map.129 = bf16[2304,384]{1,0:T(8,128)(2,1)} custom-call(s32[1]{0:T(128)S(6)} %copy.13.count_ref, bf16[320,384]{1,0:T(8,128)(2,1)S(1)} %bitcast.12, bf16[160,1152]{1,0:T(8,128)(2,1)S(1)} %get-tuple-element.36.fold_ref, s32[1,384]{1,0:T(1,128)S(1)} %copy-done, s32[1,384]{1,0:T(1,128)S(1)} %copy-done.1, s32[1,384]{1,0:T(1,128)S(1)} %copy-done.2), custom_call_target="tpu_custom_call" | custom-call | tf_op jit(solution)/shard_map/pallas_call | solution.py:411
Async XLA Ops:
  6.3 2.4 %collective-permute-start = (bf16[384,512]{1,0:T(8,128)(2,1)S(1)}, bf16[384,512]{1,0:T(8,128)(2,1)S(1)}, u32[]{:S(2)}, u32[]{:S(2)}) collective-permute-start(bf16[384,512]{1,0:T(8,128)(2,1)S(1)} %get-tuple-element.20), channel_id=1, source_target_pairs={{0,1},{1,0},{2,3},{3,2},{4,5},{5,4},{6,7},{7,6},{8,9},{9,8},{10,11... | collective-permute-start | bytes 1179656 | tf_op jit(solution)/shard_map/ppermute | solution.py:335
  11.6 1.9 %collective-permute-start.1 = (bf16[384,512]{1,0:T(8,128)(2,1)S(1)}, bf16[384,512]{1,0:T(8,128)(2,1)S(1)}, u32[]{:S(2)}, u32[]{:S(2)}) collective-permute-start(bf16[384,512]{1,0:T(8,128)(2,1)S(1)} %get-tuple-element.30), channel_id=1, source_target_pairs={{0,1},{1,0},{2,3},{3,2},{4,5},{5,4},{6,7},{7,6},{8,9},{9,8},{10,11... | collective-permute-start | bytes 1179656 | tf_op jit(solution)/shard_map/ppermute | solution.py:335
  11.7 1.9 %copy-start = (s32[1,384]{1,0:T(1,128)S(1)}, s32[1,384]{1,0:T(1,128)}, u32[]{:S(2)}) copy-start(s32[1,384]{1,0:T(1,128)} %cr_ref.3) | copy-start | bytes 4612
  11.7 1.9 %copy-start.1 = (s32[1,384]{1,0:T(1,128)S(1)}, s32[1,384]{1,0:T(1,128)}, u32[]{:S(2)}) copy-start(s32[1,384]{1,0:T(1,128)} %cc_ref.3) | copy-start | bytes 4612
  11.7 1.9 %copy-start.2 = (s32[1,384]{1,0:T(1,128)S(1)}, s32[1,384]{1,0:T(1,128)}, u32[]{:S(2)}) copy-start(s32[1,384]{1,0:T(1,128)} %rad_ref.3) | copy-start | bytes 4612
  11.7 1.9 %copy-start.3 = (s32[1,1152]{1,0:T(1,128)S(1)}, s32[1,1152]{1,0:T(1,128)}, u32[]{:S(2)}) copy-start(s32[1,1152]{1,0:T(1,128)} %constant.16.clone.slot_ref) | copy-start | bytes 13828
  19.4 16.2 %all-to-all-start = ((bf16[8,40,384]{2,1,0:T(8,128)(2,1)}), bf16[8,40,384]{2,1,0:T(8,128)(2,1)S(1)}, u32[]{:S(2)}, u32[]{:S(2)}) async-start(bf16[8,40,384]{2,1,0:T(8,128)(2,1)} %bitcast.7), calls=%async_computation | async-start | bytes 491520 | tf_op jit(solution)/shard_map/all_to_all | solution.py:399

commit v6 on v5

--- a/solution.py
+++ b/solution.py
@@ -43,10 +43,12 @@
 def band_tables():
     offsets = cycle_offsets()
     none = len(offsets)
-    own = np.full((OFFS_PAD, LANES), -1, np.int32)
+    own = np.full((OFFS_PAD + 8, LANES), -1, np.int32)
+    own[OFFS_PAD] = SIDE
     beside = np.full((2, BAND, CYCLE, 32, CYCLE), none, np.int32)
     for o, (dy, dx) in enumerate(offsets):
-        own[o] = ((CYCLE + dy) * REACH + dx) % RANGE
+        own[o] = (CYCLE + dy) * REACH + dx + CYCLE
+        own[OFFS_PAD, o] = dx
         for i in range(BAND):
             for q in range(CYCLE):
                 h = q + dx - CYCLE
@@ -101,36 +103,40 @@
     pay_ref[pl.ds(g * BAND * CYCLE, BAND * CYCLE), :] = edge.reshape(BAND * CYCLE, d.shape[1]).astype(bf16)
 
 
-def build_bands(tile, w, at, beside, bands_ref, sides_ref, weights, wide):
+def build_bands(tile, w, own_ref, beside, bands_ref, sides_ref, weights, wide):
     bands = SIDE // BAND
     blocks = RANGE // LANES
     offs = w.shape[0]
     eye = lax.broadcasted_iota(i32, (offs, LANES), 0) == lax.broadcasted_iota(i32, (offs, LANES), 1)
     weights[...] = lax.dot_general(w, jnp.where(eye, 1.0, 0.0).astype(bf16), (((0,), (0,)), ((), ())),
                                    preferred_element_type=f32)
-    column = lax.broadcasted_iota(i32, (HALF, LANES), 0)
-    lane = lax.broadcasted_iota(i32, (HALF, LANES), 1)
-    shifts = [(HALF - COL_STEP) * h for h in range(2)]
-    carried = [lane < column + shift for shift in shifts]
-    inside = [jnp.abs(lax.rem(lane, REACH) - column - shift) <= CYCLE for shift in shifts]
-    target = lax.broadcasted_iota(i32, (OFFS_PAD, RANGE), 1)
-    for i in range(0, BAND, 2):
-        for k in range(2):
-            moved = at + (i + k) * REACH
-            moved = jnp.where(moved >= RANGE, moved - RANGE, moved)
-            pick = jnp.where(target == jnp.where(at < 0, -1, moved), 1.0, 0.0).astype(bf16)
-            rows = [weights[(g * BAND + i + k) * SIDE : (g * BAND + i + k + 1) * SIDE, :OFFS_PAD] for g in range(bands)]
-            wide[k] = dot(jnp.concatenate(rows, axis=0).astype(bf16), pick)
+    at = own_ref[:OFFS_PAD, :1]
+    from_col = lax.broadcasted_iota(i32, (SIDE, LANES), 0) + own_ref[OFFS_PAD : OFFS_PAD + 1, :]
+    inside = (from_col >= 0) & (from_col < SIDE)
+    per = LANES // REACH
+    taken = wide.shape[2]
+    target = lax.broadcasted_iota(i32, (OFFS_PAD, taken), 1)
+    nothing = jnp.zeros((8, LANES), f32)
+    for b in range(per):
+        pick = jnp.where(target == jnp.where(at < 0, -1, at + b * REACH), 1.0, 0.0).astype(bf16)
+        for k in range(BAND // per):
+            rows = [weights[pl.ds((g * BAND + b + k * per) * SIDE, SIDE), :] for g in range(bands)]
+            rows = [jnp.where(inside, row, 0.0)[:, :OFFS_PAD].astype(bf16) for row in rows]
+            wide[k] = dot(jnp.concatenate(rows, axis=0), pick)
         for g in range(bands):
             for h in range(2):
                 start = g * SIDE + h * HALF
-                turned = [[pltpu.roll(wide[k, start : start + HALF, v * LANES : (v + 1) * LANES], shifts[h], 1,
-                                      stride=1, stride_axis=0) for v in range(blocks)] for k in range(2)]
+                shift = (h * (HALF - COL_STEP) - CYCLE) % LANES
+                turned = [[pltpu.roll(wide[k, start : start + HALF, v * LANES : (v + 1) * LANES], shift, 1,
+                                      stride=1, stride_axis=0) for v in range(taken // LANES)]
+                          for k in range(BAND // per)]
                 for v in range(blocks):
-                    pair = [jnp.where(inside[h], jnp.where(carried[h], turned[k][v - 1], turned[k][v]), 0.0)
-                            for k in range(2)]
-                    bands_ref[g, h, i * HALF : (i + 2) * HALF, v * LANES : (v + 1) * LANES] = jnp.concatenate(
-                        pair, axis=0).astype(bf16)
+                    for t in range(HALF // 8):
+                        pieces = [turned[k][v - k][t * 8 : (t + 1) * 8] if 0 <= v - k < taken // LANES else nothing
+                                  for k in range(BAND // per)]
+                        first = t * BAND * 8 + b * len(pieces) * 8
+                        bands_ref[g, h, first : first + len(pieces) * 8, v * LANES : (v + 1) * LANES] = (
+                            jnp.concatenate(pieces, axis=0).astype(bf16))
     for g in range(bands):
         edges = []
         for i in range(BAND):
@@ -166,7 +172,7 @@
         movies[g].start()
     for copy in small[:3]:
         copy.wait()
-    build_bands(tile, w_ref[...], own_ref[:, :1], beside_ref[...], bands_ref, sides_ref, weights, wide)
+    build_bands(tile, w_ref[...], own_ref, beside_ref[...], bands_ref, sides_ref, weights, wide)
     for copy in small[3:] + fps + movies:
         copy.wait()
     live = lax.broadcasted_iota(i32, (comps, 1), 0) < count
@@ -198,7 +204,10 @@
         for h in range(2):
             r = r_ref[first : first + high - low, h * COL_STEP : h * COL_STEP + REACH, :]
             x = dot(bands_ref[g, h, :, low * REACH : high * REACH], r.reshape((high - low) * REACH, frames))
-            halves.append(x.reshape(BAND, HALF, frames))
+            per = LANES // REACH
+            x = x.reshape(HALF // 8, per, BAND // per, 8, frames)
+            rows = [jnp.concatenate([x[t, i % per, i // per] for t in range(HALF // 8)], axis=0) for i in range(BAND)]
+            halves.append(jnp.stack(rows))
         rows = pl.ds(g * BAND, BAND)
         edge_ref[rows] = jnp.where(tile == 0, halves[1][:, HALF - CYCLE :], halves[0][:, :CYCLE])
         x_ref[rows] = jnp.concatenate(halves, axis=1).astype(bf16)
@@ -367,7 +376,7 @@
         scratch_shapes=[pltpu.VMEM((pixels, comps), bf16), pltpu.VMEM((comps, frames), bf16),
                         one_row, one_row, one_row, pltpu.VMEM(weights.shape, bf16), pltpu.VMEM(own.shape, i32),
                         pltpu.VMEM(beside.shape[1:], i32), pltpu.VMEM((pixels, LANES), f32),
-                        pltpu.VMEM((2, bands * SIDE, RANGE), f32), pltpu.SemaphoreType.DMA((2 * bands + 7,))],
+                        pltpu.VMEM((2, bands * SIDE, RANGE - LANES), f32), pltpu.SemaphoreType.DMA((2 * bands + 7,))],
         compiler_params=params(16),
     )(tile, comp_count, *inputs)
     banded = pl.pallas_call(

time: 49.2 us -> 48.4 us (0.984)
  Pallas kernels: 19.5 us -> 18.8 us
where the time goes in v6:
time: 48.4 us; the launch traced here: 48.2 us
  Pallas kernels  18.8 us (39%)
  blocking collectives  11.6 us (24%)
  waiting for transfers between devices  8.35 us (17%)
  starting transfers between devices  7.95 us (16%)
  between operations  1.4 us (3%)
    all_to_all x1, blocking collectives, shards(): lax.all_to_all(moved, 'tm', 0, 0, tiled=False).reshape(packed, comps)  11.6 us
    all_to_all x1, waiting for transfers between devices, shards(): lax.all_to_all(part.reshape(parts, block, comps), 'tm', 0, 0, tiled=False)  8.34 us
    all_to_all x1, starting transfers between devices, shards(): lax.all_to_all(part.reshape(parts, block, comps), 'tm', 0, 0, tiled=False)  7.3 us
    pallas_call x1, Pallas kernels, shards(): pl.pallas_call(functools.partial(last_kernel, block, share), out_shape=(s...  5.63 us
    pallas_call x1, Pallas kernels, shards(): pl.pallas_call(start_kernel, out_shape=(sds((pixels, comps), bf16), sds((...  4.49 us
    pallas_call x2, Pallas kernels, shards(): x, beyond = banded(tile, band_w, r)  3.61 us
    pallas_call x1, Pallas kernels, shards(): pl.pallas_call(pass_kernel, out_shape=(sds((comps, frames), bf16), r_shap...  2.91 us
    pallas_call x1, Pallas kernels, shards(): pl.pallas_call(unfold_kernel, out_shape=sds((pixels, comps), bf16), in_sp...  1.58 us
  transfers between devices with their start and end apart: 3, of which 1 were waited for; matrix products, arithmetic and copies ran while one was open for 0% of the time, Pallas kernels for 9%

profile of v6, /device:TPU:0, one launch (start us, length us, event | category | flops | bytes accessed | tf_op | source)
XLA Modules:
  0.0 48.2 jit_solution(3459310573729545090)
XLA Ops:
  1.3 4.5 %shard_map.122 = (bf16[2304,384]{1,0:T(8,128)(2,1)S(1)}, bf16[384,512]{1,0:T(8,128)(2,1)S(1)}, f32[384,128]{1,0:T(8,128)S(1)}, bf16[48,48,512]{2,1,0:T(8,128)(2,...) custom-call(s32[1]{0:T(128)} %bitcast.1.tile_ref, ...), custom_call_target="tpu_custom_call" | custom-call | tf_op jit(solution)/shard_map/pallas_call | solution.py:370
  5.8 0.5 %collective-permute-start = (bf16[384,512]{1,0:T(8,128)(2,1)S(1)}, bf16[384,512]{1,0:T(8,128)(2,1)S(1)}, u32[]{:S(2)}, u32[]{:S(2)}) collective-permute-start(bf16[384,512]{1,0:T(8,128)(2,1)S(1)} %get-tuple-element.20), channel_id=1, source_target_pairs={{0,1},{1,0},{2,3},{3,2},{4,5},{5,4},{6,7},{7,6},{8,9},{9,8},{10,11... | collective-permute-start | bytes 1179656 | tf_op jit(solution)/shard_map/ppermute | solution.py:344
  6.3 1.8 %shard_map.123 = (bf16[48,48,512]{2,1,0:T(8,128)(2,1)S(1)}, f32[48,8,512]{2,1,0:T(8,128)S(1)}) custom-call(s32[1]{0:T(128)} %bitcast.1.tile_ref, bf16[6,2,192,768]{3,2,1,0:T(8,128)(2,1)S(1)} %get-tuple-element.22.bands_ref, bf16[48,48,512]{2,1,0:T(8,128)(2,1)S(1)} %get-tuple-element.23.r_ref), custom_call_target="tpu_custom_call" | custom-call | flops 4000000000 | bytes 20000000 | tf_op jit(solution)/shard_map/pallas_call | solution.py:389
  8.1 0.0 collective-permute-done.halo_ref
  8.1 2.9 %shard_map.124 = (bf16[384,512]{1,0:T(8,128)(2,1)S(1)}, bf16[48,48,512]{2,1,0:T(8,128)(2,1)S(1)}, bf16[384,512]{1,0:T(8,128)(2,1)S(1)}) custom-call(s32[1]{0:T(128)} %bitcast.1.tile_ref, s32[1]{0:T(128)S(6)} %copy.13.count_ref, bf16[384,512]{1,0:T(8,128)(2,1)S(1)} %collective-permute-done.halo_ref, bf16[6,64,256]{2,1,0:T(8,128)(2,1)S(1)} %get-tuple-element.21.sides_ref, ...), custom_call_target="tpu_custom_call" | custom-call | tf_op jit(solution)/shard_map/pallas_call | solution.py:390
  11.1 0.1 collective-permute-start.1
  11.2 0.0 copy-start
  11.2 0.0 copy-start.1
  11.2 0.0 copy-start.2
  11.2 0.0 copy-start.3
  11.2 1.8 %shard_map.125 = (bf16[48,48,512]{2,1,0:T(8,128)(2,1)S(1)}, f32[48,8,512]{2,1,0:T(8,128)S(1)}) custom-call(s32[1]{0:T(128)} %bitcast.1.tile_ref, bf16[6,2,192,768]{3,2,1,0:T(8,128)(2,1)S(1)} %get-tuple-element.22.bands_ref, bf16[48,48,512]{2,1,0:T(8,128)(2,1)S(1)} %get-tuple-element.31.r_ref), custom_call_target="tpu_custom_call" | custom-call | flops 4000000000 | bytes 20000000 | tf_op jit(solution)/shard_map/pallas_call | solution.py:398
  13.0 0.0 collective-permute-done.1.halo_ref
  13.0 0.0 copy-done
  13.0 0.0 copy-done.1
  13.0 0.0 copy-done.2
  13.0 0.0 copy-done.3
  13.1 5.6 %shard_map.126 = (bf16[384,512]{1,0:T(8,128)(2,1)}, bf16[320,384]{1,0:T(8,128)(2,1)}, bf16[160,1152]{1,0:T(8,128)(2,1)S(1)}) custom-call(s32[1]{0:T(128)} %bitcast.1.tile_ref, s32[1]{0:T(128)S(6)} %copy.13.count_ref, bf16[384,512]{1,0:T(8,128)(2,1)S(1)} %collective-permute-done.1.halo_ref, bf16[6,64,256]{2,1,0:T(8,128)(2,1)S(1)} %get-tuple-element.21.sides_ref, ...), custom_call_target="tpu_custom_call" | custom-call | tf_op jit(solution)/shard_map/pallas_call | solution.py:399
  18.7 7.3 %all-to-all-start = ((bf16[8,40,384]{2,1,0:T(8,128)(2,1)}), bf16[8,40,384]{2,1,0:T(8,128)(2,1)S(1)}, u32[]{:S(2)}, u32[]{:S(2)}) async-start(bf16[8,40,384]{2,1,0:T(8,128)(2,1)} %bitcast.7), calls=%async_computation | async-start | bytes 491520 | tf_op jit(solution)/shard_map/all_to_all | solution.py:408
  26.0 0.6 %shard_map.127.ffold_ref = f32[320,384]{1,0:T(8,128)S(1)} custom-call(bf16[160,1152]{1,0:T(8,128)(2,1)S(1)} %get-tuple-element.36.fold_ref, bf16[2304,384]{1,0:T(8,128)(2,1)S(1)} %get-tuple-element.26.foot_ref), custom_call_target="tpu_custom_call" | custom-call | tf_op jit(solution)/shard_map/pallas_call | solution.py:409
  26.6 8.3 %all-to-all-done.parts_ref = bf16[8,40,384]{2,1,0:T(8,128)(2,1)S(1)} async-done(((bf16[8,40,384]{2,1,0:T(8,128)(2,1)}), bf16[8,40,384]{2,1,0:T(8,128)(2,1)S(1)}, u32[]{:S(2)}, u32[]{:S(2)}) %all-to-all-start) | async-done | bytes 245792 | tf_op jit(solution)/shard_map/all_to_all | solution.py:408
  34.9 0.1 shard_map.128
  35.0 11.6 %all_to_all.10 = bf16[8,40,384]{2,1,0:T(8,128)(2,1)S(1)} all-to-all(bf16[8,40,384]{2,1,0:T(8,128)(2,1)S(1)} %shard_map.128), channel_id=1, replica_groups=mesh['groups'=2,'tm'=8,'tile'=2] {'tm'}, dimensions={0} | all-to-all | bytes 491520 | tf_op jit(solution)/shard_map/all_to_all | solution.py:419
  46.6 1.6 %shard_map.129 = bf16[2304,384]{1,0:T(8,128)(2,1)} custom-call(s32[1]{0:T(128)S(6)} %copy.13.count_ref, bf16[320,384]{1,0:T(8,128)(2,1)S(1)} %bitcast.12, bf16[160,1152]{1,0:T(8,128)(2,1)S(1)} %get-tuple-element.36.fold_ref, s32[1,384]{1,0:T(1,128)S(1)} %copy-done, s32[1,384]{1,0:T(1,128)S(1)} %copy-done.1, s32[1,384]{1,0:T(1,128)S(1)} %copy-done.2), custom_call_target="tpu_custom_call" | custom-call | tf_op jit(solution)/shard_map/pallas_call | solution.py:420
Async XLA Ops:
  5.8 2.4 %collective-permute-start = (bf16[384,512]{1,0:T(8,128)(2,1)S(1)}, bf16[384,512]{1,0:T(8,128)(2,1)S(1)}, u32[]{:S(2)}, u32[]{:S(2)}) collective-permute-start(bf16[384,512]{1,0:T(8,128)(2,1)S(1)} %get-tuple-element.20), channel_id=1, source_target_pairs={{0,1},{1,0},{2,3},{3,2},{4,5},{5,4},{6,7},{7,6},{8,9},{9,8},{10,11... | collective-permute-start | bytes 1179656 | tf_op jit(solution)/shard_map/ppermute | solution.py:344
  11.1 1.9 %collective-permute-start.1 = (bf16[384,512]{1,0:T(8,128)(2,1)S(1)}, bf16[384,512]{1,0:T(8,128)(2,1)S(1)}, u32[]{:S(2)}, u32[]{:S(2)}) collective-permute-start(bf16[384,512]{1,0:T(8,128)(2,1)S(1)} %get-tuple-element.30), channel_id=1, source_target_pairs={{0,1},{1,0},{2,3},{3,2},{4,5},{5,4},{6,7},{7,6},{8,9},{9,8},{10,11... | collective-permute-start | bytes 1179656 | tf_op jit(solution)/shard_map/ppermute | solution.py:344
  11.2 1.9 %copy-start = (s32[1,384]{1,0:T(1,128)S(1)}, s32[1,384]{1,0:T(1,128)}, u32[]{:S(2)}) copy-start(s32[1,384]{1,0:T(1,128)} %cr_ref.3) | copy-start | bytes 4612
  11.2 1.9 %copy-start.1 = (s32[1,384]{1,0:T(1,128)S(1)}, s32[1,384]{1,0:T(1,128)}, u32[]{:S(2)}) copy-start(s32[1,384]{1,0:T(1,128)} %cc_ref.3) | copy-start | bytes 4612
  11.2 1.9 %copy-start.2 = (s32[1,384]{1,0:T(1,128)S(1)}, s32[1,384]{1,0:T(1,128)}, u32[]{:S(2)}) copy-start(s32[1,384]{1,0:T(1,128)} %rad_ref.3) | copy-start | bytes 4612
  11.2 1.9 %copy-start.3 = (s32[1,1152]{1,0:T(1,128)S(1)}, s32[1,1152]{1,0:T(1,128)}, u32[]{:S(2)}) copy-start(s32[1,1152]{1,0:T(1,128)} %constant.16.clone.slot_ref) | copy-start | bytes 13828
  18.7 16.2 %all-to-all-start = ((bf16[8,40,384]{2,1,0:T(8,128)(2,1)}), bf16[8,40,384]{2,1,0:T(8,128)(2,1)S(1)}, u32[]{:S(2)}, u32[]{:S(2)}) async-start(bf16[8,40,384]{2,1,0:T(8,128)(2,1)} %bitcast.7), calls=%async_computation | async-start | bytes 491520 | tf_op jit(solution)/shard_map/all_to_all | solution.py:408

commit v7 on v6

--- a/solution.py
+++ b/solution.py
@@ -16,6 +16,7 @@
 BAND = 8
 LANES = 128
 OFFS_PAD = 64
+GROUP = 256
 HALF = SIDE // 2
 REACH = HALF + CYCLE
 COL_STEP = SIDE - REACH
@@ -157,23 +158,20 @@
     comps = tr_ref.shape[0]
     band = BAND * SIDE
     bands = SIDE // BAND
-    small = [pltpu.make_async_copy(src, dst, sems.at[2 * bands + n]) for n, (src, dst) in enumerate(
+    small = [pltpu.make_async_copy(src, dst, sems.at[n]) for n, (src, dst) in enumerate(
         ((w_hbm, w_ref), (own_hbm, own_ref), (beside_hbm.at[tile], beside_ref),
          (cr_hbm, cr_ref), (cc_hbm, cc_ref), (rad_hbm, rad_ref), (tr_hbm, tr_ref)))]
-    fps, movies = [], []
-    for g in range(bands):
-        rows = pl.ds(g * band, band)
-        fps.append(pltpu.make_async_copy(fp_hbm.at[rows, :], fp_ref.at[rows, :], sems.at[g]))
-        movies.append(pltpu.make_async_copy(movie_hbm.at[rows, :], movie_ref.at[rows, :], sems.at[bands + g]))
-    for copy in small:
+    large = [pltpu.make_async_copy(fp_hbm, fp_ref, sems.at[len(small)])]
+    half = movie_ref.shape[0] // 2
+    for h in range(2):
+        rows = pl.ds(h * half, half)
+        large.append(pltpu.make_async_copy(movie_hbm.at[rows, :], movie_ref.at[rows, :], sems.at[len(small) + 1 + h]))
+    for copy in small + large:
         copy.start()
-    for g in range(bands):
-        fps[g].start()
-        movies[g].start()
     for copy in small[:3]:
         copy.wait()
     build_bands(tile, w_ref[...], own_ref, beside_ref[...], bands_ref, sides_ref, weights, wide)
-    for copy in small[3:] + fps + movies:
+    for copy in small[3:] + large[:2]:
         copy.wait()
     live = lax.broadcasted_iota(i32, (comps, 1), 0) < count
     trace = jnp.where(live, tr_ref[...].astype(f32), 0.0).astype(bf16)
@@ -182,6 +180,8 @@
     cr, rad = cr_ref[...], rad_ref[...]
     total = jnp.zeros((8, comps), f32)
     for g in range(bands):
+        if g == bands // 2:
+            large[2].wait()
         for i in range(BAND):
             row = g * BAND + i
             keep = gap_sq <= disc_limit(cr, rad, count, row)
@@ -234,18 +234,22 @@
         if back_ref is not None:
             back_ref[rows] = back.astype(bf16)
         err[pl.ds(g * band, band), :] = (back - r_ref[rows].astype(f32)).reshape(band, frames).astype(bf16)
-    grad = lax.dot_general(foot_ref[...], err[...], (((0,), (0,)), ((), ())), preferred_element_type=f32)
-    comps = grad.shape[0]
-    live = lax.broadcasted_iota(i32, (comps, 1), 0) < count
-    moved = jnp.maximum(trace_ref[...].astype(f32) - grad * den_ref[:, :1], 0.0)
-    return jnp.where(live, moved, 0.0)
+    comps = trace_ref.shape[0]
+    moved = []
+    for low in range(0, comps, GROUP):
+        some = slice(low, min(low + GROUP, comps))
+        grad = lax.dot_general(foot_ref[:, some], err[...], (((0,), (0,)), ((), ())), preferred_element_type=f32)
+        live = lax.broadcasted_iota(i32, (grad.shape[0], 1), 0) < count - low
+        new = jnp.maximum(trace_ref[some, :].astype(f32) - grad * den_ref[some, :1], 0.0)
+        moved.append(jnp.where(live, new, 0.0).astype(bf16))
+    return jnp.concatenate(moved, axis=0)
 
 
 def pass_kernel(tile_ref, count_ref, halo_ref, sides_ref, x_ref, edge_ref, r_ref, foot_ref, trace_ref, den_ref,
                 movie_ref, new_trace_ref, new_r_ref, pay_ref, wide_halo, err):
     tile, count = tile_ref[0], count_ref[0]
     trace = trace_step(tile, count, halo_ref, sides_ref, x_ref, edge_ref, r_ref, foot_ref, trace_ref, den_ref,
-                       wide_halo, err).astype(bf16)
+                       wide_halo, err)
     new_trace_ref[...] = trace
     for g in range(SIDE // BAND):
         resid_band(g, tile, movie_ref, foot_ref[pl.ds(g * BAND * SIDE, BAND * SIDE), :], trace,
@@ -257,7 +261,7 @@
                 trace_hbm, part_hbm, fold_ref, wide_halo, err, back, masked, new_trace, part_ref, sems):
     tile, count = tile_ref[0], count_ref[0]
     trace = trace_step(tile, count, halo_ref, sides_ref, x_ref, edge_ref, r_ref, foot_ref, trace_ref, den_ref,
-                       wide_halo, err, back).astype(bf16)
+                       wide_halo, err, back)
     new_trace[...] = trace
     stores = [pltpu.make_async_copy(new_trace, trace_hbm, sems.at[2])]
     stores[0].start()
@@ -376,7 +380,7 @@
         scratch_shapes=[pltpu.VMEM((pixels, comps), bf16), pltpu.VMEM((comps, frames), bf16),
                         one_row, one_row, one_row, pltpu.VMEM(weights.shape, bf16), pltpu.VMEM(own.shape, i32),
                         pltpu.VMEM(beside.shape[1:], i32), pltpu.VMEM((pixels, LANES), f32),
-                        pltpu.VMEM((2, bands * SIDE, RANGE - LANES), f32), pltpu.SemaphoreType.DMA((2 * bands + 7,))],
+                        pltpu.VMEM((2, bands * SIDE, RANGE - LANES), f32), pltpu.SemaphoreType.DMA((10,))],
         compiler_params=params(16),
     )(tile, comp_count, *inputs)
     banded = pl.pallas_call(

time: 48.4 us -> 48.3 us (level)
  no operation moved by 1% of the time
where the time goes in v7:
time: 48.3 us; the launch traced here: 48.1 us
  Pallas kernels  18.8 us (39%)
  blocking collectives  11.6 us (24%)
  waiting for transfers between devices  8.33 us (17%)
  starting transfers between devices  7.94 us (16%)
  between operations  1.39 us (3%)
    all_to_all x1, blocking collectives, shards(): lax.all_to_all(moved, 'tm', 0, 0, tiled=False).reshape(packed, comps)  11.6 us
    all_to_all x1, waiting for transfers between devices, shards(): lax.all_to_all(part.reshape(parts, block, comps), 'tm', 0, 0, tiled=False)  8.33 us
    all_to_all x1, starting transfers between devices, shards(): lax.all_to_all(part.reshape(parts, block, comps), 'tm', 0, 0, tiled=False)  7.3 us
    pallas_call x1, Pallas kernels, shards(): pl.pallas_call(functools.partial(last_kernel, block, share), out_shape=(s...  5.57 us
    pallas_call x1, Pallas kernels, shards(): pl.pallas_call(start_kernel, out_shape=(sds((pixels, comps), bf16), sds((...  4.54 us
    pallas_call x2, Pallas kernels, shards(): x, beyond = banded(tile, band_w, r)  3.62 us
    pallas_call x1, Pallas kernels, shards(): pl.pallas_call(pass_kernel, out_shape=(sds((comps, frames), bf16), r_shap...  2.83 us
    pallas_call x1, Pallas kernels, shards(): pl.pallas_call(unfold_kernel, out_shape=sds((pixels, comps), bf16), in_sp...  1.58 us
  transfers between devices with their start and end apart: 3, of which 1 were waited for; matrix products, arithmetic and copies ran while one was open for 0% of the time, Pallas kernels for 9%

profile of v7, /device:TPU:0, one launch (start us, length us, event | category | flops | bytes accessed | tf_op | source)
XLA Modules:
  0.0 48.1 jit_solution(4675628550176270130)
XLA Ops:
  1.3 4.5 %shard_map.122 = (bf16[2304,384]{1,0:T(8,128)(2,1)S(1)}, bf16[384,512]{1,0:T(8,128)(2,1)S(1)}, f32[384,128]{1,0:T(8,128)S(1)}, bf16[48,48,512]{2,1,0:T(8,128)(2,...) custom-call(s32[1]{0:T(128)} %bitcast.1.tile_ref, ...), custom_call_target="tpu_custom_call" | custom-call | tf_op jit(solution)/shard_map/pallas_call | solution.py:374
  5.8 0.5 %collective-permute-start = (bf16[384,512]{1,0:T(8,128)(2,1)S(1)}, bf16[384,512]{1,0:T(8,128)(2,1)S(1)}, u32[]{:S(2)}, u32[]{:S(2)}) collective-permute-start(bf16[384,512]{1,0:T(8,128)(2,1)S(1)} %get-tuple-element.20), channel_id=1, source_target_pairs={{0,1},{1,0},{2,3},{3,2},{4,5},{5,4},{6,7},{7,6},{8,9},{9,8},{10,11... | collective-permute-start | bytes 1179656 | tf_op jit(solution)/shard_map/ppermute | solution.py:348
  6.4 1.8 %shard_map.123 = (bf16[48,48,512]{2,1,0:T(8,128)(2,1)S(1)}, f32[48,8,512]{2,1,0:T(8,128)S(1)}) custom-call(s32[1]{0:T(128)} %bitcast.1.tile_ref, bf16[6,2,192,768]{3,2,1,0:T(8,128)(2,1)S(1)} %get-tuple-element.22.bands_ref, bf16[48,48,512]{2,1,0:T(8,128)(2,1)S(1)} %get-tuple-element.23.r_ref), custom_call_target="tpu_custom_call" | custom-call | flops 4000000000 | bytes 20000000 | tf_op jit(solution)/shard_map/pallas_call | solution.py:393
  8.2 0.0 collective-permute-done.halo_ref
  8.2 2.8 %shard_map.124 = (bf16[384,512]{1,0:T(8,128)(2,1)S(1)}, bf16[48,48,512]{2,1,0:T(8,128)(2,1)S(1)}, bf16[384,512]{1,0:T(8,128)(2,1)S(1)}) custom-call(s32[1]{0:T(128)} %bitcast.1.tile_ref, s32[1]{0:T(128)S(6)} %copy.13.count_ref, bf16[384,512]{1,0:T(8,128)(2,1)S(1)} %collective-permute-done.halo_ref, bf16[6,64,256]{2,1,0:T(8,128)(2,1)S(1)} %get-tuple-element.21.sides_ref, ...), custom_call_target="tpu_custom_call" | custom-call | tf_op jit(solution)/shard_map/pallas_call | solution.py:394
  11.0 0.1 collective-permute-start.1
  11.1 0.0 copy-start
  11.1 0.0 copy-start.1
  11.1 0.0 copy-start.2
  11.1 0.0 copy-start.3
  11.2 1.8 %shard_map.125 = (bf16[48,48,512]{2,1,0:T(8,128)(2,1)S(1)}, f32[48,8,512]{2,1,0:T(8,128)S(1)}) custom-call(s32[1]{0:T(128)} %bitcast.1.tile_ref, bf16[6,2,192,768]{3,2,1,0:T(8,128)(2,1)S(1)} %get-tuple-element.22.bands_ref, bf16[48,48,512]{2,1,0:T(8,128)(2,1)S(1)} %get-tuple-element.31.r_ref), custom_call_target="tpu_custom_call" | custom-call | flops 4000000000 | bytes 20000000 | tf_op jit(solution)/shard_map/pallas_call | solution.py:402
  13.0 0.0 collective-permute-done.1.halo_ref
  13.0 0.0 copy-done
  13.0 0.0 copy-done.1
  13.0 0.0 copy-done.2
  13.0 0.0 copy-done.3
  13.0 5.6 %shard_map.126 = (bf16[384,512]{1,0:T(8,128)(2,1)}, bf16[320,384]{1,0:T(8,128)(2,1)}, bf16[160,1152]{1,0:T(8,128)(2,1)S(1)}) custom-call(s32[1]{0:T(128)} %bitcast.1.tile_ref, s32[1]{0:T(128)S(6)} %copy.13.count_ref, bf16[384,512]{1,0:T(8,128)(2,1)S(1)} %collective-permute-done.1.halo_ref, bf16[6,64,256]{2,1,0:T(8,128)(2,1)S(1)} %get-tuple-element.21.sides_ref, ...), custom_call_target="tpu_custom_call" | custom-call | tf_op jit(solution)/shard_map/pallas_call | solution.py:403
  18.6 7.3 %all-to-all-start = ((bf16[8,40,384]{2,1,0:T(8,128)(2,1)}), bf16[8,40,384]{2,1,0:T(8,128)(2,1)S(1)}, u32[]{:S(2)}, u32[]{:S(2)}) async-start(bf16[8,40,384]{2,1,0:T(8,128)(2,1)} %bitcast.7), calls=%async_computation | async-start | bytes 491520 | tf_op jit(solution)/shard_map/all_to_all | solution.py:412
  25.9 0.6 %shard_map.127.ffold_ref = f32[320,384]{1,0:T(8,128)S(1)} custom-call(bf16[160,1152]{1,0:T(8,128)(2,1)S(1)} %get-tuple-element.36.fold_ref, bf16[2304,384]{1,0:T(8,128)(2,1)S(1)} %get-tuple-element.26.foot_ref), custom_call_target="tpu_custom_call" | custom-call | tf_op jit(solution)/shard_map/pallas_call | solution.py:413
  26.5 8.3 %all-to-all-done.parts_ref = bf16[8,40,384]{2,1,0:T(8,128)(2,1)S(1)} async-done(((bf16[8,40,384]{2,1,0:T(8,128)(2,1)}), bf16[8,40,384]{2,1,0:T(8,128)(2,1)S(1)}, u32[]{:S(2)}, u32[]{:S(2)}) %all-to-all-start) | async-done | bytes 245792 | tf_op jit(solution)/shard_map/all_to_all | solution.py:412
  34.8 0.1 shard_map.128
  34.9 11.6 %all_to_all.10 = bf16[8,40,384]{2,1,0:T(8,128)(2,1)S(1)} all-to-all(bf16[8,40,384]{2,1,0:T(8,128)(2,1)S(1)} %shard_map.128), channel_id=1, replica_groups=mesh['groups'=2,'tm'=8,'tile'=2] {'tm'}, dimensions={0} | all-to-all | bytes 491520 | tf_op jit(solution)/shard_map/all_to_all | solution.py:423
  46.5 1.6 %shard_map.129 = bf16[2304,384]{1,0:T(8,128)(2,1)} custom-call(s32[1]{0:T(128)S(6)} %copy.13.count_ref, bf16[320,384]{1,0:T(8,128)(2,1)S(1)} %bitcast.12, bf16[160,1152]{1,0:T(8,128)(2,1)S(1)} %get-tuple-element.36.fold_ref, s32[1,384]{1,0:T(1,128)S(1)} %copy-done, s32[1,384]{1,0:T(1,128)S(1)} %copy-done.1, s32[1,384]{1,0:T(1,128)S(1)} %copy-done.2), custom_call_target="tpu_custom_call" | custom-call | tf_op jit(solution)/shard_map/pallas_call | solution.py:424
Async XLA Ops:
  5.8 2.4 %collective-permute-start = (bf16[384,512]{1,0:T(8,128)(2,1)S(1)}, bf16[384,512]{1,0:T(8,128)(2,1)S(1)}, u32[]{:S(2)}, u32[]{:S(2)}) collective-permute-start(bf16[384,512]{1,0:T(8,128)(2,1)S(1)} %get-tuple-element.20), channel_id=1, source_target_pairs={{0,1},{1,0},{2,3},{3,2},{4,5},{5,4},{6,7},{7,6},{8,9},{9,8},{10,11... | collective-permute-start | bytes 1179656 | tf_op jit(solution)/shard_map/ppermute | solution.py:348
  11.0 1.9 %collective-permute-start.1 = (bf16[384,512]{1,0:T(8,128)(2,1)S(1)}, bf16[384,512]{1,0:T(8,128)(2,1)S(1)}, u32[]{:S(2)}, u32[]{:S(2)}) collective-permute-start(bf16[384,512]{1,0:T(8,128)(2,1)S(1)} %get-tuple-element.30), channel_id=1, source_target_pairs={{0,1},{1,0},{2,3},{3,2},{4,5},{5,4},{6,7},{7,6},{8,9},{9,8},{10,11... | collective-permute-start | bytes 1179656 | tf_op jit(solution)/shard_map/ppermute | solution.py:348
  11.1 1.9 %copy-start = (s32[1,384]{1,0:T(1,128)S(1)}, s32[1,384]{1,0:T(1,128)}, u32[]{:S(2)}) copy-start(s32[1,384]{1,0:T(1,128)} %cr_ref.3) | copy-start | bytes 4612
  11.1 1.9 %copy-start.1 = (s32[1,384]{1,0:T(1,128)S(1)}, s32[1,384]{1,0:T(1,128)}, u32[]{:S(2)}) copy-start(s32[1,384]{1,0:T(1,128)} %cc_ref.3) | copy-start | bytes 4612
  11.1 1.9 %copy-start.2 = (s32[1,384]{1,0:T(1,128)S(1)}, s32[1,384]{1,0:T(1,128)}, u32[]{:S(2)}) copy-start(s32[1,384]{1,0:T(1,128)} %rad_ref.3) | copy-start | bytes 4612
  11.1 1.9 %copy-start.3 = (s32[1,1152]{1,0:T(1,128)S(1)}, s32[1,1152]{1,0:T(1,128)}, u32[]{:S(2)}) copy-start(s32[1,1152]{1,0:T(1,128)} %constant.16.clone.slot_ref) | copy-start | bytes 13828
  18.6 16.2 %all-to-all-start = ((bf16[8,40,384]{2,1,0:T(8,128)(2,1)}), bf16[8,40,384]{2,1,0:T(8,128)(2,1)S(1)}, u32[]{:S(2)}, u32[]{:S(2)}) async-start(bf16[8,40,384]{2,1,0:T(8,128)(2,1)} %bitcast.7), calls=%async_computation | async-start | bytes 491520 | tf_op jit(solution)/shard_map/all_to_all | solution.py:412

commit v8 on v6

--- a/solution.py
+++ b/solution.py
@@ -16,6 +16,7 @@
 BAND = 8
 LANES = 128
 OFFS_PAD = 64
+TALL = 2
 HALF = SIDE // 2
 REACH = HALF + CYCLE
 COL_STEP = SIDE - REACH
@@ -45,11 +46,11 @@
     none = len(offsets)
     own = np.full((OFFS_PAD + 8, LANES), -1, np.int32)
     own[OFFS_PAD] = SIDE
-    beside = np.full((2, BAND, CYCLE, 32, CYCLE), none, np.int32)
+    beside = np.full((2, TALL * BAND, CYCLE, TALL * BAND + 2 * CYCLE, CYCLE), none, np.int32)
     for o, (dy, dx) in enumerate(offsets):
         own[o] = (CYCLE + dy) * REACH + dx + CYCLE
         own[OFFS_PAD, o] = dx
-        for i in range(BAND):
+        for i in range(TALL * BAND):
             for q in range(CYCLE):
                 h = q + dx - CYCLE
                 if 0 <= h < CYCLE:
@@ -57,7 +58,7 @@
                 h = q + dx + CYCLE
                 if 0 <= h < CYCLE:
                     beside[1, i, q, i + CYCLE + dy, h] = o
-    return own, beside.reshape(2, BAND * CYCLE, 32 * CYCLE)
+    return own, beside.reshape(2, TALL * BAND * CYCLE, -1)
 
 
 def fold_rows(parts):
@@ -94,13 +95,14 @@
     return gap * gap
 
 
-def resid_band(g, tile, movie_ref, foot, trace, r_ref, pay_ref):
-    band = BAND * SIDE
-    d = movie_ref[pl.ds(g * band, band), :].astype(f32) - dot(foot, trace)
-    d3 = d.reshape(BAND, SIDE, d.shape[1])
-    r_ref[pl.ds(g * BAND, BAND)] = d3.astype(bf16)
+def resid_bands(g, tile, movie_ref, foot_ref, trace, r_ref, pay_ref):
+    rows, wide = pl.ds(g * BAND, TALL * BAND), pl.ds(g * BAND * SIDE, TALL * BAND * SIDE)
+    d = movie_ref[wide, :].astype(f32) - dot(foot_ref[wide, :], trace)
+    d3 = d.reshape(TALL * BAND, SIDE, d.shape[1])
+    r_ref[rows] = d3.astype(bf16)
     edge = jnp.where(tile == 0, d3[:, SIDE - CYCLE :], d3[:, :CYCLE])
-    pay_ref[pl.ds(g * BAND * CYCLE, BAND * CYCLE), :] = edge.reshape(BAND * CYCLE, d.shape[1]).astype(bf16)
+    edge = edge.reshape(TALL * BAND * CYCLE, d.shape[1]).astype(bf16)
+    pay_ref[pl.ds(g * BAND * CYCLE, TALL * BAND * CYCLE), :] = edge
 
 
 def build_bands(tile, w, own_ref, beside, bands_ref, sides_ref, weights, wide):
@@ -137,14 +139,14 @@
                         first = t * BAND * 8 + b * len(pieces) * 8
                         bands_ref[g, h, first : first + len(pieces) * 8, v * LANES : (v + 1) * LANES] = (
                             jnp.concatenate(pieces, axis=0).astype(bf16))
-    for g in range(bands):
+    for g in range(bands // TALL):
         edges = []
-        for i in range(BAND):
-            base = (g * BAND + i) * SIDE
+        for i in range(TALL * BAND):
+            base = (g * TALL * BAND + i) * SIDE
             edges.append(jnp.where(tile == 0, weights[base + SIDE - CYCLE : base + SIDE, :],
                                    weights[base : base + CYCLE, :]))
         edge = jnp.concatenate(edges, axis=0)
-        for v in range(2):
+        for v in range(beside.shape[1] // LANES):
             lanes = slice(v * LANES, (v + 1) * LANES)
             sides_ref[g, :, lanes] = jnp.take_along_axis(edge, beside[:, lanes], axis=1).astype(bf16)
 
@@ -188,7 +190,8 @@
             foot = jnp.where(keep, fp_ref[pl.ds(row * SIDE, SIDE), :].astype(f32), 0.0)
             foot_ref[pl.ds(row * SIDE, SIDE), :] = foot.astype(bf16)
             total = total + jnp.sum((foot * foot).reshape(SIDE // 8, 8, comps), axis=0)
-        resid_band(g, tile, movie_ref, foot_ref[pl.ds(g * band, band), :], trace, r_ref, pay_ref)
+        if g % TALL == TALL - 1:
+            resid_bands(g + 1 - TALL, tile, movie_ref, foot_ref, trace, r_ref, pay_ref)
     energy = jnp.sum(total, axis=0, keepdims=True) + RIDGE
     den_ref[...] = jnp.transpose(jnp.broadcast_to(1.0 / energy, (LANES, comps)))
 
@@ -216,16 +219,17 @@
 def trace_step(tile, count, halo_ref, sides_ref, x_ref, edge_ref, r_ref, foot_ref, trace_ref, den_ref,
                wide_halo, err, back_ref=None):
     frames = x_ref.shape[2]
-    band, edge = BAND * SIDE, CYCLE * SIDE
+    edge = CYCLE * SIDE
     pad = CYCLE * CYCLE
     wide_halo[:pad, :] = jnp.zeros((pad, frames), bf16)
     wide_halo[pl.ds(pad, edge), :] = halo_ref[...]
     tail = wide_halo.shape[0] - pad - edge
     wide_halo[pl.ds(pad + edge, tail), :] = jnp.zeros((tail, frames), bf16)
-    for g in range(SIDE // BAND):
-        rows = pl.ds(g * BAND, BAND)
+    tall = TALL * BAND
+    for g in range(SIDE // tall):
+        rows = pl.ds(g * tall, tall)
         reach = sides_ref.shape[2]
-        side = dot(sides_ref[g], wide_halo[pl.ds(g * BAND * CYCLE, reach), :]).reshape(BAND, CYCLE, frames)
+        side = dot(sides_ref[g], wide_halo[pl.ds(g * tall * CYCLE, reach), :]).reshape(tall, CYCLE, frames)
         side = (edge_ref[rows] + side).astype(bf16).astype(f32)
         x = x_ref[rows].astype(f32)
         left = jnp.where(tile == 0, x[:, :CYCLE], side)
@@ -233,7 +237,8 @@
         back = jnp.concatenate([left, x[:, CYCLE : SIDE - CYCLE], right], axis=1)
         if back_ref is not None:
             back_ref[rows] = back.astype(bf16)
-        err[pl.ds(g * band, band), :] = (back - r_ref[rows].astype(f32)).reshape(band, frames).astype(bf16)
+        wide = (back - r_ref[rows].astype(f32)).reshape(tall * SIDE, frames)
+        err[pl.ds(g * tall * SIDE, tall * SIDE), :] = wide.astype(bf16)
     grad = lax.dot_general(foot_ref[...], err[...], (((0,), (0,)), ((), ())), preferred_element_type=f32)
     comps = grad.shape[0]
     live = lax.broadcasted_iota(i32, (comps, 1), 0) < count
@@ -247,9 +252,8 @@
     trace = trace_step(tile, count, halo_ref, sides_ref, x_ref, edge_ref, r_ref, foot_ref, trace_ref, den_ref,
                        wide_halo, err).astype(bf16)
     new_trace_ref[...] = trace
-    for g in range(SIDE // BAND):
-        resid_band(g, tile, movie_ref, foot_ref[pl.ds(g * BAND * SIDE, BAND * SIDE), :], trace,
-                   new_r_ref, pay_ref)
+    for g in range(0, SIDE // BAND, TALL):
+        resid_bands(g, tile, movie_ref, foot_ref, trace, new_r_ref, pay_ref)
 
 
 def last_kernel(block, share, tile_ref, count_ref, halo_ref, sides_ref, x_ref, edge_ref, r_ref, foot_ref, trace_ref,
@@ -360,7 +364,7 @@
     slots, share, block = fold_rows(parts)
     packed = parts * block
     sds = jax.ShapeDtypeStruct
-    halo_pad = pltpu.VMEM((edge + 3 * CYCLE * CYCLE, frames), bf16)
+    halo_pad = pltpu.VMEM((edge + 2 * CYCLE * CYCLE, frames), bf16)
     err_buf = pltpu.VMEM((pixels, frames), bf16)
     one_row = pltpu.VMEM((1, comps), i32)
 
@@ -371,7 +375,7 @@
         start_kernel,
         out_shape=(sds((pixels, comps), bf16), sds((comps, frames), bf16), sds((comps, LANES), f32),
                    r_shape, sds((edge, frames), bf16), sds((pixels, frames), bf16),
-                   sds((bands, 2, BAND * HALF, RANGE), bf16), sds((bands, CYCLE * BAND, beside.shape[2]), bf16)),
+                   sds((bands, 2, BAND * HALF, RANGE), bf16), sds((bands // TALL,) + beside.shape[1:], bf16)),
         in_specs=[SM, SM] + [HB] * 9, out_specs=[VM] * 8,
         scratch_shapes=[pltpu.VMEM((pixels, comps), bf16), pltpu.VMEM((comps, frames), bf16),
                         one_row, one_row, one_row, pltpu.VMEM(weights.shape, bf16), pltpu.VMEM(own.shape, i32),

time: 48.4 us -> 48.2 us (level)
  no operation moved by 1% of the time
where the time goes in v8:
time: 48.2 us; the launch traced here: 47.9 us
  Pallas kernels  18.6 us (39%)
  blocking collectives  11.6 us (24%)
  waiting for transfers between devices  8.34 us (17%)
  starting transfers between devices  7.91 us (16%)
  between operations  1.41 us (3%)
    all_to_all x1, blocking collectives, shards(): lax.all_to_all(moved, 'tm', 0, 0, tiled=False).reshape(packed, comps)  11.6 us
    all_to_all x1, waiting for transfers between devices, shards(): lax.all_to_all(part.reshape(parts, block, comps), 'tm', 0, 0, tiled=False)  8.33 us
    all_to_all x1, starting transfers between devices, shards(): lax.all_to_all(part.reshape(parts, block, comps), 'tm', 0, 0, tiled=False)  7.27 us
    pallas_call x1, Pallas kernels, shards(): pl.pallas_call(functools.partial(last_kernel, block, share), out_shape=(s...  5.52 us
    pallas_call x1, Pallas kernels, shards(): pl.pallas_call(start_kernel, out_shape=(sds((pixels, comps), bf16), sds((...  4.48 us
    pallas_call x2, Pallas kernels, shards(): x, beyond = banded(tile, band_w, r)  3.62 us
    pallas_call x1, Pallas kernels, shards(): pl.pallas_call(pass_kernel, out_shape=(sds((comps, frames), bf16), r_shap...  2.83 us
    pallas_call x1, Pallas kernels, shards(): pl.pallas_call(unfold_kernel, out_shape=sds((pixels, comps), bf16), in_sp...  1.58 us
  transfers between devices with their start and end apart: 3, of which 1 were waited for; matrix products, arithmetic and copies ran while one was open for 0% of the time, Pallas kernels for 9%

profile of v8, /device:TPU:0, one launch (start us, length us, event | category | flops | bytes accessed | tf_op | source)
XLA Modules:
  0.0 47.9 jit_solution(2149207847254800287)
XLA Ops:
  1.3 4.5 %shard_map.122 = (bf16[2304,384]{1,0:T(8,128)(2,1)S(1)}, bf16[384,512]{1,0:T(8,128)(2,1)S(1)}, f32[384,128]{1,0:T(8,128)S(1)}, bf16[48,48,512]{2,1,0:T(8,128)(2,...) custom-call(s32[1]{0:T(128)} %bitcast.1.tile_ref, ...), custom_call_target="tpu_custom_call" | custom-call | tf_op jit(solution)/shard_map/pallas_call | solution.py:374
  5.8 0.6 %collective-permute-start = (bf16[384,512]{1,0:T(8,128)(2,1)S(1)}, bf16[384,512]{1,0:T(8,128)(2,1)S(1)}, u32[]{:S(2)}, u32[]{:S(2)}) collective-permute-start(bf16[384,512]{1,0:T(8,128)(2,1)S(1)} %get-tuple-element.20), channel_id=1, source_target_pairs={{0,1},{1,0},{2,3},{3,2},{4,5},{5,4},{6,7},{7,6},{8,9},{9,8},{10,11... | collective-permute-start | bytes 1179656 | tf_op jit(solution)/shard_map/ppermute | solution.py:348
  6.3 1.8 %shard_map.123 = (bf16[48,48,512]{2,1,0:T(8,128)(2,1)S(1)}, f32[48,8,512]{2,1,0:T(8,128)S(1)}) custom-call(s32[1]{0:T(128)} %bitcast.1.tile_ref, bf16[6,2,192,768]{3,2,1,0:T(8,128)(2,1)S(1)} %get-tuple-element.22.bands_ref, bf16[48,48,512]{2,1,0:T(8,128)(2,1)S(1)} %get-tuple-element.23.r_ref), custom_call_target="tpu_custom_call" | custom-call | flops 4000000000 | bytes 20000000 | tf_op jit(solution)/shard_map/pallas_call | solution.py:393
  8.1 0.0 collective-permute-done.halo_ref
  8.1 2.8 %shard_map.124 = (bf16[384,512]{1,0:T(8,128)(2,1)S(1)}, bf16[48,48,512]{2,1,0:T(8,128)(2,1)S(1)}, bf16[384,512]{1,0:T(8,128)(2,1)S(1)}) custom-call(s32[1]{0:T(128)} %bitcast.1.tile_ref, s32[1]{0:T(128)S(6)} %copy.13.count_ref, bf16[384,512]{1,0:T(8,128)(2,1)S(1)} %collective-permute-done.halo_ref, bf16[3,128,256]{2,1,0:T(8,128)(2,1)S(1)} %get-tuple-element.21.sides_ref, ...), custom_call_target="tpu_custom_call" | custom-call | tf_op jit(solution)/shard_map/pallas_call | solution.py:394
  11.0 0.1 collective-permute-start.1
  11.1 0.0 copy-start
  11.1 0.0 copy-start.1
  11.1 0.0 copy-start.2
  11.1 0.0 copy-start.3
  11.1 1.8 %shard_map.125 = (bf16[48,48,512]{2,1,0:T(8,128)(2,1)S(1)}, f32[48,8,512]{2,1,0:T(8,128)S(1)}) custom-call(s32[1]{0:T(128)} %bitcast.1.tile_ref, bf16[6,2,192,768]{3,2,1,0:T(8,128)(2,1)S(1)} %get-tuple-element.22.bands_ref, bf16[48,48,512]{2,1,0:T(8,128)(2,1)S(1)} %get-tuple-element.31.r_ref), custom_call_target="tpu_custom_call" | custom-call | flops 4000000000 | bytes 20000000 | tf_op jit(solution)/shard_map/pallas_call | solution.py:402
  12.9 0.0 collective-permute-done.1.halo_ref
  12.9 0.0 copy-done
  12.9 0.0 copy-done.1
  13.0 0.0 copy-done.2
  13.0 0.0 copy-done.3
  13.0 5.5 %shard_map.126 = (bf16[384,512]{1,0:T(8,128)(2,1)}, bf16[320,384]{1,0:T(8,128)(2,1)}, bf16[160,1152]{1,0:T(8,128)(2,1)S(1)}) custom-call(s32[1]{0:T(128)} %bitcast.1.tile_ref, s32[1]{0:T(128)S(6)} %copy.13.count_ref, bf16[384,512]{1,0:T(8,128)(2,1)S(1)} %collective-permute-done.1.halo_ref, bf16[3,128,256]{2,1,0:T(8,128)(2,1)S(1)} %get-tuple-element.21.sides_ref, ...), custom_call_target="tpu_custom_call" | custom-call | tf_op jit(solution)/shard_map/pallas_call | solution.py:403
  18.5 7.3 %all-to-all-start = ((bf16[8,40,384]{2,1,0:T(8,128)(2,1)}), bf16[8,40,384]{2,1,0:T(8,128)(2,1)S(1)}, u32[]{:S(2)}, u32[]{:S(2)}) async-start(bf16[8,40,384]{2,1,0:T(8,128)(2,1)} %bitcast.7), calls=%async_computation | async-start | bytes 491520 | tf_op jit(solution)/shard_map/all_to_all | solution.py:412
  25.8 0.6 %shard_map.127.ffold_ref = f32[320,384]{1,0:T(8,128)S(1)} custom-call(bf16[160,1152]{1,0:T(8,128)(2,1)S(1)} %get-tuple-element.36.fold_ref, bf16[2304,384]{1,0:T(8,128)(2,1)S(1)} %get-tuple-element.26.foot_ref), custom_call_target="tpu_custom_call" | custom-call | tf_op jit(solution)/shard_map/pallas_call | solution.py:413
  26.4 8.3 %all-to-all-done.parts_ref = bf16[8,40,384]{2,1,0:T(8,128)(2,1)S(1)} async-done(((bf16[8,40,384]{2,1,0:T(8,128)(2,1)}), bf16[8,40,384]{2,1,0:T(8,128)(2,1)S(1)}, u32[]{:S(2)}, u32[]{:S(2)}) %all-to-all-start) | async-done | bytes 245792 | tf_op jit(solution)/shard_map/all_to_all | solution.py:412
  34.7 0.1 shard_map.128
  34.7 11.6 %all_to_all.10 = bf16[8,40,384]{2,1,0:T(8,128)(2,1)S(1)} all-to-all(bf16[8,40,384]{2,1,0:T(8,128)(2,1)S(1)} %shard_map.128), channel_id=1, replica_groups=mesh['groups'=2,'tm'=8,'tile'=2] {'tm'}, dimensions={0} | all-to-all | bytes 491520 | tf_op jit(solution)/shard_map/all_to_all | solution.py:423
  46.4 1.6 %shard_map.129 = bf16[2304,384]{1,0:T(8,128)(2,1)} custom-call(s32[1]{0:T(128)S(6)} %copy.13.count_ref, bf16[320,384]{1,0:T(8,128)(2,1)S(1)} %bitcast.12, bf16[160,1152]{1,0:T(8,128)(2,1)S(1)} %get-tuple-element.36.fold_ref, s32[1,384]{1,0:T(1,128)S(1)} %copy-done, s32[1,384]{1,0:T(1,128)S(1)} %copy-done.1, s32[1,384]{1,0:T(1,128)S(1)} %copy-done.2), custom_call_target="tpu_custom_call" | custom-call | tf_op jit(solution)/shard_map/pallas_call | solution.py:424
Async XLA Ops:
  5.8 2.4 %collective-permute-start = (bf16[384,512]{1,0:T(8,128)(2,1)S(1)}, bf16[384,512]{1,0:T(8,128)(2,1)S(1)}, u32[]{:S(2)}, u32[]{:S(2)}) collective-permute-start(bf16[384,512]{1,0:T(8,128)(2,1)S(1)} %get-tuple-element.20), channel_id=1, source_target_pairs={{0,1},{1,0},{2,3},{3,2},{4,5},{5,4},{6,7},{7,6},{8,9},{9,8},{10,11... | collective-permute-start | bytes 1179656 | tf_op jit(solution)/shard_map/ppermute | solution.py:348
  11.0 1.9 %collective-permute-start.1 = (bf16[384,512]{1,0:T(8,128)(2,1)S(1)}, bf16[384,512]{1,0:T(8,128)(2,1)S(1)}, u32[]{:S(2)}, u32[]{:S(2)}) collective-permute-start(bf16[384,512]{1,0:T(8,128)(2,1)S(1)} %get-tuple-element.30), channel_id=1, source_target_pairs={{0,1},{1,0},{2,3},{3,2},{4,5},{5,4},{6,7},{7,6},{8,9},{9,8},{10,11... | collective-permute-start | bytes 1179656 | tf_op jit(solution)/shard_map/ppermute | solution.py:348
  11.1 1.9 %copy-start = (s32[1,384]{1,0:T(1,128)S(1)}, s32[1,384]{1,0:T(1,128)}, u32[]{:S(2)}) copy-start(s32[1,384]{1,0:T(1,128)} %cr_ref.3) | copy-start | bytes 4612
  11.1 1.9 %copy-start.1 = (s32[1,384]{1,0:T(1,128)S(1)}, s32[1,384]{1,0:T(1,128)}, u32[]{:S(2)}) copy-start(s32[1,384]{1,0:T(1,128)} %cc_ref.3) | copy-start | bytes 4612
  11.1 1.9 %copy-start.2 = (s32[1,384]{1,0:T(1,128)S(1)}, s32[1,384]{1,0:T(1,128)}, u32[]{:S(2)}) copy-start(s32[1,384]{1,0:T(1,128)} %rad_ref.3) | copy-start | bytes 4612
  11.1 1.9 %copy-start.3 = (s32[1,1152]{1,0:T(1,128)S(1)}, s32[1,1152]{1,0:T(1,128)}, u32[]{:S(2)}) copy-start(s32[1,1152]{1,0:T(1,128)} %constant.16.clone.slot_ref) | copy-start | bytes 13828
  18.5 16.2 %all-to-all-start = ((bf16[8,40,384]{2,1,0:T(8,128)(2,1)}), bf16[8,40,384]{2,1,0:T(8,128)(2,1)S(1)}, u32[]{:S(2)}, u32[]{:S(2)}) async-start(bf16[8,40,384]{2,1,0:T(8,128)(2,1)} %bitcast.7), calls=%async_computation | async-start | bytes 491520 | tf_op jit(solution)/shard_map/all_to_all | solution.py:412

commit v9 on v8

--- a/solution.py
+++ b/solution.py
@@ -317,27 +317,42 @@
     den = total[share : share + 1] + total[share + 1 : share + 2] + RIDGE
     foot = ffold_ref[pl.ds(pl.multiple_of(me_ref[0] * block, 8), block), :]
     moved = jnp.maximum(foot - total / den, 0.0).astype(bf16)
-    for j in range(parts):
-        out_ref[j] = moved
-
-
-def unfold_kernel(count_ref, all_ref, fold_ref, cr_ref, cc_ref, rad_ref, out_hbm, buf, sems):
-    count = count_ref[0]
+    out_ref[...] = moved
+
+
+def pair_kernel(me_ref, own_ref, other_ref, out_ref):
+    odd = lax.rem(me_ref[0], 2) == 1
+    block = own_ref.shape[0]
+    own, other = own_ref[...].astype(f32), other_ref[...].astype(f32)
+    both = jnp.concatenate([jnp.where(odd, other, own), jnp.where(odd, own, other)], axis=0)
+    out_ref[...] = both.astype(bf16)
+
+
+def unfold_kernel(steps, far, me_ref, count_ref, fold_ref, cr_ref, cc_ref, rad_ref, *refs):
+    pairs, out_hbm, every, buf, sems = refs[: len(steps)], refs[-4], refs[-3], refs[-2], refs[-1]
+    count, me = count_ref[0], me_ref[0]
     half = fold_ref.shape[0]
+    pair = pairs[0].shape[0]
+    in_half = half // pair
+    mine = me // 2
+    h = mine // in_half
+    if far:
+        h = 1 - h
+    for step, ref in zip(steps, pairs):
+        place = lax.rem(jnp.bitwise_xor(mine, step // 2), in_half)
+        every[pl.ds(pl.multiple_of(place * pair, 16), pair), :] = ref[...]
     gap_sq = col_gap_sq(cc_ref[...])
     cr, rad = cr_ref[...], rad_ref[...]
     band = BAND * SIDE
     stores = []
-    for g in range(SIDE // BAND):
-        h, b = g % 2, g // 2
-        wide = lax.dot_general(fold_ref[:, b * band : (b + 1) * band], all_ref[h * half : (h + 1) * half, :],
+    for b in range(SIDE // BAND // 2):
+        wide = lax.dot_general(fold_ref[:, b * band : (b + 1) * band], every[...],
                                (((0,), (0,)), ((), ())), preferred_element_type=f32)
         for i in range(BAND):
-            row = g * BAND + i
-            keep = gap_sq <= disc_limit(cr, rad, count, row)
-            buf[pl.ds(row * SIDE, SIDE), :] = jnp.where(keep, wide[i * SIDE : (i + 1) * SIDE], 0.0).astype(bf16)
-        rows = pl.ds(g * band, band)
-        stores.append(pltpu.make_async_copy(buf.at[rows, :], out_hbm.at[rows, :], sems.at[g]))
+            keep = gap_sq <= disc_limit(cr, rad, count, (2 * b + h) * BAND + i)
+            buf[pl.ds(b * band + i * SIDE, SIDE), :] = jnp.where(keep, wide[i * SIDE : (i + 1) * SIDE], 0.0).astype(bf16)
+        rows = pl.ds(pl.multiple_of((2 * b + h) * band, band), band)
+        stores.append(pltpu.make_async_copy(buf.at[pl.ds(b * band, band), :], out_hbm.at[rows, :], sems.at[b]))
         stores[-1].start()
     for store in stores:
         store.wait()
@@ -346,6 +361,10 @@
 def swap(x):
     count = lax.axis_size("tile")
     return lax.ppermute(x, "tile", [(i, count - 1 - i) for i in range(count)])
+
+
+def from_xor(x, step):
+    return lax.ppermute(x, "tm", [(i, i ^ step) for i in range(lax.axis_size("tm"))])
 
 
 def shards(movie, cycle_weights, footprints, traces, centre_row, centre_col, radius, comp_count):
@@ -417,17 +436,32 @@
     )(fold, foot)
     moved = pl.pallas_call(
         functools.partial(share_kernel, share),
-        out_shape=sds((parts, block, comps), bf16),
+        out_shape=sds((block, comps), bf16),
         in_specs=[SM, VM, VM], out_specs=VM, compiler_params=params(),
     )(me, received, ffold)
-    every = lax.all_to_all(moved, "tm", 0, 0, tiled=False).reshape(packed, comps)
-    new_foot = pl.pallas_call(
-        unfold_kernel,
-        out_shape=sds((pixels, comps), bf16),
-        in_specs=[SM] + [VM] * 5, out_specs=HB,
-        scratch_shapes=[pltpu.VMEM((pixels, comps), bf16), pltpu.SemaphoreType.DMA((bands,))],
-        compiler_params=params(),
-    )(comp_count, every, fold, centre_row, centre_col, radius)
+    pair = pl.pallas_call(
+        pair_kernel,
+        out_shape=sds((2 * block, comps), bf16),
+        in_specs=[SM, VM, VM], out_specs=VM, compiler_params=params(),
+    )(me, moved, from_xor(moved, 1))
+    pairs = [pair] + [from_xor(pair, step) for step in range(2, parts, 2)]
+    new_foot = None
+    for far in range(2):
+        steps = list(range(far * parts // 2, (far + 1) * parts // 2, 2))
+        args = [me, comp_count, fold, centre_row, centre_col, radius] + [pairs[step // 2] for step in steps]
+        specs = [SM, SM] + [VM] * (len(args) - 2)
+        if far:
+            args, specs = args + [new_foot], specs + [HB]
+        new_foot = pl.pallas_call(
+            functools.partial(unfold_kernel, steps, far),
+            out_shape=sds((pixels, comps), bf16),
+            in_specs=specs, out_specs=HB,
+            scratch_shapes=[pltpu.VMEM((packed // 2, comps), bf16), pltpu.VMEM((pixels // 2, comps), bf16),
+                            pltpu.SemaphoreType.DMA((bands // 2,))],
+            input_output_aliases={len(args) - 1: 0} if far else {},
+            compiler_params=params(),
+            cost_estimate=pl.CostEstimate(flops=1_000_000_000, bytes_accessed=1_000_000, transcendentals=0),
+        )(*args)
     return (new_foot[None], trace[None])
 
 

time: 48.2 us -> 48.9 us (1.015)
  blocking collectives: 11.6 us -> 0 us
  waiting for transfers between devices: 8.34 us -> 14.5 us
  starting transfers between devices: 7.91 us -> 12.8 us
  Pallas kernels: 18.6 us -> 19.7 us
    all_to_all x1 -> x0, blocking collectives: 11.6 us -> none  [shards(): lax.all_to_all(moved, 'tm', 0, 0, tiled=False).reshape(packed, comps)]
    ppermute x0 -> x4, waiting for transfers between devices: none -> 6.15 us  [from_xor(): lax.ppermute(x, 'tm', [(i, i ^ step) for i in range(lax.axis_size('tm'))])]
    ppermute x0 -> x4, starting transfers between devices: none -> 4.92 us  [from_xor(): lax.ppermute(x, 'tm', [(i, i ^ step) for i in range(lax.axis_size('tm'))])]
    pallas_call x2 -> x4, Pallas kernels: 1.63 us -> 2.56 us  [the longest x2 2.49 us: shards(): pl.pallas_call(functools.partial(unfold_kernel, steps, far), out_shape=sd...]
  transfers between devices with their start and end apart: 3 -> 7, of which waited for: 1 -> 5; matrix products, arithmetic and copies ran while one was open for 0% -> 0% of each run, Pallas kernels for 9% -> 11%
where the time goes in v9:
time: 48.9 us; the launch traced here: 48.6 us
  Pallas kernels  19.7 us (40%)
  waiting for transfers between devices  14.5 us (30%)
  starting transfers between devices  12.8 us (26%)
  between operations  1.59 us (3%)
    all_to_all x1, waiting for transfers between devices, shards(): lax.all_to_all(part.reshape(parts, block, comps), 'tm', 0, 0, tiled=False)  8.32 us
    all_to_all x1, starting transfers between devices, shards(): lax.all_to_all(part.reshape(parts, block, comps), 'tm', 0, 0, tiled=False)  7.26 us
    ppermute x4, waiting for transfers between devices, from_xor(): lax.ppermute(x, 'tm', [(i, i ^ step) for i in range(lax.axis_size('tm'))])  6.15 us
    pallas_call x1, Pallas kernels, shards(): pl.pallas_call(functools.partial(last_kernel, block, share), out_shape=(s...  5.69 us
    ppermute x4, starting transfers between devices, from_xor(): lax.ppermute(x, 'tm', [(i, i ^ step) for i in range(lax.axis_size('tm'))])  4.92 us
    pallas_call x1, Pallas kernels, shards(): pl.pallas_call(start_kernel, out_shape=(sds((pixels, comps), bf16), sds((...  4.47 us
    pallas_call x2, Pallas kernels, shards(): x, beyond = banded(tile, band_w, r)  3.62 us
    pallas_call x1, Pallas kernels, shards(): pl.pallas_call(pass_kernel, out_shape=(sds((comps, frames), bf16), r_shap...  2.83 us
  transfers between devices with their start and end apart: 7, of which 5 were waited for; matrix products, arithmetic and copies ran while one was open for 0% of the time, Pallas kernels for 11%

profile of v9, /device:TPU:0, one launch (start us, length us, event | category | flops | bytes accessed | tf_op | source)
XLA Modules:
  0.0 48.6 jit_solution(9006870314621068270)
XLA Ops:
  1.3 4.5 %shard_map.122 = (bf16[2304,384]{1,0:T(8,128)(2,1)S(1)}, bf16[384,512]{1,0:T(8,128)(2,1)S(1)}, f32[384,128]{1,0:T(8,128)S(1)}, bf16[48,48,512]{2,1,0:T(8,128)(2,...) custom-call(s32[1]{0:T(128)} %bitcast.1.tile_ref, ...), custom_call_target="tpu_custom_call" | custom-call | tf_op jit(solution)/shard_map/pallas_call | solution.py:393
  5.8 0.6 %collective-permute-start = (bf16[384,512]{1,0:T(8,128)(2,1)S(1)}, bf16[384,512]{1,0:T(8,128)(2,1)S(1)}, u32[]{:S(2)}, u32[]{:S(2)}) collective-permute-start(bf16[384,512]{1,0:T(8,128)(2,1)S(1)} %get-tuple-element.20), channel_id=1, source_target_pairs={{0,1},{1,0},{2,3},{3,2},{4,5},{5,4},{6,7},{7,6},{8,9},{9,8},{10,11... | collective-permute-start | bytes 1179656 | tf_op jit(solution)/shard_map/ppermute | solution.py:363
  6.3 1.8 %shard_map.123 = (bf16[48,48,512]{2,1,0:T(8,128)(2,1)S(1)}, f32[48,8,512]{2,1,0:T(8,128)S(1)}) custom-call(s32[1]{0:T(128)} %bitcast.1.tile_ref, bf16[6,2,192,768]{3,2,1,0:T(8,128)(2,1)S(1)} %get-tuple-element.22.bands_ref, bf16[48,48,512]{2,1,0:T(8,128)(2,1)S(1)} %get-tuple-element.23.r_ref), custom_call_target="tpu_custom_call" | custom-call | flops 4000000000 | bytes 20000000 | tf_op jit(solution)/shard_map/pallas_call | solution.py:412
  8.1 0.0 collective-permute-done.halo_ref
  8.1 2.8 %shard_map.124 = (bf16[384,512]{1,0:T(8,128)(2,1)S(1)}, bf16[48,48,512]{2,1,0:T(8,128)(2,1)S(1)}, bf16[384,512]{1,0:T(8,128)(2,1)S(1)}) custom-call(s32[1]{0:T(128)} %bitcast.1.tile_ref, s32[1]{0:T(128)S(6)} %copy.15.count_ref, bf16[384,512]{1,0:T(8,128)(2,1)S(1)} %collective-permute-done.halo_ref, bf16[3,128,256]{2,1,0:T(8,128)(2,1)S(1)} %get-tuple-element.21.sides_ref, ...), custom_call_target="tpu_custom_call" | custom-call | tf_op jit(solution)/shard_map/pallas_call | solution.py:413
  11.0 0.1 collective-permute-start.1
  11.1 0.0 copy-start
  11.1 0.0 copy-start.1
  11.1 0.0 copy-start.2
  11.1 0.0 copy-start.3
  11.1 1.8 %shard_map.125 = (bf16[48,48,512]{2,1,0:T(8,128)(2,1)S(1)}, f32[48,8,512]{2,1,0:T(8,128)S(1)}) custom-call(s32[1]{0:T(128)} %bitcast.1.tile_ref, bf16[6,2,192,768]{3,2,1,0:T(8,128)(2,1)S(1)} %get-tuple-element.22.bands_ref, bf16[48,48,512]{2,1,0:T(8,128)(2,1)S(1)} %get-tuple-element.31.r_ref), custom_call_target="tpu_custom_call" | custom-call | flops 4000000000 | bytes 20000000 | tf_op jit(solution)/shard_map/pallas_call | solution.py:421
  12.9 0.0 collective-permute-done.1.halo_ref
  12.9 0.0 copy-done
  12.9 0.0 copy-done.1
  13.0 0.0 copy-done.2
  13.0 0.0 copy-done.3
  13.0 5.7 %shard_map.126 = (bf16[384,512]{1,0:T(8,128)(2,1)}, bf16[320,384]{1,0:T(8,128)(2,1)}, bf16[160,1152]{1,0:T(8,128)(2,1)S(1)}) custom-call(s32[1]{0:T(128)} %bitcast.1.tile_ref, s32[1]{0:T(128)S(6)} %copy.15.count_ref, bf16[384,512]{1,0:T(8,128)(2,1)S(1)} %collective-permute-done.1.halo_ref, bf16[3,128,256]{2,1,0:T(8,128)(2,1)S(1)} %get-tuple-element.21.sides_ref, ...), custom_call_target="tpu_custom_call" | custom-call | tf_op jit(solution)/shard_map/pallas_call | solution.py:422
  18.7 7.3 %all-to-all-start = ((bf16[8,40,384]{2,1,0:T(8,128)(2,1)}), bf16[8,40,384]{2,1,0:T(8,128)(2,1)S(1)}, u32[]{:S(2)}, u32[]{:S(2)}) async-start(bf16[8,40,384]{2,1,0:T(8,128)(2,1)} %bitcast.7), calls=%async_computation | async-start | bytes 491520 | tf_op jit(solution)/shard_map/all_to_all | solution.py:431
  25.9 0.6 %shard_map.127.ffold_ref = f32[320,384]{1,0:T(8,128)S(1)} custom-call(bf16[160,1152]{1,0:T(8,128)(2,1)S(1)} %get-tuple-element.35.fold_ref, bf16[2304,384]{1,0:T(8,128)(2,1)S(1)} %get-tuple-element.26.foot_ref), custom_call_target="tpu_custom_call" | custom-call | tf_op jit(solution)/shard_map/pallas_call | solution.py:432
  26.5 8.3 %all-to-all-done.parts_ref = bf16[8,40,384]{2,1,0:T(8,128)(2,1)S(1)} async-done(((bf16[8,40,384]{2,1,0:T(8,128)(2,1)}), bf16[8,40,384]{2,1,0:T(8,128)(2,1)S(1)}, u32[]{:S(2)}, u32[]{:S(2)}) %all-to-all-start) | async-done | bytes 245792 | tf_op jit(solution)/shard_map/all_to_all | solution.py:431
  34.9 1.4 %collective-permute-start.2 = (bf16[40,384]{1,0:T(8,128)(2,1)S(1)}, bf16[40,384]{1,0:T(8,128)(2,1)S(1)}, u32[]{:S(2)}, u32[]{:S(2)}) collective-permute-start(bf16[40,384]{1,0:T(8,128)(2,1)S(1)} %shard_map.128.own_ref), channel_id=1, source_target_pairs={{0,2},{2,0},{4,6},{6,4},{8,10},{10,8},{12,14},{14,12},{1,3},{3,1},... | collective-permute-start | bytes 92168 | tf_op jit(solution)/shard_map/ppermute | solution.py:367
  36.2 2.6 %collective-permute-done.2.other_ref = bf16[40,384]{1,0:T(8,128)(2,1)S(1)} collective-permute-done((bf16[40,384]{1,0:T(8,128)(2,1)S(1)}, bf16[40,384]{1,0:T(8,128)(2,1)S(1)}, u32[]{:S(2)}, u32[]{:S(2)}) %collective-permute-start.2) | collective-permute-done | bytes 30752 | tf_op jit(solution)/shard_map/ppermute | solution.py:367
  38.9 1.0 %collective-permute-start.5 = (bf16[80,384]{1,0:T(8,128)(2,1)S(1)}, bf16[80,384]{1,0:T(8,128)(2,1)S(1)}, u32[]{:S(2)}, u32[]{:S(2)}) collective-permute-start(bf16[80,384]{1,0:T(8,128)(2,1)S(1)} %shard_map.129.refs_0_), channel_id=1, source_target_pairs={{0,4},{2,6},{4,0},{6,2},{8,12},{10,14},{12,8},{14,10},{1,5},{3,7},... | collective-permute-start | bytes 184328 | tf_op jit(solution)/shard_map/ppermute | solution.py:367
  39.9 1.5 %collective-permute-start.4 = (bf16[80,384]{1,0:T(8,128)(2,1)S(1)}, bf16[80,384]{1,0:T(8,128)(2,1)S(1)}, u32[]{:S(2)}, u32[]{:S(2)}) collective-permute-start(bf16[80,384]{1,0:T(8,128)(2,1)S(1)} %shard_map.129.refs_0_), channel_id=1, source_target_pairs={{0,12},{2,14},{4,8},{6,10},{8,4},{10,6},{12,0},{14,2},{1,13},{3,15... | collective-permute-start | bytes 184328 | tf_op jit(solution)/shard_map/ppermute | solution.py:367
  41.3 1.1 %collective-permute-start.3 = (bf16[80,384]{1,0:T(8,128)(2,1)S(1)}, bf16[80,384]{1,0:T(8,128)(2,1)S(1)}, u32[]{:S(2)}, u32[]{:S(2)}) collective-permute-start(bf16[80,384]{1,0:T(8,128)(2,1)S(1)} %shard_map.129.refs_0_), channel_id=1, source_target_pairs={{0,8},{2,10},{4,12},{6,14},{8,0},{10,2},{12,4},{14,6},{1,9},{3,11}... | collective-permute-start | bytes 184328 | tf_op jit(solution)/shard_map/ppermute | solution.py:367
  42.4 1.4 %collective-permute-done.5.refs_1_ = bf16[80,384]{1,0:T(8,128)(2,1)S(1)} collective-permute-done((bf16[80,384]{1,0:T(8,128)(2,1)S(1)}, bf16[80,384]{1,0:T(8,128)(2,1)S(1)}, u32[]{:S(2)}, u32[]{:S(2)}) %collective-permute-start.5) | collective-permute-done | bytes 61472 | tf_op jit(solution)/shard_map/ppermute | solution.py:367
  43.8 1.2 %shard_map.130.refs_2_ = bf16[2304,384]{1,0:T(8,128)(2,1)} custom-call(s32[1]{0:T(128)} %bitcast.me_ref, s32[1]{0:T(128)S(6)} %copy.15.count_ref, bf16[160,1152]{1,0:T(8,128)(2,1)S(1)} %get-tuple-element.35.fold_ref, s32[1,384]{1,0:T(1,128)S(1)} %copy-done, s32[1,384]{1,0:T(1,128)S(1)} %copy-done.1, s32[1,384]{1,0:T(1,128)S(1)} %copy-done.2, ...), custom_call_target="tpu_custom_call" | custom-call | flops 1000000000 | bytes 1000000 | tf_op jit(solution)/shard_map/pallas_call | solution.py:455
  45.0 0.9 %collective-permute-done.4.refs_1_ = bf16[80,384]{1,0:T(8,128)(2,1)S(1)} collective-permute-done((bf16[80,384]{1,0:T(8,128)(2,1)S(1)}, bf16[80,384]{1,0:T(8,128)(2,1)S(1)}, u32[]{:S(2)}, u32[]{:S(2)}) %collective-permute-start.4) | collective-permute-done | bytes 61472 | tf_op jit(solution)/shard_map/ppermute | solution.py:367
  45.9 1.3 %collective-permute-done.3.refs_0_ = bf16[80,384]{1,0:T(8,128)(2,1)S(1)} collective-permute-done((bf16[80,384]{1,0:T(8,128)(2,1)S(1)}, bf16[80,384]{1,0:T(8,128)(2,1)S(1)}, u32[]{:S(2)}, u32[]{:S(2)}) %collective-permute-start.3) | collective-permute-done | bytes 61472 | tf_op jit(solution)/shard_map/ppermute | solution.py:367
  47.2 1.2 %shard_map.131 = bf16[2304,384]{1,0:T(8,128)(2,1)} custom-call(s32[1]{0:T(128)} %bitcast.me_ref, s32[1]{0:T(128)S(6)} %copy.15.count_ref, bf16[160,1152]{1,0:T(8,128)(2,1)S(1)} %get-tuple-element.35.fold_ref, s32[1,384]{1,0:T(1,128)S(1)} %copy-done, s32[1,384]{1,0:T(1,128)S(1)} %copy-done.1, s32[1,384]{1,0:T(1,128)S(1)} %copy-done.2, ...), custom_call_target="tpu_custom_call", output_to_operand_aliasing={{}: (8, {})} | custom-call | flops 1000000000 | bytes 1000000 | tf_op jit(solution)/shard_map/pallas_call | solution.py:455
  (2 shorter events, 0.1 us)
Async XLA Ops:
  5.8 2.4 %collective-permute-start = (bf16[384,512]{1,0:T(8,128)(2,1)S(1)}, bf16[384,512]{1,0:T(8,128)(2,1)S(1)}, u32[]{:S(2)}, u32[]{:S(2)}) collective-permute-start(bf16[384,512]{1,0:T(8,128)(2,1)S(1)} %get-tuple-element.20), channel_id=1, source_target_pairs={{0,1},{1,0},{2,3},{3,2},{4,5},{5,4},{6,7},{7,6},{8,9},{9,8},{10,11... | collective-permute-start | bytes 1179656 | tf_op jit(solution)/shard_map/ppermute | solution.py:363
  11.0 1.9 %collective-permute-start.1 = (bf16[384,512]{1,0:T(8,128)(2,1)S(1)}, bf16[384,512]{1,0:T(8,128)(2,1)S(1)}, u32[]{:S(2)}, u32[]{:S(2)}) collective-permute-start(bf16[384,512]{1,0:T(8,128)(2,1)S(1)} %get-tuple-element.30), channel_id=1, source_target_pairs={{0,1},{1,0},{2,3},{3,2},{4,5},{5,4},{6,7},{7,6},{8,9},{9,8},{10,11... | collective-permute-start | bytes 1179656 | tf_op jit(solution)/shard_map/ppermute | solution.py:363
  11.1 1.9 %copy-start = (s32[1,384]{1,0:T(1,128)S(1)}, s32[1,384]{1,0:T(1,128)}, u32[]{:S(2)}) copy-start(s32[1,384]{1,0:T(1,128)} %cr_ref.5) | copy-start | bytes 4612
  11.1 1.9 %copy-start.1 = (s32[1,384]{1,0:T(1,128)S(1)}, s32[1,384]{1,0:T(1,128)}, u32[]{:S(2)}) copy-start(s32[1,384]{1,0:T(1,128)} %cc_ref.5) | copy-start | bytes 4612
  11.1 1.9 %copy-start.2 = (s32[1,384]{1,0:T(1,128)S(1)}, s32[1,384]{1,0:T(1,128)}, u32[]{:S(2)}) copy-start(s32[1,384]{1,0:T(1,128)} %rad_ref.5) | copy-start | bytes 4612
  11.1 1.9 %copy-start.3 = (s32[1,1152]{1,0:T(1,128)S(1)}, s32[1,1152]{1,0:T(1,128)}, u32[]{:S(2)}) copy-start(s32[1,1152]{1,0:T(1,128)} %constant.16.clone.slot_ref) | copy-start | bytes 13828
  18.7 16.2 %all-to-all-start = ((bf16[8,40,384]{2,1,0:T(8,128)(2,1)}), bf16[8,40,384]{2,1,0:T(8,128)(2,1)S(1)}, u32[]{:S(2)}, u32[]{:S(2)}) async-start(bf16[8,40,384]{2,1,0:T(8,128)(2,1)} %bitcast.7), calls=%async_computation | async-start | bytes 491520 | tf_op jit(solution)/shard_map/all_to_all | solution.py:431
  34.9 4.0 %collective-permute-start.2 = (bf16[40,384]{1,0:T(8,128)(2,1)S(1)}, bf16[40,384]{1,0:T(8,128)(2,1)S(1)}, u32[]{:S(2)}, u32[]{:S(2)}) collective-permute-start(bf16[40,384]{1,0:T(8,128)(2,1)S(1)} %shard_map.128.own_ref), channel_id=1, source_target_pairs={{0,2},{2,0},{4,6},{6,4},{8,10},{10,8},{12,14},{14,12},{1,3},{3,1},... | collective-permute-start | bytes 92168 | tf_op jit(solution)/shard_map/ppermute | solution.py:367
  38.9 4.9 %collective-permute-start.5 = (bf16[80,384]{1,0:T(8,128)(2,1)S(1)}, bf16[80,384]{1,0:T(8,128)(2,1)S(1)}, u32[]{:S(2)}, u32[]{:S(2)}) collective-permute-start(bf16[80,384]{1,0:T(8,128)(2,1)S(1)} %shard_map.129.refs_0_), channel_id=1, source_target_pairs={{0,4},{2,6},{4,0},{6,2},{8,12},{10,14},{12,8},{14,10},{1,5},{3,7},... | collective-permute-start | bytes 184328 | tf_op jit(solution)/shard_map/ppermute | solution.py:367
  39.9 6.0 %collective-permute-start.4 = (bf16[80,384]{1,0:T(8,128)(2,1)S(1)}, bf16[80,384]{1,0:T(8,128)(2,1)S(1)}, u32[]{:S(2)}, u32[]{:S(2)}) collective-permute-start(bf16[80,384]{1,0:T(8,128)(2,1)S(1)} %shard_map.129.refs_0_), channel_id=1, source_target_pairs={{0,12},{2,14},{4,8},{6,10},{8,4},{10,6},{12,0},{14,2},{1,13},{3,15... | collective-permute-start | bytes 184328 | tf_op jit(solution)/shard_map/ppermute | solution.py:367
  41.3 5.9 %collective-permute-start.3 = (bf16[80,384]{1,0:T(8,128)(2,1)S(1)}, bf16[80,384]{1,0:T(8,128)(2,1)S(1)}, u32[]{:S(2)}, u32[]{:S(2)}) collective-permute-start(bf16[80,384]{1,0:T(8,128)(2,1)S(1)} %shard_map.129.refs_0_), channel_id=1, source_target_pairs={{0,8},{2,10},{4,12},{6,14},{8,0},{10,2},{12,4},{14,6},{1,9},{3,11}... | collective-permute-start | bytes 184328 | tf_op jit(solution)/shard_map/ppermute | solution.py:367
